TPU v7x, 256 devices: a whole 4x4x8 slice. The times are simulated.
256 devices in a mesh: row: 32 (over z, x_lo, core), head: 8 (over y, x_hi).
Axes of the slice: x: 4 (x_hi: 2, x_lo: 2; x = x_hi * 2 + x_lo), y: 4, z: 8, core: 2. Of those that a mesh axis runs over, the one named last changes fastest.
Arguments:
- sequence_matrix: float32 [64, 512, 256], P('row', 'head'), may hold values from -6 to 6
- pair_representation: float32 [512, 512, 128], P('row', 'head'), may hold values from -6 to 6
- alignment_row_mask: int32 [64], P('row'), may hold values 0 or 1
- residue_mask: int32 [512], replicated, may hold values 0 or 1
- attention_scale_vector: float32 [256], replicated, may hold values from 0.1 to 1.9
- asking_factor_matrix: float32 [256, 256], replicated, may hold values from -0.375 to 0.375
- lookup_factor_matrix: float32 [256, 256], replicated, may hold values from -0.375 to 0.375
- content_factor_matrix: float32 [256, 256], replicated, may hold values from -0.375 to 0.375
- sigmoid_factor_matrix: float32 [256, 256], replicated, may hold values from -0.375 to 0.375
- final_factor_matrix: float32 [256, 256], replicated, may hold values from -0.375 to 0.375
- pair_norm_gain: float32 [128], replicated, may hold values from 0.1 to 1.9
- bias_weight: float32 [128, 8], replicated, may hold values from -20 to 20
- tensor_scale_vector: float32 [256], replicated, may hold values from 0.1 to 1.9
- first_factor_matrix: float32 [256, 32], replicated, may hold values from -0.375 to 0.375
- second_factor_matrix: float32 [256, 32], replicated, may hold values from -0.375 to 0.375
- outer_weight: float32 [1024, 128], replicated, may hold values from -1 to 1
Outputs:
- msa_out: float32 [64, 512, 256], P('row', 'head')
- pair_out: float32 [512, 512, 128], P('row', 'head')
All inputs are finite; a program needn't handle non-finite values. No bound on the sum of `alignment_row_mask` on one device may be relied on, other than what follows from the above.
Results may differ from a plain program's by a relative error of at most 0.0003.
Values sent between devices are 32-bit elements; how exact they have to be, the bound alone decides.
No kernel may reach another device: no remote copies, remote signals or barrier semaphores. Data moves between devices by JAX's collectives and lax.ppermute only.
A program may use at most 64 MiB of HBM per device.

v0:
```python
import math

import jax
import jax.numpy as jnp
import numpy as np
from jax import lax
from jax.experimental import pallas as pl
from jax.experimental.pallas import tpu as pltpu
from jax.sharding import PartitionSpec as P

exact = lax.Precision.HIGHEST
f32 = jnp.float32
bf16 = jnp.bfloat16
MIB = 1024 * 1024

Z, A, H = 8, 4, 8
STEPS = (16, 8, 4, 2, 1)


def spread_table():
    far = np.zeros((H, H), np.int32)
    ring = lambda d, n: min(d % n, -d % n)
    for c in range(H):
        def plane(h):
            return ring(h // 2 - c // 2, 4) + 2 * ((h ^ c) & 1)

        columns = sorted(range(H), key=lambda h: (-plane(h), (h // 2 - c // 2) % 4))
        planes = sorted(range(Z), key=lambda b: (ring(b - c, Z), (b - c) % Z))
        for h, b in zip(columns, planes):
            far[c][h] = b
    return far


FAR = spread_table()


def reverse_bits(v):
    return int(format(v, "05b")[::-1], 2)


def bias_moves():
    return [
        ((4 * b + a) * H + h, (4 * int(FAR[b][h]) + a) * H + b)
        for b in range(Z)
        for a in range(A)
        for h in range(H)
    ]


def tables():
    bias = np.zeros((Z * A, H, 32), np.int32)
    left = np.zeros((Z * A, H, 32), np.int32)
    for r in range(Z * A):
        for h in range(H):
            for block in range(H):
                for a in range(A):
                    bias[r, h, block * A + a] = reverse_bits(r ^ (4 * int(FAR[h][block]) + a))
            for a in range(A):
                for column in range(H):
                    source = 4 * int(FAR[r // 4][column]) + a
                    left[r, h, a * H + column] = reverse_bits(r ^ source)
    return np.concatenate([bias, left], axis=-1).reshape(Z * A * H, 64)


TABLES = tables()


def gather_row(block):
    for step in STEPS:
        other = lax.ppermute(block, "row", [(r, r ^ step) for r in range(Z * A)])
        block = jnp.concatenate([block, other], axis=0)
    return block


def split(v):
    high = v.astype(bf16)
    return high, (v - high.astype(f32)).astype(bf16)


def dot(a, b, dims=((1,), (0,))):
    return lax.dot_general(a, b, (dims, ((), ())), preferred_element_type=f32)


def dot_exact(a, b, dims=((1,), (0,))):
    return lax.dot_general(a, b, (dims, ((), ())), precision=exact, preferred_element_type=f32)


def norm_rows(v, gain):
    center = v - jnp.mean(v, axis=-1, keepdims=True)
    spread = jnp.mean(center * center, axis=-1, keepdims=True)
    return center * lax.rsqrt(spread + 1e-05) * gain


def bias_kernel(pair_ref, gain_ref, weight_ref, out_ref):
    rows = pair_ref[...].reshape(1024, 128)
    normed = norm_rows(rows, gain_ref[...])
    pick = lax.broadcasted_iota(jnp.int32, (8, 128), 0) == (
        lax.broadcasted_iota(jnp.int32, (8, 128), 1) // 16
    )
    wide = dot_exact(weight_ref[...], jnp.where(pick, 1.0, 0.0))
    result = dot_exact(normed, wide)
    lane = lax.broadcasted_iota(jnp.int32, (64, 128), 1) % 16
    total = jnp.zeros((64, 128), f32)
    for i in range(16):
        total = jnp.where(lane == i, result[64 * i : 64 * i + 64], total)
    out_ref[0] = total


def logits_kernel(
    all_ref, own_ref, gain_ref, wq_ref, wk_ref, wv_ref, wg_ref, logit_ref, vh_ref, vl_ref, gate_ref
):
    gain = gain_ref[...]
    own = norm_rows(own_ref[...].reshape(128, 256), gain)
    query = dot_exact(own, wq_ref[...]) * (1.0 / math.sqrt(32))
    gate_ref[...] = jax.nn.sigmoid(dot_exact(own, wg_ref[...]))
    head_of_lane = lax.broadcasted_iota(jnp.int32, (128, 256), 1) // 32
    head_of_row = lax.broadcasted_iota(jnp.int32, (128, 256), 0) // 16
    keep = head_of_lane == head_of_row
    for s in range(2):
        rows = norm_rows(
            jnp.concatenate([all_ref[b, s] for b in range(8)], axis=0), gain
        )
        keys = dot_exact(rows, wk_ref[...])
        high, low = split(dot_exact(wv_ref[...], rows, ((0,), (1,))))
        vh_ref[s] = high
        vl_ref[s] = low
        spread = []
        for a in range(4):
            part = query[64 * s + 16 * a : 64 * s + 16 * a + 16]
            spread.append(jnp.where(keep, jnp.concatenate([part] * 8, axis=0), 0.0))
        spread = jnp.concatenate(spread, axis=0)
        logit_ref[s] = dot_exact(keys, spread, ((1,), (1,)))


def attend_kernel(
    index_ref,
    bias_ref,
    logit_ref,
    key_ref,
    vh_ref,
    vl_ref,
    gate_ref,
    own_ref,
    wf_ref,
    gain_ref,
    first_ref,
    second_ref,
    live_ref,
    mask_ref,
    msa_ref,
    left_ref,
    right_ref,
    y_ref,
):
    lane = lax.broadcasted_iota(jnp.int32, (32, 128), 1) // 16
    folded = [jnp.zeros((32, 128), f32) for _ in range(8)]
    for s in range(2):
        for a in range(4):
            columns = pl.ds(128 * a, 128)
            tiles = []
            for b in range(8):
                rows = pl.ds(64 * b, 64)
                tiles.append(
                    (logit_ref[s, rows, columns] + bias_ref[index_ref[b * 4 + a]])
                    + key_ref[rows, :]
                )
            logits = jnp.concatenate(tiles, axis=0)
            exponent = jnp.exp(logits - jnp.max(logits, axis=0, keepdims=True))
            weights = exponent / jnp.sum(exponent, axis=0, keepdims=True)
            high, low = split(weights)
            vh = vh_ref[s]
            part = dot(vh, high) + dot(vh, low) + dot(vl_ref[s], high)
            for h in range(8):
                moved = pltpu.roll(
                    part[32 * h : 32 * h + 32], (64 * s + 16 * a - 16 * h) % 128, 1
                )
                folded[h] = jnp.where(lane == 4 * s + a, moved, folded[h])
    attended = jnp.transpose(jnp.concatenate(folded, axis=0)) * gate_ref[...]
    updated = own_ref[...].reshape(128, 256) + dot_exact(attended, wf_ref[...])
    msa_ref[...] = updated.reshape(2, 64, 256)
    y = norm_rows(updated, gain_ref[...]) * live_ref[...]
    right_ref[0, 0:32, :] = dot_exact(second_ref[...], y, ((1,), (1,)))
    right_ref[0, 32:40, :] = mask_ref[...]
    y_ref[...] = dot_exact(y, first_ref[...])
    lane = lax.broadcasted_iota(jnp.int32, (32, 128), 1) // 32
    left = jnp.zeros((32, 128), f32)
    for k in range(4):
        left = jnp.where(lane == k, y_ref[pl.ds(k, 32, stride=4), :], left)
    for s in range(2):
        for a in range(4):
            left_ref[a, 4 * s : 4 * s + 4, :] = left[16 * s + 4 * a : 16 * s + 4 * a + 4]


def outer_kernel(
    index_ref,
    rows_live_ref,
    left_in_ref,
    right_in_ref,
    weight_ref,
    pair_ref,
    cols_live_ref,
    out_ref,
    sorted_ref,
    left_ref,
    right_ref,
):
    for p in range(32):
        spot = pl.multiple_of(index_ref[p] * 8, 8)
        sorted_ref[pl.ds(spot, 8), :] = left_in_ref[p]
    count = jnp.zeros((8, 128), f32)
    for k in range(32):
        count = count + right_in_ref[40 * k + 32 : 40 * k + 40, :]
    count = jnp.sum(count)
    left_rows = []
    for s in range(2):
        left_rows.append(
            jnp.concatenate(
                [sorted_ref[pl.ds(4 * s + q, 32, stride=8), :] for q in range(4)], axis=1
            )
        )
    left = jnp.concatenate(left_rows, axis=0)
    high = left.astype(bf16).astype(f32)
    low = left - high
    left_ref[...] = jnp.transpose(jnp.concatenate([high, high, low, jnp.zeros_like(low)], axis=0)).astype(bf16)
    lane = lax.broadcasted_iota(jnp.int32, (32, 128), 1) < 64
    for d in range(16):
        even = right_in_ref[pl.ds(2 * d, 32, stride=40), :]
        odd = right_in_ref[pl.ds(2 * d + 1, 32, stride=40), :]
        both = jnp.concatenate(
            [
                jnp.where(lane, even, pltpu.roll(odd, 64, 1)),
                jnp.where(lane, pltpu.roll(even, 64, 1), odd),
            ],
            axis=0,
        )
        high, low = split(both)
        columns = pl.ds(128 * d, 128)
        right_ref[0:64, columns] = high
        right_ref[64:128, columns] = low
        right_ref[128:192, columns] = high
        right_ref[192:256, columns] = jnp.zeros((64, 128), bf16)
    weight_high, weight_low = split(weight_ref[...])
    lane = lax.broadcasted_iota(jnp.int32, (128, 128), 1) < 64
    for q in range(8):
        outer = dot(left_ref[64 * q : 64 * q + 64, :], right_ref[...])
        stacked = jnp.concatenate(
            [
                jnp.concatenate(
                    [outer[32 * e : 32 * e + 32, 128 * d : 128 * d + 128] for d in range(16)],
                    axis=0,
                )
                for e in range(2)
            ],
            axis=1,
        )
        high, low = split(stacked)
        y = dot(weight_high, high) + dot(weight_high, low) + dot(weight_low, high)
        top, bottom = y[0:128], y[128:256]
        total = jnp.where(
            lane,
            top[:, 0:128] + pltpu.roll(bottom[:, 0:128], 64, 1),
            pltpu.roll(top[:, 128:256], 64, 1) + bottom[:, 128:256],
        )
        total = jnp.transpose(total)
        for e in range(2):
            i = 2 * q + e
            norm = count * rows_live_ref[i] * cols_live_ref[...] + 0.001
            out_ref[i] = pair_ref[i] + total[64 * e : 64 * e + 64] / norm


def spec(count):
    return [pl.BlockSpec(memory_space=pltpu.VMEM)] * count


def smem(count):
    return [pl.BlockSpec(memory_space=pltpu.SMEM)] * count


def struct(*shape, dtype=f32):
    return jax.ShapeDtypeStruct(shape, dtype)


def call(kernel, numbers, inputs, outputs, scratch=(), limit=48, flops=0, touched=0):
    return pl.pallas_call(
        kernel,
        in_specs=smem(numbers) + spec(inputs),
        out_specs=spec(len(outputs)),
        out_shape=outputs,
        scratch_shapes=list(scratch),
        compiler_params=pltpu.CompilerParams(vmem_limit_bytes=limit * MIB),
        cost_estimate=pl.CostEstimate(flops=flops, bytes_accessed=touched, transcendentals=0),
    )


def body(
    sequence_matrix,
    pair_representation,
    alignment_row_mask,
    residue_mask,
    attention_scale_vector,
    asking_factor_matrix,
    lookup_factor_matrix,
    content_factor_matrix,
    sigmoid_factor_matrix,
    final_factor_matrix,
    pair_norm_gain,
    bias_weight,
    tensor_scale_vector,
    first_factor_matrix,
    second_factor_matrix,
    outer_weight,
):
    head_index = lax.axis_index("head")
    row_index = lax.axis_index("row")
    both = ("row", "head")
    everyone = lax.all_to_all(
        jnp.broadcast_to(sequence_matrix[None], (H, *sequence_matrix.shape)),
        "head",
        0,
        0,
        tiled=True,
    )
    (block,) = call(bias_kernel, 0, 3, [struct(1, 64, 128)], flops=2 * 1024 * 128 * 128 * 6, touched=600000)(
        pair_representation, pair_norm_gain[None], bias_weight
    )
    bias = gather_row(lax.ppermute(block, both, bias_moves()))

    residue_live = residue_mask.astype(f32)
    key_bias = jnp.broadcast_to(((residue_live - 1.0) * 1000000000.0)[:, None], (512, 128))
    cols_live = lax.dynamic_slice_in_dim(residue_live, head_index * 64, 64)
    rows_live = lax.dynamic_slice_in_dim(residue_live, row_index * 16, 16)
    row_live = alignment_row_mask.astype(f32)
    live = (row_live[:, None] * cols_live[None, :]).reshape(128, 1)
    mask_tile = jnp.zeros((8, 128), f32).at[0, 0:2].set(row_live)
    device_tables = lax.dynamic_index_in_dim(
        jnp.asarray(TABLES), row_index * H + head_index, 0, keepdims=False
    )
    weight = (
        outer_weight.reshape(32, 16, 2, 128).transpose(2, 3, 1, 0).reshape(256, 512)
    )

    logits, vh, vl, gate = call(
        logits_kernel,
        0,
        7,
        [
            struct(2, 512, 512),
            struct(2, 256, 512, dtype=bf16),
            struct(2, 256, 512, dtype=bf16),
            struct(128, 256),
        ],
        flops=6 * 2 * 1024 * 256 * 1024,
        touched=6 * MIB,
    )(
        everyone,
        sequence_matrix,
        attention_scale_vector[None],
        asking_factor_matrix,
        lookup_factor_matrix,
        content_factor_matrix,
        sigmoid_factor_matrix,
    )
    msa_out, left, right = call(
        attend_kernel,
        1,
        13,
        [struct(2, 64, 256), struct(4, 8, 128), struct(1, 40, 128)],
        scratch=[pltpu.VMEM((128, 128), f32)],
        flops=3 * 2 * 1024 * 512 * 256,
        touched=6 * MIB,
    )(
        device_tables[0:32],
        bias,
        logits,
        key_bias,
        vh,
        vl,
        gate,
        sequence_matrix,
        final_factor_matrix,
        tensor_scale_vector[None],
        jnp.tile(first_factor_matrix, (1, 4)),
        second_factor_matrix.T,
        live,
        mask_tile,
    )
    left = lax.ppermute(left, both, [(d, s) for s, d in bias_moves()])
    right = gather_row(right)
    left = lax.all_to_all(
        jnp.broadcast_to(left[:, None], (A, H, 8, 128)).reshape(A * H, 8, 128),
        both,
        0,
        0,
        tiled=True,
        axis_index_groups=[[32 * z + k for k in range(32)] for z in range(Z)],
    )
    (pair_out,) = call(
        outer_kernel,
        2,
        5,
        [struct(16, 64, 128)],
        scratch=[
            pltpu.VMEM((256, 128), f32),
            pltpu.VMEM((512, 256), bf16),
            pltpu.VMEM((256, 2048), bf16),
        ],
        flops=3 * 2 * 1024 * 1024 * 256,
        touched=4 * MIB,
    )(
        device_tables[32:64],
        rows_live,
        left,
        right.reshape(32 * 40, 128),
        weight,
        pair_representation,
        cols_live[:, None],
    )
    return msa_out, pair_out


def solution(mesh):
    cells = P("row", "head", None)
    return jax.shard_map(
        body,
        mesh=mesh,
        in_specs=(cells, cells, P("row")) + (P(),) * 13,
        out_specs=(cells, cells),
        check_vma=False,
    )
```

profile of v0, /device:TPU:1, one launch (start us, length us, event | category | flops | bytes accessed | tf_op | source)
XLA Modules:
  0.0 111.9 jit_solution(16747626550088567851)
XLA Ops:
  0.6 0.0 copy-start.16
  0.6 0.0 copy-start.20
  0.7 0.8 copy.24.weight_ref
  1.5 1.0 copy-done.4
  2.5 0.7 copy-done.11
  3.1 0.9 shard_map.176
  4.0 7.8 %collective-permute-start = (f32[1,64,128]{2,1,0:T(8,128)S(1)}, f32[1,64,128]{2,1,0:T(8,128)S(1)}, u32[]{:S(2)}, u32[]{:S(2)}) collective-permute-start(f32[1,64,128]{2,1,0:T(8,128)S(1)} %shard_map.176), channel_id=1, source_target_pairs={{0,128},{1,64},{2,96},{3,32},{4,192},{5,0},{6,160},{7,224},{8,136}... | collective-permute-start | bytes 98312 | tf_op jit(solution)/shard_map/ppermute | solution.py:326
  11.8 2.0 %broadcast_in_dim.15 = f32[8,2,64,256]{3,2,1,0:T(8,128)} broadcast(f32[2,64,256]{2,1,0:T(8,128)} %own_ref.3), dimensions={1,2,3} | broadcast | bytes 1179648 | tf_op jit(solution)/shard_map/broadcast_in_dim | solution.py:317
  13.8 0.0 copy-start.9
  13.9 0.0 copy-start.10
  13.9 4.9 %all-to-all-start = ((f32[8,2,64,256]{3,2,1,0:T(8,128)}), f32[8,2,64,256]{3,2,1,0:T(8,128)S(1)}, u32[]{:S(2)}, u32[]{:S(2)}) async-start(f32[8,2,64,256]{3,2,1,0:T(8,128)} %broadcast_in_dim.15), calls=%async_computation | async-start | bytes 2097152 | tf_op jit(solution)/shard_map/all_to_all | solution.py:316
  18.8 0.0 collective-permute-done
  18.8 3.1 %collective-permute-start.1 = (f32[1,64,128]{2,1,0:T(8,128)S(1)}, f32[1,64,128]{2,1,0:T(8,128)S(1)}, u32[]{:S(2)}, u32[]{:S(2)}) collective-permute-start(f32[1,64,128]{2,1,0:T(8,128)S(1)} %collective-permute-done), channel_id=1, source_target_pairs={{0,128},{8,136},{16,144},{24,152},{32,160},{40,168},{48,176},{56,1... | collective-permute-start | bytes 98312 | tf_op jit(solution)/shard_map/ppermute | solution.py:70
  21.9 0.1 dynamic_slice.11
  22.0 3.6 %collective-permute-done.1 = f32[1,64,128]{2,1,0:T(8,128)S(1)} collective-permute-done((f32[1,64,128]{2,1,0:T(8,128)S(1)}, f32[1,64,128]{2,1,0:T(8,128)S(1)}, u32[]{:S(2)}, u32[]{:S(2)}) %collective-permute-start.1) | collective-permute-done | bytes 32800 | tf_op jit(solution)/shard_map/ppermute | solution.py:70
  25.6 0.7 collective-permute-start.2
  26.2 0.1 broadcast_multiply_fusion
  26.3 3.7 %collective-permute-done.2 = f32[2,64,128]{2,1,0:T(8,128)S(1)} collective-permute-done((f32[2,64,128]{2,1,0:T(8,128)S(1)}, f32[2,64,128]{2,1,0:T(8,128)S(1)}, u32[]{:S(2)}, u32[]{:S(2)}) %collective-permute-start.2) | collective-permute-done | bytes 65568 | tf_op jit(solution)/shard_map/ppermute | solution.py:70
  30.0 0.7 pad_maximum_fusion.2
  30.6 1.7 %collective-permute-start.3 = (f32[4,64,128]{2,1,0:T(8,128)}, f32[4,64,128]{2,1,0:T(8,128)}, u32[]{:S(2)}, u32[]{:S(2)}) collective-permute-start(f32[4,64,128]{2,1,0:T(8,128)} %pad_maximum_fusion.2), channel_id=1, source_target_pairs={{0,32},{8,40},{16,48},{24,56},{32,0},{40,8},{48,16},{56,24},{64,96... | collective-permute-start | bytes 393224 | tf_op jit(solution)/shard_map/ppermute | solution.py:70
  32.3 1.3 %constant_dynamic-slice_fusion = s32[1,64]{1,0:T(1,128)} fusion(s32[256,64]{1,0:T(8,128)} %constant.58.clone, s32[]{:T(128)S(6)} %select_n.10), kind=kLoop, calls=%fused_computation.33 | loop fusion | bytes 516 | tf_op jit(solution)/shard_map/jit(dynamic_index_in_dim)/dynamic_slice | solution.py:335
  33.6 0.1 copy.25.first_ref
  33.7 0.1 mul.47.live_ref
  33.9 1.4 %constant_dynamic-update-slice_fusion.4 = (f32[16,64,128]{2,1,0:T(8,128)}, f32[32,64,128]{2,1,0:T(8,128)S(1)}) fusion(f32[1,64,128]{2,1,0:T(8,128)} %copy-done.13), kind=kLoop, calls=%fused_computation.10 | loop fusion | bytes 98304
  35.3 0.0 collective-permute-done.3
  35.3 0.9 pad_maximum_fusion
  36.2 1.7 %collective-permute-start.4 = (f32[8,64,128]{2,1,0:T(8,128)S(1)}, f32[8,64,128]{2,1,0:T(8,128)S(1)}, u32[]{:S(2)}, u32[]{:S(2)}) collective-permute-start(f32[8,64,128]{2,1,0:T(8,128)S(1)} %pad_maximum_fusion), channel_id=1, source_target_pairs={{0,16},{8,24},{16,0},{24,8},{32,48},{40,56},{48,32},{56,40},{64,80... | collective-permute-start | bytes 786440 | tf_op jit(solution)/shard_map/ppermute | solution.py:70
  37.9 1.4 %constant_dynamic-update-slice_fusion.3 = (f32[16,64,128]{2,1,0:T(8,128)}, f32[32,64,128]{2,1,0:T(8,128)S(1)}) fusion(f32[16,64,128]{2,1,0:T(8,128)} %get-tuple-element.42, f32[1,64,128]{2,1,0:T(8,128)} %copy-done.14, f32[32,64,128]{2,1,0:T(8,128)S(1)} %get-tuple-element.43), kind=kLoop, calls=%fused_computation.9 | loop fusion | bytes 98304
  39.3 0.6 constant_dynamic-update-slice_fusion.2
  39.9 1.6 %constant_dynamic-update-slice_fusion.1 = (f32[16,64,128]{2,1,0:T(8,128)}, f32[32,64,128]{2,1,0:T(8,128)S(1)}) fusion(f32[16,64,128]{2,1,0:T(8,128)} %get-tuple-element.36, f32[4,64,128]{2,1,0:T(8,128)} %collective-permute-done.3, f32[32,64,128]{2,1,0:T(8,128)S(1)} %get-tuple-element.37), kind=kLoop, calls=%fused_computation.7 | loop fusion | bytes 393216
  41.5 0.2 collective-permute-done.4
  41.7 0.7 constant_dynamic-update-slice_fusion
  42.4 5.0 %collective-permute-start.5 = (f32[16,64,128]{2,1,0:T(8,128)}, f32[16,64,128]{2,1,0:T(8,128)}, u32[]{:S(2)}, u32[]{:S(2)}) collective-permute-start(f32[16,64,128]{2,1,0:T(8,128)} %get-tuple-element.28), channel_id=1, source_target_pairs={{0,8},{8,0},{16,24},{24,16},{32,40},{40,32},{48,56},{56,48},{64,72... | collective-permute-start | bytes 1572872 | tf_op jit(solution)/shard_map/ppermute | solution.py:70
  47.5 0.1 slice_bitcast_fusion
  47.5 0.0 all-to-all-done.all_ref
  47.6 0.0 copy-start.1
  47.6 0.0 copy-start.2
  47.6 0.0 copy-start.3
  47.6 4.1 %shard_map.177 = (f32[2,512,512]{2,1,0:T(8,128)S(1)}, bf16[2,256,512]{2,1,0:T(8,128)(2,1)S(1)}, bf16[2,256,512]{2,1,0:T(8,128)(2,1)S(1)}, f32[128,256]{1,0:T(8,128)S(1)}) custom-call(f32[8,2,64,256]{3,2,1,0:T(8,128)S(1)} %all-to-all-done.all_ref, f32[2,64,256]{2,1,0:T(8,128)S(1)} %copy-done, f32[1,256]{1,0:T(1,128)S(1)} %bitcast.27, ...), custom_call_target="tpu_custom_call" | custom-call | flops 3221225472 | bytes 6291456 | tf_op jit(solution)/shard_map/pallas_call | solution.py:342
  51.8 0.0 collective-permute-done.5
  51.8 1.1 constant_dynamic-update-slice_fusion.5.bias_ref
  52.9 0.1 broadcast_in_dim.17.key_ref
  53.1 4.1 %shard_map.178 = (f32[2,64,256]{2,1,0:T(8,128)}, f32[4,8,128]{2,1,0:T(8,128)S(1)}, f32[1,40,128]{2,1,0:T(8,128)S(1)}) custom-call(s32[32]{0:T(128)S(1)} %get-tuple-element.49.index_ref, f32[32,64,128]{2,1,0:T(8,128)S(1)} %constant_dynamic-update-slice_fusion.5.bias_ref, f32[2,512,512]{2,1,0:T(8,128)S(1)} %get-tuple-element.21.logit_ref, ...), custom_call_target="tpu_custom_call" | custom-call | flops 805306368 | bytes 6291456 | tf_op jit(solution)/shard_map/pallas_call | solution.py:363
  57.2 3.0 %collective-permute-start.7 = (f32[1,40,128]{2,1,0:T(8,128)S(1)}, f32[1,40,128]{2,1,0:T(8,128)S(1)}, u32[]{:S(2)}, u32[]{:S(2)}) collective-permute-start(f32[1,40,128]{2,1,0:T(8,128)S(1)} %get-tuple-element.27), channel_id=1, source_target_pairs={{0,128},{8,136},{16,144},{24,152},{32,160},{40,168},{48,176},{56,1... | collective-permute-start | bytes 61448 | tf_op jit(solution)/shard_map/ppermute | solution.py:70
  60.2 3.5 %collective-permute-done.7 = f32[1,40,128]{2,1,0:T(8,128)S(1)} collective-permute-done((f32[1,40,128]{2,1,0:T(8,128)S(1)}, f32[1,40,128]{2,1,0:T(8,128)S(1)}, u32[]{:S(2)}, u32[]{:S(2)}) %collective-permute-start.7) | collective-permute-done | bytes 20512 | tf_op jit(solution)/shard_map/ppermute | solution.py:70
  63.7 1.7 %collective-permute-start.8 = (f32[2,40,128]{2,1,0:T(8,128)S(1)}, f32[2,40,128]{2,1,0:T(8,128)S(1)}, u32[]{:S(2)}, u32[]{:S(2)}) collective-permute-start(f32[2,40,128]{2,1,0:T(8,128)S(1)} %pad_maximum_fusion.5), channel_id=1, source_target_pairs={{0,64},{8,72},{16,80},{24,88},{32,96},{40,104},{48,112},{56,120},{... | collective-permute-start | bytes 122888 | tf_op jit(solution)/shard_map/ppermute | solution.py:70
  65.4 2.1 %collective-permute-done.8 = f32[2,40,128]{2,1,0:T(8,128)S(1)} collective-permute-done((f32[2,40,128]{2,1,0:T(8,128)S(1)}, f32[2,40,128]{2,1,0:T(8,128)S(1)}, u32[]{:S(2)}, u32[]{:S(2)}) %collective-permute-start.8) | collective-permute-done | bytes 40992 | tf_op jit(solution)/shard_map/ppermute | solution.py:70
  67.5 1.5 %collective-permute-start.9 = (f32[4,40,128]{2,1,0:T(8,128)S(1)}, f32[4,40,128]{2,1,0:T(8,128)S(1)}, u32[]{:S(2)}, u32[]{:S(2)}) collective-permute-start(f32[4,40,128]{2,1,0:T(8,128)S(1)} %pad_maximum_fusion.3), channel_id=1, source_target_pairs={{0,32},{8,40},{16,48},{24,56},{32,0},{40,8},{48,16},{56,24},{64,96... | collective-permute-start | bytes 245768 | tf_op jit(solution)/shard_map/ppermute | solution.py:70
  69.0 1.8 %collective-permute-done.9 = f32[4,40,128]{2,1,0:T(8,128)S(1)} collective-permute-done((f32[4,40,128]{2,1,0:T(8,128)S(1)}, f32[4,40,128]{2,1,0:T(8,128)S(1)}, u32[]{:S(2)}, u32[]{:S(2)}) %collective-permute-start.9) | collective-permute-done | bytes 81952 | tf_op jit(solution)/shard_map/ppermute | solution.py:70
  70.8 2.1 %collective-permute-start.10 = (f32[8,40,128]{2,1,0:T(8,128)S(1)}, f32[8,40,128]{2,1,0:T(8,128)S(1)}, u32[]{:S(2)}, u32[]{:S(2)}) collective-permute-start(f32[8,40,128]{2,1,0:T(8,128)S(1)} %pad_maximum_fusion.1), channel_id=1, source_target_pairs={{0,16},{8,24},{16,0},{24,8},{32,48},{40,56},{48,32},{56,40},{64,80... | collective-permute-start | bytes 491528 | tf_op jit(solution)/shard_map/ppermute | solution.py:70
  73.0 2.7 %collective-permute-done.10 = f32[8,40,128]{2,1,0:T(8,128)S(1)} collective-permute-done((f32[8,40,128]{2,1,0:T(8,128)S(1)}, f32[8,40,128]{2,1,0:T(8,128)S(1)}, u32[]{:S(2)}, u32[]{:S(2)}) %collective-permute-start.10) | collective-permute-done | bytes 163872 | tf_op jit(solution)/shard_map/ppermute | solution.py:70
  75.7 4.4 %collective-permute-start.11 = (f32[16,40,128]{2,1,0:T(8,128)S(1)}, f32[16,40,128]{2,1,0:T(8,128)S(1)}, u32[]{:S(2)}, u32[]{:S(2)}) collective-permute-start(f32[16,40,128]{2,1,0:T(8,128)S(1)} %get-tuple-element.30), channel_id=1, source_target_pairs={{0,8},{8,0},{16,24},{24,16},{32,40},{40,32},{48,56},{56,48},{64,72... | collective-permute-start | bytes 983048 | tf_op jit(solution)/shard_map/ppermute | solution.py:70
  80.1 6.7 %collective-permute-start.6 = (f32[4,8,128]{2,1,0:T(8,128)S(1)}, f32[4,8,128]{2,1,0:T(8,128)S(1)}, u32[]{:S(2)}, u32[]{:S(2)}) collective-permute-start(f32[4,8,128]{2,1,0:T(8,128)S(1)} %get-tuple-element.26), channel_id=1, source_target_pairs={{128,0},{64,1},{96,2},{32,3},{192,4},{0,5},{160,6},{224,7},{136,8}... | collective-permute-start | bytes 49160 | tf_op jit(solution)/shard_map/ppermute | solution.py:387
  86.8 0.9 collective-permute-done.6
  87.7 0.7 broadcast_in_dim.38
  88.3 10.3 %all-to-all-start.1 = ((f32[32,8,128]{2,1,0:T(8,128)}), f32[32,8,128]{2,1,0:T(8,128)S(1)}, u32[]{:S(2)}, u32[]{:S(2)}) async-start(f32[32,8,128]{2,1,0:T(8,128)} %bitcast.8), calls=%async_computation.1 | async-start | bytes 262144 | tf_op jit(solution)/shard_map/all_to_all | solution.py:389
  98.7 0.1 dynamic-slice_bitcast_fusion
  98.8 0.1 dynamic_slice.12.rows_live_ref
  98.9 0.3 copy.27
  99.2 0.2 copy.28.weight_ref
  99.4 0.1 copy.29.cols_live_ref
  99.5 0.0 collective-permute-done.11
  99.5 6.9 %all-to-all-done.1.left_in_ref = f32[32,8,128]{2,1,0:T(8,128)S(1)} async-done(((f32[32,8,128]{2,1,0:T(8,128)}), f32[32,8,128]{2,1,0:T(8,128)S(1)}, u32[]{:S(2)}, u32[]{:S(2)}) %all-to-all-start.1) | async-done | bytes 131104 | tf_op jit(solution)/shard_map/all_to_all | solution.py:389
  106.4 5.5 %shard_map.179 = f32[16,64,128]{2,1,0:T(8,128)} custom-call(s32[32]{0:T(128)S(1)} %get-tuple-element.48.index_ref, f32[16]{0:T(128)S(1)} %dynamic_slice.12.rows_live_ref, f32[32,8,128]{2,1,0:T(8,128)S(1)} %all-to-all-done.1.left_in_ref, f32[1280,128]{1,0:T(8,128)S(1)} %bitcast.26, f32[256,512]{1,0:T(8,128)S(1)} %copy.28.weight_ref, ...), custom_call_target="tpu_custom_call" | custom-call | flops 1610612736 | bytes 4194304 | tf_op jit(solution)/shard_map/pallas_call | solution.py:397
  (49 shorter events, 0.2 us)
Async XLA Ops:
  0.6 18.1 %copy-start.16 = (s32[512]{0:T(512)S(1)}, s32[512]{0:T(512)}, u32[]{:S(2)}) copy-start(s32[512]{0:T(512)} %param.22) | copy-start | bytes 6148
  0.6 21.3 %copy-start.20 = (s32[2]{0:T(128)S(1)}, s32[2]{0:T(128)}, u32[]{:S(2)}) copy-start(s32[2]{0:T(128)} %param.21) | copy-start | bytes 28
  1.4 1.0 copy-start.4
  2.5 0.7 copy-start.11
  3.1 30.4 %copy-start.15 = (f32[256,32]{0,1:T(8,128)S(1)}, f32[256,32]{0,1:T(8,128)}, u32[]{:S(2)}) copy-start(f32[256,32]{0,1:T(8,128)} %param.32) | copy-start | bytes 98308
  4.0 14.8 %collective-permute-start = (f32[1,64,128]{2,1,0:T(8,128)S(1)}, f32[1,64,128]{2,1,0:T(8,128)S(1)}, u32[]{:S(2)}, u32[]{:S(2)}) collective-permute-start(f32[1,64,128]{2,1,0:T(8,128)S(1)} %shard_map.176), channel_id=1, source_target_pairs={{0,128},{1,64},{2,96},{3,32},{4,192},{5,0},{6,160},{7,224},{8,136}... | collective-permute-start | bytes 98312 | tf_op jit(solution)/shard_map/ppermute | solution.py:326
  13.8 33.7 %copy-start = (f32[2,64,256]{2,1,0:T(8,128)S(1)}, f32[2,64,256]{2,1,0:T(8,128)}, u32[]{:S(2)}) copy-start(f32[2,64,256]{2,1,0:T(8,128)} %own_ref.3) | copy-start | bytes 393220
  13.8 33.7 %copy-start.6 = (f32[256,256]{1,0:T(8,128)S(1)}, f32[256,256]{1,0:T(8,128)}, u32[]{:S(2)}) copy-start(f32[256,256]{1,0:T(8,128)} %wq_ref.1) | copy-start | bytes 786436
  13.8 33.7 %copy-start.7 = (f32[256,256]{1,0:T(8,128)S(1)}, f32[256,256]{1,0:T(8,128)}, u32[]{:S(2)}) copy-start(f32[256,256]{1,0:T(8,128)} %wk_ref.1) | copy-start | bytes 786436
  13.8 33.7 %copy-start.8 = (f32[256,256]{1,0:T(8,128)S(1)}, f32[256,256]{1,0:T(8,128)}, u32[]{:S(2)}) copy-start(f32[256,256]{1,0:T(8,128)} %wv_ref.1) | copy-start | bytes 786436
  13.8 33.7 %copy-start.9 = (f32[256,256]{1,0:T(8,128)S(1)}, f32[256,256]{1,0:T(8,128)}, u32[]{:S(2)}) copy-start(f32[256,256]{1,0:T(8,128)} %wg_ref.1) | copy-start | bytes 786436
  13.9 33.7 %copy-start.10 = (f32[256]{0:T(256)S(1)}, f32[256]{0:T(256)}, u32[]{:S(2)}) copy-start(f32[256]{0:T(256)} %param.23) | copy-start | bytes 3076
  13.9 33.7 %all-to-all-start = ((f32[8,2,64,256]{3,2,1,0:T(8,128)}), f32[8,2,64,256]{3,2,1,0:T(8,128)S(1)}, u32[]{:S(2)}, u32[]{:S(2)}) async-start(f32[8,2,64,256]{3,2,1,0:T(8,128)} %broadcast_in_dim.15), calls=%async_computation | async-start | bytes 2097152 | tf_op jit(solution)/shard_map/all_to_all | solution.py:316
  18.8 14.8 %copy-start.13 = (f32[1,64,128]{2,1,0:T(8,128)}, f32[1,64,128]{2,1,0:T(8,128)S(1)}, u32[]{:S(2)}) copy-start(f32[1,64,128]{2,1,0:T(8,128)S(1)} %collective-permute-done) | copy-start | bytes 98308
  18.8 6.8 %collective-permute-start.1 = (f32[1,64,128]{2,1,0:T(8,128)S(1)}, f32[1,64,128]{2,1,0:T(8,128)S(1)}, u32[]{:S(2)}, u32[]{:S(2)}) collective-permute-start(f32[1,64,128]{2,1,0:T(8,128)S(1)} %collective-permute-done), channel_id=1, source_target_pairs={{0,128},{8,136},{16,144},{24,152},{32,160},{40,168},{48,176},{56,1... | collective-permute-start | bytes 98312 | tf_op jit(solution)/shard_map/ppermute | solution.py:70
  21.9 4.3 %copy-start.17 = (f32[512]{0:T(512)}, f32[512]{0:T(512)S(1)}, u32[]{:S(2)}) copy-start(f32[512]{0:T(512)S(1)} %convert_element_type.6) | copy-start | bytes 6148
  25.6 8.0 %copy-start.14 = (f32[1,64,128]{2,1,0:T(8,128)}, f32[1,64,128]{2,1,0:T(8,128)S(1)}, u32[]{:S(2)}) copy-start(f32[1,64,128]{2,1,0:T(8,128)S(1)} %collective-permute-done.1) | copy-start | bytes 98308
  25.6 4.4 %collective-permute-start.2 = (f32[2,64,128]{2,1,0:T(8,128)S(1)}, f32[2,64,128]{2,1,0:T(8,128)S(1)}, u32[]{:S(2)}, u32[]{:S(2)}) collective-permute-start(f32[2,64,128]{2,1,0:T(8,128)S(1)} %pad_maximum_fusion.4), channel_id=1, source_target_pairs={{0,64},{8,72},{16,80},{24,88},{32,96},{40,104},{48,112},{56,120},{... | collective-permute-start | bytes 196616 | tf_op jit(solution)/shard_map/ppermute | solution.py:70
  30.6 4.6 %collective-permute-start.3 = (f32[4,64,128]{2,1,0:T(8,128)}, f32[4,64,128]{2,1,0:T(8,128)}, u32[]{:S(2)}, u32[]{:S(2)}) collective-permute-start(f32[4,64,128]{2,1,0:T(8,128)} %pad_maximum_fusion.2), channel_id=1, source_target_pairs={{0,32},{8,40},{16,48},{24,56},{32,0},{40,8},{48,16},{56,24},{64,96... | collective-permute-start | bytes 393224 | tf_op jit(solution)/shard_map/ppermute | solution.py:70
  33.9 13.6 %copy-start.19 = (s32[1,64]{1,0:T(1,128)S(1)}, s32[1,64]{1,0:T(1,128)}, u32[]{:S(2)}) copy-start(s32[1,64]{1,0:T(1,128)} %constant_dynamic-slice_fusion) | copy-start | bytes 772
  36.2 5.5 %collective-permute-start.4 = (f32[8,64,128]{2,1,0:T(8,128)S(1)}, f32[8,64,128]{2,1,0:T(8,128)S(1)}, u32[]{:S(2)}, u32[]{:S(2)}) collective-permute-start(f32[8,64,128]{2,1,0:T(8,128)S(1)} %pad_maximum_fusion), channel_id=1, source_target_pairs={{0,16},{8,24},{16,0},{24,8},{32,48},{40,56},{48,32},{56,40},{64,80... | collective-permute-start | bytes 786440 | tf_op jit(solution)/shard_map/ppermute | solution.py:70
  42.4 9.4 %collective-permute-start.5 = (f32[16,64,128]{2,1,0:T(8,128)}, f32[16,64,128]{2,1,0:T(8,128)}, u32[]{:S(2)}, u32[]{:S(2)}) collective-permute-start(f32[16,64,128]{2,1,0:T(8,128)} %get-tuple-element.28), channel_id=1, source_target_pairs={{0,8},{8,0},{16,24},{24,16},{32,40},{40,32},{48,56},{56,48},{64,72... | collective-permute-start | bytes 1572872 | tf_op jit(solution)/shard_map/ppermute | solution.py:70
  47.6 5.4 %copy-start.1 = (f32[256,256]{1,0:T(8,128)S(1)}, f32[256,256]{1,0:T(8,128)}, u32[]{:S(2)}) copy-start(f32[256,256]{1,0:T(8,128)} %wf_ref.1) | copy-start | bytes 786436
  47.6 5.4 %copy-start.2 = (f32[256,32]{0,1:T(8,128)S(1)}, f32[256,32]{0,1:T(8,128)}, u32[]{:S(2)}) copy-start(f32[256,32]{0,1:T(8,128)} %param.33) | copy-start | bytes 98308
  47.6 5.4 %copy-start.3 = (f32[256]{0:T(256)S(1)}, f32[256]{0:T(256)}, u32[]{:S(2)}) copy-start(f32[256]{0:T(256)} %param.31) | copy-start | bytes 3076
  53.0 45.7 %copy-start.18 = (f32[512]{0:T(512)S(1)}, f32[512]{0:T(512)}, u32[]{:S(2)}) copy-start(f32[512]{0:T(512)} %copy-done.17) | copy-start | bytes 6148
  57.2 41.7 %copy-start.12 = (f32[1024,128]{1,0:T(8,128)S(1)}, f32[1024,128]{1,0:T(8,128)}, u32[]{:S(2)}) copy-start(f32[1024,128]{1,0:T(8,128)} %param.34) | copy-start | bytes 1572868
  57.2 6.6 %collective-permute-start.7 = (f32[1,40,128]{2,1,0:T(8,128)S(1)}, f32[1,40,128]{2,1,0:T(8,128)S(1)}, u32[]{:S(2)}, u32[]{:S(2)}) collective-permute-start(f32[1,40,128]{2,1,0:T(8,128)S(1)} %get-tuple-element.27), channel_id=1, source_target_pairs={{0,128},{8,136},{16,144},{24,152},{32,160},{40,168},{48,176},{56,1... | collective-permute-start | bytes 61448 | tf_op jit(solution)/shard_map/ppermute | solution.py:70
  63.7 3.8 %collective-permute-start.8 = (f32[2,40,128]{2,1,0:T(8,128)S(1)}, f32[2,40,128]{2,1,0:T(8,128)S(1)}, u32[]{:S(2)}, u32[]{:S(2)}) collective-permute-start(f32[2,40,128]{2,1,0:T(8,128)S(1)} %pad_maximum_fusion.5), channel_id=1, source_target_pairs={{0,64},{8,72},{16,80},{24,88},{32,96},{40,104},{48,112},{56,120},{... | collective-permute-start | bytes 122888 | tf_op jit(solution)/shard_map/ppermute | solution.py:70
  67.5 3.3 %collective-permute-start.9 = (f32[4,40,128]{2,1,0:T(8,128)S(1)}, f32[4,40,128]{2,1,0:T(8,128)S(1)}, u32[]{:S(2)}, u32[]{:S(2)}) collective-permute-start(f32[4,40,128]{2,1,0:T(8,128)S(1)} %pad_maximum_fusion.3), channel_id=1, source_target_pairs={{0,32},{8,40},{16,48},{24,56},{32,0},{40,8},{48,16},{56,24},{64,96... | collective-permute-start | bytes 245768 | tf_op jit(solution)/shard_map/ppermute | solution.py:70
  70.8 4.8 %collective-permute-start.10 = (f32[8,40,128]{2,1,0:T(8,128)S(1)}, f32[8,40,128]{2,1,0:T(8,128)S(1)}, u32[]{:S(2)}, u32[]{:S(2)}) collective-permute-start(f32[8,40,128]{2,1,0:T(8,128)S(1)} %pad_maximum_fusion.1), channel_id=1, source_target_pairs={{0,16},{8,24},{16,0},{24,8},{32,48},{40,56},{48,32},{56,40},{64,80... | collective-permute-start | bytes 491528 | tf_op jit(solution)/shard_map/ppermute | solution.py:70
  75.7 23.8 %collective-permute-start.11 = (f32[16,40,128]{2,1,0:T(8,128)S(1)}, f32[16,40,128]{2,1,0:T(8,128)S(1)}, u32[]{:S(2)}, u32[]{:S(2)}) collective-permute-start(f32[16,40,128]{2,1,0:T(8,128)S(1)} %get-tuple-element.30), channel_id=1, source_target_pairs={{0,8},{8,0},{16,24},{24,16},{32,40},{40,32},{48,56},{56,48},{64,72... | collective-permute-start | bytes 983048 | tf_op jit(solution)/shard_map/ppermute | solution.py:70
  80.1 7.6 %collective-permute-start.6 = (f32[4,8,128]{2,1,0:T(8,128)S(1)}, f32[4,8,128]{2,1,0:T(8,128)S(1)}, u32[]{:S(2)}, u32[]{:S(2)}) collective-permute-start(f32[4,8,128]{2,1,0:T(8,128)S(1)} %get-tuple-element.26), channel_id=1, source_target_pairs={{128,0},{64,1},{96,2},{32,3},{192,4},{0,5},{160,6},{224,7},{136,8}... | collective-permute-start | bytes 49160 | tf_op jit(solution)/shard_map/ppermute | solution.py:387
  88.3 18.0 %copy-start.5 = (f32[16,64,128]{2,1,0:T(8,128)S(1)}, f32[16,64,128]{2,1,0:T(8,128)}, u32[]{:S(2)}) copy-start(f32[16,64,128]{2,1,0:T(8,128)} %pair_ref.3) | copy-start | bytes 1572868
  88.3 18.0 %all-to-all-start.1 = ((f32[32,8,128]{2,1,0:T(8,128)}), f32[32,8,128]{2,1,0:T(8,128)S(1)}, u32[]{:S(2)}, u32[]{:S(2)}) async-start(f32[32,8,128]{2,1,0:T(8,128)} %bitcast.8), calls=%async_computation.1 | async-start | bytes 262144 | tf_op jit(solution)/shard_map/all_to_all | solution.py:389
where the time goes:
time: 112 us
  starting transfers between devices  54.7 us (49%)
  waiting for transfers between devices  25.3 us (23%)
  local copies, waits for them, and re-layouts  14.6 us (13%)
  Pallas kernels  14.6 us (13%)
  other arithmetic  1.72 us (2%)
    ppermute x10, starting transfers between devices, gather_row(): other = lax.ppermute(block, 'row', [(r, r ^ step) for r in range(Z * A)])  24.9 us
    ppermute x10, waiting for transfers between devices, gather_row(): other = lax.ppermute(block, 'row', [(r, r ^ step) for r in range(Z * A)])  17.5 us
    all_to_all x1, starting transfers between devices, body(): lax.all_to_all(jnp.broadcast_to(left[:, None], (A, H, 8, 128)).reshape(A...  10.3 us
    ppermute x1, starting transfers between devices, body(): bias = gather_row(lax.ppermute(block, both, bias_moves()))  7.82 us
    unnamed x52, local copies, waits for them, and re-layouts  7.61 us
    all_to_all x1, waiting for transfers between devices, body(): lax.all_to_all(jnp.broadcast_to(left[:, None], (A, H, 8, 128)).reshape(A...  6.87 us
    ppermute x1, starting transfers between devices, body(): left = lax.ppermute(left, both, [(d, s) for s, d in bias_moves()])  6.72 us
    pallas_call x1, Pallas kernels, body(): call(outer_kernel, 2, 5, [struct(16, 64, 128)], scratch=[pltpu.VMEM((256,...  5.47 us
  transfers between devices with their start and end apart: 14, of which 9 were waited for; matrix products, arithmetic and copies ran while one was open for 11% of the time, Pallas kernels for 4%

commit v1 on v0

--- a/solution.py
+++ b/solution.py
@@ -14,9 +14,6 @@
 MIB = 1024 * 1024
 
 Z, A, H = 8, 4, 8
-STEPS = (16, 8, 4, 2, 1)
-
-
 def spread_table():
     far = np.zeros((H, H), np.int32)
     ring = lambda d, n: min(d % n, -d % n)
@@ -32,10 +29,6 @@
 
 
 FAR = spread_table()
-
-
-def reverse_bits(v):
-    return int(format(v, "05b")[::-1], 2)
 
 
 def bias_moves():
@@ -47,29 +40,38 @@
     ]
 
 
-def tables():
-    bias = np.zeros((Z * A, H, 32), np.int32)
-    left = np.zeros((Z * A, H, 32), np.int32)
-    for r in range(Z * A):
-        for h in range(H):
-            for block in range(H):
-                for a in range(A):
-                    bias[r, h, block * A + a] = reverse_bits(r ^ (4 * int(FAR[h][block]) + a))
-            for a in range(A):
-                for column in range(H):
-                    source = 4 * int(FAR[r // 4][column]) + a
-                    left[r, h, a * H + column] = reverse_bits(r ^ source)
-    return np.concatenate([bias, left], axis=-1).reshape(Z * A * H, 64)
-
-
-TABLES = tables()
-
-
-def gather_row(block):
-    for step in STEPS:
-        other = lax.ppermute(block, "row", [(r, r ^ step) for r in range(Z * A)])
-        block = jnp.concatenate([block, other], axis=0)
-    return block
+def from_plane(v, far):
+    return lax.ppermute(v, "row", [(r, (r - 4 * far) % 32) for r in range(Z * A)])
+
+
+def from_neighbour(v, bit):
+    return lax.ppermute(v, "row", [(r, r ^ bit) for r in range(Z * A)])
+
+
+def gather_row(own, before_far=None, before_side=None):
+    near = jnp.concatenate([from_plane(own, -1), own, from_plane(own, 1)], axis=0)
+    if before_far is not None:
+        near = lax.optimization_barrier((near, before_far))[0]
+    pieces = [near, from_plane(near, 3), from_plane(near[1:3], -3)]
+    if before_side is not None:
+        pieces = list(lax.optimization_barrier((*pieces, before_side)))[:3]
+    sides = [from_neighbour(p, 2) for p in pieces]
+    return (
+        pieces
+        + [from_neighbour(p, 1) for p in pieces]
+        + sides
+        + [from_neighbour(p, 1) for p in sides]
+    )
+
+
+SIZES = (3, 3, 2) * 4
+STARTS = tuple(sum(SIZES[:k]) for k in range(12))
+
+
+def position(row, source_plane, source_side):
+    side = jnp.bitwise_xor(jnp.bitwise_and(row, 3), source_side)
+    plane = jnp.bitwise_and(source_plane - jnp.right_shift(row, 2) + 1, 7)
+    return side * 8 + plane
 
 
 def split(v):
@@ -91,19 +93,26 @@
     return center * lax.rsqrt(spread + 1e-05) * gain
 
 
-def bias_kernel(pair_ref, gain_ref, weight_ref, out_ref):
+def bias_kernel(pair_ref, gain_ref, weight_ref, own_ref, out_ref, copies_ref, sems):
+    copies = [
+        pltpu.make_async_copy(own_ref, copies_ref.at[k], sems.at[k]) for k in range(H)
+    ]
+    for copy in copies:
+        copy.start()
     rows = pair_ref[...].reshape(1024, 128)
     normed = norm_rows(rows, gain_ref[...])
     pick = lax.broadcasted_iota(jnp.int32, (8, 128), 0) == (
         lax.broadcasted_iota(jnp.int32, (8, 128), 1) // 16
     )
-    wide = dot_exact(weight_ref[...], jnp.where(pick, 1.0, 0.0))
+    wide = dot_exact(weight_ref[...], jnp.where(pick, 1.0, 0.0), ((0,), (0,)))
     result = dot_exact(normed, wide)
     lane = lax.broadcasted_iota(jnp.int32, (64, 128), 1) % 16
     total = jnp.zeros((64, 128), f32)
     for i in range(16):
         total = jnp.where(lane == i, result[64 * i : 64 * i + 64], total)
     out_ref[0] = total
+    for copy in copies:
+        copy.wait()
 
 
 def logits_kernel(
@@ -133,8 +142,15 @@
 
 
 def attend_kernel(
-    index_ref,
-    bias_ref,
+    far_ref,
+    *refs,
+):
+    attend(far_ref, refs[:12], *refs[12:])
+
+
+def attend(
+    far_ref,
+    piece_refs,
     logit_ref,
     key_ref,
     vh_ref,
@@ -150,8 +166,13 @@
     msa_ref,
     left_ref,
     right_ref,
+    bias_ref,
     y_ref,
 ):
+    for piece_ref, start, size in zip(piece_refs, STARTS, SIZES):
+        bias_ref[start : start + size] = piece_ref[...]
+    row = lax.axis_index("row")
+    column = lax.axis_index("head")
     lane = lax.broadcasted_iota(jnp.int32, (32, 128), 1) // 16
     folded = [jnp.zeros((32, 128), f32) for _ in range(8)]
     for s in range(2):
@@ -161,7 +182,7 @@
             for b in range(8):
                 rows = pl.ds(64 * b, 64)
                 tiles.append(
-                    (logit_ref[s, rows, columns] + bias_ref[index_ref[b * 4 + a]])
+                    (logit_ref[s, rows, columns] + bias_ref[position(row, far_ref[column * H + b], a)])
                     + key_ref[rows, :]
                 )
             logits = jnp.concatenate(tiles, axis=0)
@@ -192,20 +213,34 @@
 
 
 def outer_kernel(
-    index_ref,
+    far_ref,
     rows_live_ref,
+    *refs,
+):
+    outer_product(far_ref, rows_live_ref, refs[:12], *refs[12:])
+
+
+def outer_product(
+    far_ref,
+    rows_live_ref,
+    piece_refs,
     left_in_ref,
-    right_in_ref,
     weight_ref,
     pair_ref,
     cols_live_ref,
     out_ref,
+    right_in_ref,
     sorted_ref,
     left_ref,
     right_ref,
 ):
+    for piece_ref, start, size in zip(piece_refs, STARTS, SIZES):
+        for k in range(size):
+            right_in_ref[40 * (start + k) : 40 * (start + k) + 40, :] = piece_ref[k]
+    row = lax.axis_index("row")
     for p in range(32):
-        spot = pl.multiple_of(index_ref[p] * 8, 8)
+        source = position(row, far_ref[jnp.right_shift(row, 2) * H + p % H], p // H)
+        spot = pl.multiple_of(source * 8, 8)
         sorted_ref[pl.ds(spot, 8), :] = left_in_ref[p]
     count = jnp.zeros((8, 128), f32)
     for k in range(32):
@@ -268,7 +303,7 @@
             out_ref[i] = pair_ref[i] + total[64 * e : 64 * e + 64] / norm
 
 
-def spec(count):
+def vmem(count):
     return [pl.BlockSpec(memory_space=pltpu.VMEM)] * count
 
 
@@ -276,16 +311,20 @@
     return [pl.BlockSpec(memory_space=pltpu.SMEM)] * count
 
 
+def anywhere(count):
+    return [pl.BlockSpec(memory_space=pl.ANY)] * count
+
+
 def struct(*shape, dtype=f32):
     return jax.ShapeDtypeStruct(shape, dtype)
 
 
-def call(kernel, numbers, inputs, outputs, scratch=(), limit=48, flops=0, touched=0):
+def call(kernel, inputs, outputs, shapes, scratch=(), limit=48, flops=0, touched=0):
     return pl.pallas_call(
         kernel,
-        in_specs=smem(numbers) + spec(inputs),
-        out_specs=spec(len(outputs)),
-        out_shape=outputs,
+        in_specs=inputs,
+        out_specs=outputs,
+        out_shape=shapes,
         scratch_shapes=list(scratch),
         compiler_params=pltpu.CompilerParams(vmem_limit_bytes=limit * MIB),
         cost_estimate=pl.CostEstimate(flops=flops, bytes_accessed=touched, transcendentals=0),
@@ -313,16 +352,16 @@
     head_index = lax.axis_index("head")
     row_index = lax.axis_index("row")
     both = ("row", "head")
-    everyone = lax.all_to_all(
-        jnp.broadcast_to(sequence_matrix[None], (H, *sequence_matrix.shape)),
-        "head",
-        0,
-        0,
-        tiled=True,
-    )
-    (block,) = call(bias_kernel, 0, 3, [struct(1, 64, 128)], flops=2 * 1024 * 128 * 128 * 6, touched=600000)(
-        pair_representation, pair_norm_gain[None], bias_weight
-    )
+    block, copies = call(
+        bias_kernel,
+        vmem(3) + anywhere(1),
+        vmem(1) + anywhere(1),
+        [struct(1, 64, 128), struct(H, 2, 64, 256)],
+        scratch=[pltpu.SemaphoreType.DMA((H,))],
+        flops=2 * 1024 * 128 * 128 * 6,
+        touched=600000,
+    )(pair_representation, pair_norm_gain[None], bias_weight.T, sequence_matrix)
+    everyone = lax.all_to_all(copies, "head", 0, 0, tiled=True)
     bias = gather_row(lax.ppermute(block, both, bias_moves()))
 
     residue_live = residue_mask.astype(f32)
@@ -332,17 +371,15 @@
     row_live = alignment_row_mask.astype(f32)
     live = (row_live[:, None] * cols_live[None, :]).reshape(128, 1)
     mask_tile = jnp.zeros((8, 128), f32).at[0, 0:2].set(row_live)
-    device_tables = lax.dynamic_index_in_dim(
-        jnp.asarray(TABLES), row_index * H + head_index, 0, keepdims=False
-    )
+    far = jnp.asarray(FAR.reshape(-1))
     weight = (
         outer_weight.reshape(32, 16, 2, 128).transpose(2, 3, 1, 0).reshape(256, 512)
     )
 
     logits, vh, vl, gate = call(
         logits_kernel,
-        0,
-        7,
+        vmem(7),
+        vmem(4),
         [
             struct(2, 512, 512),
             struct(2, 256, 512, dtype=bf16),
@@ -362,15 +399,15 @@
     )
     msa_out, left, right = call(
         attend_kernel,
-        1,
-        13,
+        smem(1) + vmem(24),
+        vmem(3),
         [struct(2, 64, 256), struct(4, 8, 128), struct(1, 40, 128)],
-        scratch=[pltpu.VMEM((128, 128), f32)],
+        scratch=[pltpu.VMEM((32, 64, 128), f32), pltpu.VMEM((128, 128), f32)],
         flops=3 * 2 * 1024 * 512 * 256,
         touched=6 * MIB,
     )(
-        device_tables[0:32],
-        bias,
+        far,
+        *bias,
         logits,
         key_bias,
         vh,
@@ -385,7 +422,7 @@
         mask_tile,
     )
     left = lax.ppermute(left, both, [(d, s) for s, d in bias_moves()])
-    right = gather_row(right)
+    arrived = left
     left = lax.all_to_all(
         jnp.broadcast_to(left[:, None], (A, H, 8, 128)).reshape(A * H, 8, 128),
         both,
@@ -394,12 +431,14 @@
         tiled=True,
         axis_index_groups=[[32 * z + k for k in range(32)] for z in range(Z)],
     )
+    right = gather_row(right, arrived, left)
     (pair_out,) = call(
         outer_kernel,
-        2,
-        5,
+        smem(2) + vmem(16),
+        vmem(1),
         [struct(16, 64, 128)],
         scratch=[
+            pltpu.VMEM((1280, 128), f32),
             pltpu.VMEM((256, 128), f32),
             pltpu.VMEM((512, 256), bf16),
             pltpu.VMEM((256, 2048), bf16),
@@ -407,10 +446,10 @@
         flops=3 * 2 * 1024 * 1024 * 256,
         touched=4 * MIB,
     )(
-        device_tables[32:64],
+        far,
         rows_live,
+        *right,
         left,
-        right.reshape(32 * 40, 128),
         weight,
         pair_representation,
         cols_live[:, None],

time: 112 us -> 92.2 us (0.82)
  waiting for transfers between devices: 25.3 us -> 10.6 us
  local copies, waits for them, and re-layouts: 14.6 us -> 5.22 us
  starting transfers between devices: 54.7 us -> 60 us
  other arithmetic: 1.72 us -> 0.09 us
    ppermute x10 -> x26, waiting for transfers between devices: 17.5 us -> 9.36 us  [the longest x8 7.72 us: from_plane(): lax.ppermute(v, 'row', [(r, (r - 4 * far) % 32) for r in range(Z * A)])]
    all_to_all x1, waiting for transfers between devices: 6.87 us -> 0.39 us  [body(): lax.all_to_all(jnp.broadcast_to(left[:, None], (A, H, 8, 128)).reshape(A...]
    ppermute x10 -> x26, starting transfers between devices: 24.9 us -> 31.1 us  [the longest x18 19.9 us: from_neighbour(): return lax.ppermute(v, 'row', [(r, r ^ bit) for r in range(Z * A)])]
    unnamed x52 -> x41, local copies, waits for them, and re-layouts: 7.61 us -> 3.41 us
    broadcast_in_dim x1 -> x0, local copies, waits for them, and re-layouts: 2 us -> none  [body(): jnp.broadcast_to(sequence_matrix[None], (H, *sequence_matrix.shape))]
    concatenate x4 -> x1, local copies, waits for them, and re-layouts: 1.86 us -> 0.01 us  [gather_row(): jnp.concatenate([from_plane(own, -1), own, from_plane(own, 1)], axis=0)]
    concatenate x6 -> x2, other arithmetic: 1.64 us -> 0.01 us  [gather_row(): jnp.concatenate([from_plane(own, -1), own, from_plane(own, 1)], axis=0)]
    dynamic_slice x1 -> x0, local copies, waits for them, and re-layouts: 1.27 us -> none  [body(): lax.dynamic_index_in_dim(jnp.asarray(TABLES), row_index * H + head_index,...]
  transfers between devices with their start and end apart: 14 -> 30, of which waited for: 9 -> 8; matrix products, arithmetic and copies ran while one was open for 11% -> 2% of each run, Pallas kernels for 4% -> 4%
where the time goes in v1:
time: 92.2 us; the launch traced here: 91.8 us
  starting transfers between devices  60 us (65%)
  Pallas kernels  14.9 us (16%)
  waiting for transfers between devices  10.6 us (11%)
  local copies, waits for them, and re-layouts  5.22 us (6%)
  between operations  1.01 us (1%)
    ppermute x18, starting transfers between devices, from_neighbour(): return lax.ppermute(v, 'row', [(r, r ^ bit) for r in range(Z * A)])  19.9 us
    ppermute x8, starting transfers between devices, from_plane(): lax.ppermute(v, 'row', [(r, (r - 4 * far) % 32) for r in range(Z * A)])  11.2 us
    all_to_all x1, starting transfers between devices, body(): lax.all_to_all(jnp.broadcast_to(left[:, None], (A, H, 8, 128)).reshape(A...  10.3 us
    ppermute x1, starting transfers between devices, body(): bias = gather_row(lax.ppermute(block, both, bias_moves()))  7.81 us
    ppermute x8, waiting for transfers between devices, from_plane(): lax.ppermute(v, 'row', [(r, (r - 4 * far) % 32) for r in range(Z * A)])  7.72 us
    ppermute x1, starting transfers between devices, body(): left = lax.ppermute(left, both, [(d, s) for s, d in bias_moves()])  6.07 us
    pallas_call x1, Pallas kernels, body(): call(outer_kernel, smem(2) + vmem(16), vmem(1), [struct(16, 64, 128)], sc...  5.5 us
    all_to_all x1, starting transfers between devices, body(): everyone = lax.all_to_all(copies, 'head', 0, 0, tiled=True)  4.74 us
  transfers between devices with their start and end apart: 30, of which 8 were waited for; matrix products, arithmetic and copies ran while one was open for 2% of the time, Pallas kernels for 4%

profile of v1, /device:TPU:1, one launch (start us, length us, event | category | flops | bytes accessed | tf_op | source)
XLA Modules:
  0.0 91.8 jit_solution(18047784516948548474)
XLA Ops:
  0.7 0.9 copy-done.1
  1.6 1.0 %copy-done.6 = f32[16,64,128]{2,1,0:T(8,128)S(1)} copy-done((f32[16,64,128]{2,1,0:T(8,128)S(1)}, f32[16,64,128]{2,1,0:T(8,128)}, u32[]{:S(2)}) %copy-start.6) | copy-done | bytes 524312
  2.6 0.7 copy-done.12
  3.3 0.7 copy-done.14
  4.0 1.1 %shard_map.176 = (f32[1,64,128]{2,1,0:T(8,128)S(1)}, f32[8,2,64,256]{3,2,1,0:T(8,128)}) custom-call(f32[16,64,128]{2,1,0:T(8,128)S(1)} %copy-done.6, f32[1,128]{1,0:T(1,128)S(1)} %bitcast.24, f32[8,128]{1,0:T(8,128)S(1)} %bitcast.22, f32[2,64,256]{2,1,0:T(8,128)S(1)} %copy-done.1), custom_call_target="tpu_custom_call" | custom-call | flops 201326592 | bytes 600000 | tf_op jit(solution)/shard_map/pallas_call | solution.py:355
  5.1 7.8 %collective-permute-start = (f32[1,64,128]{2,1,0:T(8,128)S(1)}, f32[1,64,128]{2,1,0:T(8,128)S(1)}, u32[]{:S(2)}, u32[]{:S(2)}) collective-permute-start(f32[1,64,128]{2,1,0:T(8,128)S(1)} %get-tuple-element.27), channel_id=1, source_target_pairs={{0,128},{1,64},{2,96},{3,32},{4,192},{5,0},{6,160},{7,224},{8,136}... | collective-permute-start | bytes 98312 | tf_op jit(solution)/shard_map/ppermute | solution.py:365
  12.9 4.7 %all-to-all-start = ((f32[8,2,64,256]{3,2,1,0:T(8,128)}), f32[8,2,64,256]{3,2,1,0:T(8,128)S(1)}, u32[]{:S(2)}, u32[]{:S(2)}) async-start(f32[8,2,64,256]{3,2,1,0:T(8,128)} %get-tuple-element.28), calls=%async_computation | async-start | bytes 2097152 | tf_op jit(solution)/shard_map/all_to_all | solution.py:364
  17.6 0.0 collective-permute-done
  17.6 1.8 %collective-permute-start.1 = (f32[1,64,128]{2,1,0:T(8,128)S(1)}, f32[1,64,128]{2,1,0:T(8,128)S(1)}, u32[]{:S(2)}, u32[]{:S(2)}) collective-permute-start(f32[1,64,128]{2,1,0:T(8,128)S(1)} %collective-permute-done), channel_id=1, source_target_pairs={{0,32},{8,40},{16,48},{24,56},{32,64},{40,72},{48,80},{56,88},{64,... | collective-permute-start | bytes 98312 | tf_op jit(solution)/shard_map/ppermute | solution.py:44
  19.4 1.3 %collective-permute-start.2 = (f32[1,64,128]{2,1,0:T(8,128)S(1)}, f32[1,64,128]{2,1,0:T(8,128)S(1)}, u32[]{:S(2)}, u32[]{:S(2)}) collective-permute-start(f32[1,64,128]{2,1,0:T(8,128)S(1)} %collective-permute-done), channel_id=1, source_target_pairs={{0,224},{8,232},{16,240},{24,248},{32,0},{40,8},{48,16},{56,24},{6... | collective-permute-start | bytes 98312 | tf_op jit(solution)/shard_map/ppermute | solution.py:44
  20.7 1.2 %collective-permute-done.1 = f32[1,64,128]{2,1,0:T(8,128)S(1)} collective-permute-done((f32[1,64,128]{2,1,0:T(8,128)S(1)}, f32[1,64,128]{2,1,0:T(8,128)S(1)}, u32[]{:S(2)}, u32[]{:S(2)}) %collective-permute-start.1) | collective-permute-done | bytes 32800 | tf_op jit(solution)/shard_map/ppermute | solution.py:44
  21.9 0.5 collective-permute-done.2
  22.5 1.9 %collective-permute-start.3 = (f32[3,64,128]{2,1,0:T(8,128)S(1)}, f32[3,64,128]{2,1,0:T(8,128)S(1)}, u32[]{:S(2)}, u32[]{:S(2)}) collective-permute-start(f32[3,64,128]{2,1,0:T(8,128)S(1)} %constant_dynamic-update-slice_fusion.refs_0_), channel_id=1, source_target_pairs={{0,160},{8,168},{16,176},{24,184},{32,192},{40,200},{48,208},{56,2... | collective-permute-start | bytes 294920 | tf_op jit(solution)/shard_map/ppermute | solution.py:44
  24.4 1.4 %collective-permute-start.4 = (f32[2,64,128]{2,1,0:T(8,128)S(1)}, f32[2,64,128]{2,1,0:T(8,128)S(1)}, u32[]{:S(2)}, u32[]{:S(2)}) collective-permute-start(f32[2,64,128]{2,1,0:T(8,128)S(1)} %pad_maximum_fusion), channel_id=1, source_target_pairs={{0,96},{8,104},{16,112},{24,120},{32,128},{40,136},{48,144},{56,15... | collective-permute-start | bytes 196616 | tf_op jit(solution)/shard_map/ppermute | solution.py:44
  25.8 0.1 dynamic_slice.6
  25.8 3.0 %collective-permute-start.5 = (f32[3,64,128]{2,1,0:T(8,128)S(1)}, f32[3,64,128]{2,1,0:T(8,128)S(1)}, u32[]{:S(2)}, u32[]{:S(2)}) collective-permute-start(f32[3,64,128]{2,1,0:T(8,128)S(1)} %constant_dynamic-update-slice_fusion.refs_0_), channel_id=1, source_target_pairs={{0,8},{8,0},{16,24},{24,16},{32,40},{40,32},{48,56},{56,48},{64,72... | collective-permute-start | bytes 294920 | tf_op jit(solution)/shard_map/ppermute | solution.py:48
  28.8 0.6 collective-permute-start.8
  29.4 2.1 %collective-permute-done.4.refs_2_ = f32[2,64,128]{2,1,0:T(8,128)S(1)} collective-permute-done((f32[2,64,128]{2,1,0:T(8,128)S(1)}, f32[2,64,128]{2,1,0:T(8,128)S(1)}, u32[]{:S(2)}, u32[]{:S(2)}) %collective-permute-start.4) | collective-permute-done | bytes 65568 | tf_op jit(solution)/shard_map/ppermute | solution.py:44
  31.5 0.5 collective-permute-start.10
  32.0 0.0 collective-permute-done.3.refs_1_
  32.0 1.0 %collective-permute-start.9 = (f32[3,64,128]{2,1,0:T(8,128)S(1)}, f32[3,64,128]{2,1,0:T(8,128)S(1)}, u32[]{:S(2)}, u32[]{:S(2)}) collective-permute-start(f32[3,64,128]{2,1,0:T(8,128)S(1)} %collective-permute-done.3.refs_1_), channel_id=1, source_target_pairs={{0,16},{8,24},{16,0},{24,8},{32,48},{40,56},{48,32},{56,40},{64,80... | collective-permute-start | bytes 294920 | tf_op jit(solution)/shard_map/ppermute | solution.py:48
  33.0 0.1 broadcast_multiply_fusion
  33.0 0.1 copy.23.refs_20_
  33.1 0.1 mul.43.refs_22_
  33.3 4.8 %collective-permute-start.7 = (f32[2,64,128]{2,1,0:T(8,128)S(1)}, f32[2,64,128]{2,1,0:T(8,128)S(1)}, u32[]{:S(2)}, u32[]{:S(2)}) collective-permute-start(f32[2,64,128]{2,1,0:T(8,128)S(1)} %collective-permute-done.4.refs_2_), channel_id=1, source_target_pairs={{0,8},{8,0},{16,24},{24,16},{32,40},{40,32},{48,56},{56,48},{64,72... | collective-permute-start | bytes 196616 | tf_op jit(solution)/shard_map/ppermute | solution.py:48
  38.1 0.1 collective-permute-start.6
  38.2 0.4 collective-permute-start.11
  38.6 1.3 %collective-permute-start.13 = (f32[2,64,128]{2,1,0:T(8,128)S(1)}, f32[2,64,128]{2,1,0:T(8,128)S(1)}, u32[]{:S(2)}, u32[]{:S(2)}) collective-permute-start(f32[2,64,128]{2,1,0:T(8,128)S(1)} %collective-permute-done.10.refs_8_), channel_id=1, source_target_pairs={{0,8},{8,0},{16,24},{24,16},{32,40},{40,32},{48,56},{56,48},{64,72... | collective-permute-start | bytes 196616 | tf_op jit(solution)/shard_map/ppermute | solution.py:48
  39.9 1.9 %collective-permute-start.12 = (f32[3,64,128]{2,1,0:T(8,128)S(1)}, f32[3,64,128]{2,1,0:T(8,128)S(1)}, u32[]{:S(2)}, u32[]{:S(2)}) collective-permute-start(f32[3,64,128]{2,1,0:T(8,128)S(1)} %collective-permute-done.9.refs_7_), channel_id=1, source_target_pairs={{0,8},{8,0},{16,24},{24,16},{32,40},{40,32},{48,56},{56,48},{64,72... | collective-permute-start | bytes 294920 | tf_op jit(solution)/shard_map/ppermute | solution.py:48
  41.8 0.0 copy-start
  41.8 0.0 copy-start.3
  41.9 0.0 copy-start.4
  41.9 0.0 copy-start.5
  41.9 4.1 %shard_map.177 = (f32[2,512,512]{2,1,0:T(8,128)S(1)}, bf16[2,256,512]{2,1,0:T(8,128)(2,1)S(1)}, bf16[2,256,512]{2,1,0:T(8,128)(2,1)S(1)}, f32[128,256]{1,0:T(8,128)S(1)}) custom-call(f32[8,2,64,256]{3,2,1,0:T(8,128)S(1)} %all-to-all-done.all_ref, f32[2,64,256]{2,1,0:T(8,128)S(1)} %copy-done.2, f32[1,256]{1,0:T(1,128)S(1)} %bitcast.23, ...), custom_call_target="tpu_custom_call" | custom-call | flops 3221225472 | bytes 6291456 | tf_op jit(solution)/shard_map/pallas_call | solution.py:379
  46.1 0.1 broadcast_in_dim.14.refs_13_
  46.2 0.0 copy-start.15
  46.2 4.2 %shard_map.178 = (f32[2,64,256]{2,1,0:T(8,128)}, f32[4,8,128]{2,1,0:T(8,128)S(1)}, f32[1,40,128]{2,1,0:T(8,128)S(1)}) custom-call(s32[64]{0:T(128)S(1)} %copy-done.5, f32[3,64,128]{2,1,0:T(8,128)S(1)} %constant_dynamic-update-slice_fusion.refs_0_, f32[3,64,128]{2,1,0:T(8,128)S(1)} %collective-permute-done.3.refs_1_, ...), custom_call_target="tpu_custom_call" | custom-call | flops 805306368 | bytes 6291456 | tf_op jit(solution)/shard_map/pallas_call | solution.py:400
  50.5 0.0 collective-permute-start.15
  50.5 1.4 %collective-permute-start.14 = (f32[1,40,128]{2,1,0:T(8,128)S(1)}, f32[1,40,128]{2,1,0:T(8,128)S(1)}, u32[]{:S(2)}, u32[]{:S(2)}) collective-permute-start(f32[1,40,128]{2,1,0:T(8,128)S(1)} %get-tuple-element.34), channel_id=1, source_target_pairs={{0,32},{8,40},{16,48},{24,56},{32,64},{40,72},{48,80},{56,88},{64,... | collective-permute-start | bytes 61448 | tf_op jit(solution)/shard_map/ppermute | solution.py:44
  51.9 6.1 %collective-permute-start.16 = (f32[4,8,128]{2,1,0:T(8,128)S(1)}, f32[4,8,128]{2,1,0:T(8,128)S(1)}, u32[]{:S(2)}, u32[]{:S(2)}) collective-permute-start(f32[4,8,128]{2,1,0:T(8,128)S(1)} %get-tuple-element.35), channel_id=1, source_target_pairs={{128,0},{64,1},{96,2},{32,3},{192,4},{0,5},{160,6},{224,7},{136,8}... | collective-permute-start | bytes 49160 | tf_op jit(solution)/shard_map/ppermute | solution.py:424
  58.0 0.9 collective-permute-done.16
  58.9 0.7 broadcast_in_dim.31
  59.5 10.3 %all-to-all-start.1 = ((f32[32,8,128]{2,1,0:T(8,128)}), f32[32,8,128]{2,1,0:T(8,128)S(1)}, u32[]{:S(2)}, u32[]{:S(2)}) async-start(f32[32,8,128]{2,1,0:T(8,128)} %bitcast.7), calls=%async_computation.1 | async-start | bytes 262144 | tf_op jit(solution)/shard_map/all_to_all | solution.py:426
  69.9 0.7 collective-permute-start.17
  70.5 2.7 %collective-permute-start.18 = (f32[2,40,128]{2,1,0:T(8,128)S(1)}, f32[2,40,128]{2,1,0:T(8,128)S(1)}, u32[]{:S(2)}, u32[]{:S(2)}) collective-permute-start(f32[2,40,128]{2,1,0:T(8,128)S(1)} %slice.21), channel_id=1, source_target_pairs={{0,96},{8,104},{16,112},{24,120},{32,128},{40,136},{48,144},{56,15... | collective-permute-start | bytes 122888 | tf_op jit(solution)/shard_map/ppermute | solution.py:44
  73.2 3.9 %collective-permute-done.18.refs_2_ = f32[2,40,128]{2,1,0:T(8,128)S(1)} collective-permute-done((f32[2,40,128]{2,1,0:T(8,128)S(1)}, f32[2,40,128]{2,1,0:T(8,128)S(1)}, u32[]{:S(2)}, u32[]{:S(2)}) %collective-permute-start.18) | collective-permute-done | bytes 40992 | tf_op jit(solution)/shard_map/ppermute | solution.py:44
  77.1 0.4 all-to-all-done.1.refs_12_
  77.5 0.7 collective-permute-start.22
  78.2 0.7 collective-permute-start.23
  79.0 1.3 %collective-permute-start.21 = (f32[2,40,128]{2,1,0:T(8,128)S(1)}, f32[2,40,128]{2,1,0:T(8,128)S(1)}, u32[]{:S(2)}, u32[]{:S(2)}) collective-permute-start(f32[2,40,128]{2,1,0:T(8,128)S(1)} %collective-permute-done.18.refs_2_), channel_id=1, source_target_pairs={{0,8},{8,0},{16,24},{24,16},{32,40},{40,32},{48,56},{56,48},{64,72... | collective-permute-start | bytes 122888 | tf_op jit(solution)/shard_map/ppermute | solution.py:48
  80.3 1.4 %collective-permute-start.24 = (f32[2,40,128]{2,1,0:T(8,128)S(1)}, f32[2,40,128]{2,1,0:T(8,128)S(1)}, u32[]{:S(2)}, u32[]{:S(2)}) collective-permute-start(f32[2,40,128]{2,1,0:T(8,128)S(1)} %collective-permute-done.18.refs_2_), channel_id=1, source_target_pairs={{0,16},{8,24},{16,0},{24,8},{32,48},{40,56},{48,32},{56,40},{64,80... | collective-permute-start | bytes 122888 | tf_op jit(solution)/shard_map/ppermute | solution.py:48
  81.7 0.3 collective-permute-start.19
  82.0 0.2 collective-permute-start.20
  82.2 1.5 %collective-permute-done.24.refs_8_ = f32[2,40,128]{2,1,0:T(8,128)S(1)} collective-permute-done((f32[2,40,128]{2,1,0:T(8,128)S(1)}, f32[2,40,128]{2,1,0:T(8,128)S(1)}, u32[]{:S(2)}, u32[]{:S(2)}) %collective-permute-start.24) | collective-permute-done | bytes 40992 | tf_op jit(solution)/shard_map/ppermute | solution.py:48
  83.7 1.2 %collective-permute-start.27 = (f32[2,40,128]{2,1,0:T(8,128)S(1)}, f32[2,40,128]{2,1,0:T(8,128)S(1)}, u32[]{:S(2)}, u32[]{:S(2)}) collective-permute-start(f32[2,40,128]{2,1,0:T(8,128)S(1)} %collective-permute-done.24.refs_8_), channel_id=1, source_target_pairs={{0,8},{8,0},{16,24},{24,16},{32,40},{40,32},{48,56},{56,48},{64,72... | collective-permute-start | bytes 122888 | tf_op jit(solution)/shard_map/ppermute | solution.py:48
  84.9 0.0 collective-permute-start.25
  84.9 0.5 collective-permute-start.26
  85.4 0.1 dynamic-slice_bitcast_fusion
  85.5 0.1 dynamic_slice.7.rows_live_ref
  85.6 0.3 copy.25
  85.9 0.2 copy.26.refs_13_
  86.1 0.1 copy.27.refs_15_
  86.2 0.1 collective-permute-done.26.refs_10_
  86.3 5.5 %shard_map.179 = f32[16,64,128]{2,1,0:T(8,128)} custom-call(s32[64]{0:T(128)S(1)} %copy-done.5, f32[16]{0:T(128)S(1)} %dynamic_slice.7.rows_live_ref, f32[3,40,128]{2,1,0:T(8,128)S(1)} %pad_maximum_fusion.1.refs_0_, f32[3,40,128]{2,1,0:T(8,128)S(1)} %collective-permute-done.17.refs_1_, f32[2,40,128]{2,1,0:T(8,128)S(1)} %collective-permute-done.18.refs_2_, ...), custom_call_target="tpu_custom_call" | custom-call | flops 1610612736 | bytes 4194304 | tf_op jit(solution)/shard_map/pallas_call | solution.py:435
  (61 shorter events, 0.2 us)
Async XLA Ops:
  0.6 18.8 %copy-start.17 = (s32[512]{0:T(512)S(1)}, s32[512]{0:T(512)}, u32[]{:S(2)}) copy-start(s32[512]{0:T(512)} %param.22) | copy-start | bytes 6148
  0.6 25.1 %copy-start.18 = (s32[2]{0:T(128)S(1)}, s32[2]{0:T(128)}, u32[]{:S(2)}) copy-start(s32[2]{0:T(128)} %param.21) | copy-start | bytes 28
  0.7 41.1 %copy-start.13 = (f32[256]{0:T(256)S(1)}, f32[256]{0:T(256)}, u32[]{:S(2)}) copy-start(f32[256]{0:T(256)} %param.23) | copy-start | bytes 3076
  0.7 0.9 %copy-start.1 = (f32[2,64,256]{2,1,0:T(8,128)S(1)}, f32[2,64,256]{2,1,0:T(8,128)}, u32[]{:S(2)}) copy-start(f32[2,64,256]{2,1,0:T(8,128)} %refs_17_.1) | copy-start | bytes 393220
  1.6 1.0 %copy-start.6 = (f32[16,64,128]{2,1,0:T(8,128)S(1)}, f32[16,64,128]{2,1,0:T(8,128)}, u32[]{:S(2)}) copy-start(f32[16,64,128]{2,1,0:T(8,128)} %refs_14_.1) | copy-start | bytes 1572868
  2.6 0.7 copy-start.12
  3.3 0.7 copy-start.14
  4.0 29.1 %copy-start.16 = (f32[256,32]{0,1:T(8,128)S(1)}, f32[256,32]{0,1:T(8,128)}, u32[]{:S(2)}) copy-start(f32[256,32]{0,1:T(8,128)} %param.32) | copy-start | bytes 98308
  4.0 37.8 %copy-start.2 = (f32[2,64,256]{2,1,0:T(8,128)S(1)}, f32[2,64,256]{2,1,0:T(8,128)}, u32[]{:S(2)}) copy-start(f32[2,64,256]{2,1,0:T(8,128)} %refs_17_.1) | copy-start | bytes 393220
  4.0 37.8 %copy-start.8 = (f32[256,256]{1,0:T(8,128)S(1)}, f32[256,256]{1,0:T(8,128)}, u32[]{:S(2)}) copy-start(f32[256,256]{1,0:T(8,128)} %wq_ref.1) | copy-start | bytes 786436
  4.0 37.8 %copy-start.9 = (f32[256,256]{1,0:T(8,128)S(1)}, f32[256,256]{1,0:T(8,128)}, u32[]{:S(2)}) copy-start(f32[256,256]{1,0:T(8,128)} %wk_ref.1) | copy-start | bytes 786436
  4.0 37.8 %copy-start.10 = (f32[256,256]{1,0:T(8,128)S(1)}, f32[256,256]{1,0:T(8,128)}, u32[]{:S(2)}) copy-start(f32[256,256]{1,0:T(8,128)} %wv_ref.1) | copy-start | bytes 786436
  4.0 37.8 %copy-start.11 = (f32[256,256]{1,0:T(8,128)S(1)}, f32[256,256]{1,0:T(8,128)}, u32[]{:S(2)}) copy-start(f32[256,256]{1,0:T(8,128)} %wg_ref.1) | copy-start | bytes 786436
  5.1 12.6 %collective-permute-start = (f32[1,64,128]{2,1,0:T(8,128)S(1)}, f32[1,64,128]{2,1,0:T(8,128)S(1)}, u32[]{:S(2)}, u32[]{:S(2)}) collective-permute-start(f32[1,64,128]{2,1,0:T(8,128)S(1)} %get-tuple-element.27), channel_id=1, source_target_pairs={{0,128},{1,64},{2,96},{3,32},{4,192},{5,0},{6,160},{7,224},{8,136}... | collective-permute-start | bytes 98312 | tf_op jit(solution)/shard_map/ppermute | solution.py:365
  12.9 28.9 %all-to-all-start = ((f32[8,2,64,256]{3,2,1,0:T(8,128)}), f32[8,2,64,256]{3,2,1,0:T(8,128)S(1)}, u32[]{:S(2)}, u32[]{:S(2)}) async-start(f32[8,2,64,256]{3,2,1,0:T(8,128)} %get-tuple-element.28), calls=%async_computation | async-start | bytes 2097152 | tf_op jit(solution)/shard_map/all_to_all | solution.py:364
  17.6 4.3 %collective-permute-start.1 = (f32[1,64,128]{2,1,0:T(8,128)S(1)}, f32[1,64,128]{2,1,0:T(8,128)S(1)}, u32[]{:S(2)}, u32[]{:S(2)}) collective-permute-start(f32[1,64,128]{2,1,0:T(8,128)S(1)} %collective-permute-done), channel_id=1, source_target_pairs={{0,32},{8,40},{16,48},{24,56},{32,64},{40,72},{48,80},{56,88},{64,... | collective-permute-start | bytes 98312 | tf_op jit(solution)/shard_map/ppermute | solution.py:44
  19.4 3.1 %collective-permute-start.2 = (f32[1,64,128]{2,1,0:T(8,128)S(1)}, f32[1,64,128]{2,1,0:T(8,128)S(1)}, u32[]{:S(2)}, u32[]{:S(2)}) collective-permute-start(f32[1,64,128]{2,1,0:T(8,128)S(1)} %collective-permute-done), channel_id=1, source_target_pairs={{0,224},{8,232},{16,240},{24,248},{32,0},{40,8},{48,16},{56,24},{6... | collective-permute-start | bytes 98312 | tf_op jit(solution)/shard_map/ppermute | solution.py:44
  22.5 9.5 %collective-permute-start.3 = (f32[3,64,128]{2,1,0:T(8,128)S(1)}, f32[3,64,128]{2,1,0:T(8,128)S(1)}, u32[]{:S(2)}, u32[]{:S(2)}) collective-permute-start(f32[3,64,128]{2,1,0:T(8,128)S(1)} %constant_dynamic-update-slice_fusion.refs_0_), channel_id=1, source_target_pairs={{0,160},{8,168},{16,176},{24,184},{32,192},{40,200},{48,208},{56,2... | collective-permute-start | bytes 294920 | tf_op jit(solution)/shard_map/ppermute | solution.py:44
  24.4 7.1 %collective-permute-start.4 = (f32[2,64,128]{2,1,0:T(8,128)S(1)}, f32[2,64,128]{2,1,0:T(8,128)S(1)}, u32[]{:S(2)}, u32[]{:S(2)}) collective-permute-start(f32[2,64,128]{2,1,0:T(8,128)S(1)} %pad_maximum_fusion), channel_id=1, source_target_pairs={{0,96},{8,104},{16,112},{24,120},{32,128},{40,136},{48,144},{56,15... | collective-permute-start | bytes 196616 | tf_op jit(solution)/shard_map/ppermute | solution.py:44
  25.8 12.3 %collective-permute-start.5 = (f32[3,64,128]{2,1,0:T(8,128)S(1)}, f32[3,64,128]{2,1,0:T(8,128)S(1)}, u32[]{:S(2)}, u32[]{:S(2)}) collective-permute-start(f32[3,64,128]{2,1,0:T(8,128)S(1)} %constant_dynamic-update-slice_fusion.refs_0_), channel_id=1, source_target_pairs={{0,8},{8,0},{16,24},{24,16},{32,40},{40,32},{48,56},{56,48},{64,72... | collective-permute-start | bytes 294920 | tf_op jit(solution)/shard_map/ppermute | solution.py:48
  28.8 9.4 %collective-permute-start.8 = (f32[3,64,128]{2,1,0:T(8,128)S(1)}, f32[3,64,128]{2,1,0:T(8,128)S(1)}, u32[]{:S(2)}, u32[]{:S(2)}) collective-permute-start(f32[3,64,128]{2,1,0:T(8,128)S(1)} %constant_dynamic-update-slice_fusion.refs_0_), channel_id=1, source_target_pairs={{0,16},{8,24},{16,0},{24,8},{32,48},{40,56},{48,32},{56,40},{64,80... | collective-permute-start | bytes 294920 | tf_op jit(solution)/shard_map/ppermute | solution.py:48
  31.5 7.2 %collective-permute-start.10 = (f32[2,64,128]{2,1,0:T(8,128)S(1)}, f32[2,64,128]{2,1,0:T(8,128)S(1)}, u32[]{:S(2)}, u32[]{:S(2)}) collective-permute-start(f32[2,64,128]{2,1,0:T(8,128)S(1)} %collective-permute-done.4.refs_2_), channel_id=1, source_target_pairs={{0,16},{8,24},{16,0},{24,8},{32,48},{40,56},{48,32},{56,40},{64,80... | collective-permute-start | bytes 196616 | tf_op jit(solution)/shard_map/ppermute | solution.py:48
  32.0 7.9 %collective-permute-start.9 = (f32[3,64,128]{2,1,0:T(8,128)S(1)}, f32[3,64,128]{2,1,0:T(8,128)S(1)}, u32[]{:S(2)}, u32[]{:S(2)}) collective-permute-start(f32[3,64,128]{2,1,0:T(8,128)S(1)} %collective-permute-done.3.refs_1_), channel_id=1, source_target_pairs={{0,16},{8,24},{16,0},{24,8},{32,48},{40,56},{48,32},{56,40},{64,80... | collective-permute-start | bytes 294920 | tf_op jit(solution)/shard_map/ppermute | solution.py:48
  33.3 12.7 %collective-permute-start.7 = (f32[2,64,128]{2,1,0:T(8,128)S(1)}, f32[2,64,128]{2,1,0:T(8,128)S(1)}, u32[]{:S(2)}, u32[]{:S(2)}) collective-permute-start(f32[2,64,128]{2,1,0:T(8,128)S(1)} %collective-permute-done.4.refs_2_), channel_id=1, source_target_pairs={{0,8},{8,0},{16,24},{24,16},{32,40},{40,32},{48,56},{56,48},{64,72... | collective-permute-start | bytes 196616 | tf_op jit(solution)/shard_map/ppermute | solution.py:48
  38.1 7.9 %collective-permute-start.6 = (f32[3,64,128]{2,1,0:T(8,128)S(1)}, f32[3,64,128]{2,1,0:T(8,128)S(1)}, u32[]{:S(2)}, u32[]{:S(2)}) collective-permute-start(f32[3,64,128]{2,1,0:T(8,128)S(1)} %collective-permute-done.3.refs_1_), channel_id=1, source_target_pairs={{0,8},{8,0},{16,24},{24,16},{32,40},{40,32},{48,56},{56,48},{64,72... | collective-permute-start | bytes 294920 | tf_op jit(solution)/shard_map/ppermute | solution.py:48
  38.2 7.8 %collective-permute-start.11 = (f32[3,64,128]{2,1,0:T(8,128)S(1)}, f32[3,64,128]{2,1,0:T(8,128)S(1)}, u32[]{:S(2)}, u32[]{:S(2)}) collective-permute-start(f32[3,64,128]{2,1,0:T(8,128)S(1)} %collective-permute-done.8.refs_6_), channel_id=1, source_target_pairs={{0,8},{8,0},{16,24},{24,16},{32,40},{40,32},{48,56},{56,48},{64,72... | collective-permute-start | bytes 294920 | tf_op jit(solution)/shard_map/ppermute | solution.py:48
  38.6 7.4 %collective-permute-start.13 = (f32[2,64,128]{2,1,0:T(8,128)S(1)}, f32[2,64,128]{2,1,0:T(8,128)S(1)}, u32[]{:S(2)}, u32[]{:S(2)}) collective-permute-start(f32[2,64,128]{2,1,0:T(8,128)S(1)} %collective-permute-done.10.refs_8_), channel_id=1, source_target_pairs={{0,8},{8,0},{16,24},{24,16},{32,40},{40,32},{48,56},{56,48},{64,72... | collective-permute-start | bytes 196616 | tf_op jit(solution)/shard_map/ppermute | solution.py:48
  39.9 6.1 %collective-permute-start.12 = (f32[3,64,128]{2,1,0:T(8,128)S(1)}, f32[3,64,128]{2,1,0:T(8,128)S(1)}, u32[]{:S(2)}, u32[]{:S(2)}) collective-permute-start(f32[3,64,128]{2,1,0:T(8,128)S(1)} %collective-permute-done.9.refs_7_), channel_id=1, source_target_pairs={{0,8},{8,0},{16,24},{24,16},{32,40},{40,32},{48,56},{56,48},{64,72... | collective-permute-start | bytes 294920 | tf_op jit(solution)/shard_map/ppermute | solution.py:48
  41.8 4.4 %copy-start = (f32[256,256]{1,0:T(8,128)S(1)}, f32[256,256]{1,0:T(8,128)}, u32[]{:S(2)}) copy-start(f32[256,256]{1,0:T(8,128)} %refs_18_.1) | copy-start | bytes 786436
  41.8 4.4 %copy-start.3 = (f32[256,32]{0,1:T(8,128)S(1)}, f32[256,32]{0,1:T(8,128)}, u32[]{:S(2)}) copy-start(f32[256,32]{0,1:T(8,128)} %param.33) | copy-start | bytes 98308
  41.9 4.4 %copy-start.4 = (f32[256]{0:T(256)S(1)}, f32[256]{0:T(256)}, u32[]{:S(2)}) copy-start(f32[256]{0:T(256)} %param.31) | copy-start | bytes 3076
  41.9 4.4 %copy-start.5 = (s32[64]{0:T(128)S(1)}, s32[64]{0:T(128)}, u32[]{:S(2)}) copy-start(s32[64]{0:T(128)} %constant.51.clone.far_ref) | copy-start | bytes 772
  46.2 39.4 %copy-start.15 = (f32[1024,128]{1,0:T(8,128)S(1)}, f32[1024,128]{1,0:T(8,128)}, u32[]{:S(2)}) copy-start(f32[1024,128]{1,0:T(8,128)} %param.34) | copy-start | bytes 1572868
  50.5 35.9 %copy-start.7 = (f32[16,64,128]{2,1,0:T(8,128)S(1)}, f32[16,64,128]{2,1,0:T(8,128)}, u32[]{:S(2)}) copy-start(f32[16,64,128]{2,1,0:T(8,128)} %refs_14_.1) | copy-start | bytes 1572868
  50.5 19.4 %collective-permute-start.15 = (f32[1,40,128]{2,1,0:T(8,128)S(1)}, f32[1,40,128]{2,1,0:T(8,128)S(1)}, u32[]{:S(2)}, u32[]{:S(2)}) collective-permute-start(f32[1,40,128]{2,1,0:T(8,128)S(1)} %get-tuple-element.34), channel_id=1, source_target_pairs={{0,224},{8,232},{16,240},{24,248},{32,0},{40,8},{48,16},{56,24},{6... | collective-permute-start | bytes 61448 | tf_op jit(solution)/shard_map/ppermute | solution.py:44
  50.5 19.4 %collective-permute-start.14 = (f32[1,40,128]{2,1,0:T(8,128)S(1)}, f32[1,40,128]{2,1,0:T(8,128)S(1)}, u32[]{:S(2)}, u32[]{:S(2)}) collective-permute-start(f32[1,40,128]{2,1,0:T(8,128)S(1)} %get-tuple-element.34), channel_id=1, source_target_pairs={{0,32},{8,40},{16,48},{24,56},{32,64},{40,72},{48,80},{56,88},{64,... | collective-permute-start | bytes 61448 | tf_op jit(solution)/shard_map/ppermute | solution.py:44
  51.9 6.9 %collective-permute-start.16 = (f32[4,8,128]{2,1,0:T(8,128)S(1)}, f32[4,8,128]{2,1,0:T(8,128)S(1)}, u32[]{:S(2)}, u32[]{:S(2)}) collective-permute-start(f32[4,8,128]{2,1,0:T(8,128)S(1)} %get-tuple-element.35), channel_id=1, source_target_pairs={{128,0},{64,1},{96,2},{32,3},{192,4},{0,5},{160,6},{224,7},{136,8}... | collective-permute-start | bytes 49160 | tf_op jit(solution)/shard_map/ppermute | solution.py:424
  59.5 18.0 %all-to-all-start.1 = ((f32[32,8,128]{2,1,0:T(8,128)}), f32[32,8,128]{2,1,0:T(8,128)S(1)}, u32[]{:S(2)}, u32[]{:S(2)}) async-start(f32[32,8,128]{2,1,0:T(8,128)} %bitcast.7), calls=%async_computation.1 | async-start | bytes 262144 | tf_op jit(solution)/shard_map/all_to_all | solution.py:426
  69.9 7.3 %collective-permute-start.17 = (f32[3,40,128]{2,1,0:T(8,128)S(1)}, f32[3,40,128]{2,1,0:T(8,128)S(1)}, u32[]{:S(2)}, u32[]{:S(2)}) collective-permute-start(f32[3,40,128]{2,1,0:T(8,128)S(1)} %pad_maximum_fusion.1.refs_0_), channel_id=1, source_target_pairs={{0,160},{8,168},{16,176},{24,184},{32,192},{40,200},{48,208},{56,2... | collective-permute-start | bytes 184328 | tf_op jit(solution)/shard_map/ppermute | solution.py:44
  70.5 6.6 %collective-permute-start.18 = (f32[2,40,128]{2,1,0:T(8,128)S(1)}, f32[2,40,128]{2,1,0:T(8,128)S(1)}, u32[]{:S(2)}, u32[]{:S(2)}) collective-permute-start(f32[2,40,128]{2,1,0:T(8,128)S(1)} %slice.21), channel_id=1, source_target_pairs={{0,96},{8,104},{16,112},{24,120},{32,128},{40,136},{48,144},{56,15... | collective-permute-start | bytes 122888 | tf_op jit(solution)/shard_map/ppermute | solution.py:44
  77.5 7.4 %collective-permute-start.22 = (f32[3,40,128]{2,1,0:T(8,128)S(1)}, f32[3,40,128]{2,1,0:T(8,128)S(1)}, u32[]{:S(2)}, u32[]{:S(2)}) collective-permute-start(f32[3,40,128]{2,1,0:T(8,128)S(1)} %pad_maximum_fusion.1.refs_0_), channel_id=1, source_target_pairs={{0,16},{8,24},{16,0},{24,8},{32,48},{40,56},{48,32},{56,40},{64,80... | collective-permute-start | bytes 184328 | tf_op jit(solution)/shard_map/ppermute | solution.py:48
  78.2 6.7 %collective-permute-start.23 = (f32[3,40,128]{2,1,0:T(8,128)S(1)}, f32[3,40,128]{2,1,0:T(8,128)S(1)}, u32[]{:S(2)}, u32[]{:S(2)}) collective-permute-start(f32[3,40,128]{2,1,0:T(8,128)S(1)} %collective-permute-done.17.refs_1_), channel_id=1, source_target_pairs={{0,16},{8,24},{16,0},{24,8},{32,48},{40,56},{48,32},{56,40},{64,80... | collective-permute-start | bytes 184328 | tf_op jit(solution)/shard_map/ppermute | solution.py:48
  79.0 3.0 %collective-permute-start.21 = (f32[2,40,128]{2,1,0:T(8,128)S(1)}, f32[2,40,128]{2,1,0:T(8,128)S(1)}, u32[]{:S(2)}, u32[]{:S(2)}) collective-permute-start(f32[2,40,128]{2,1,0:T(8,128)S(1)} %collective-permute-done.18.refs_2_), channel_id=1, source_target_pairs={{0,8},{8,0},{16,24},{24,16},{32,40},{40,32},{48,56},{56,48},{64,72... | collective-permute-start | bytes 122888 | tf_op jit(solution)/shard_map/ppermute | solution.py:48
  80.3 3.4 %collective-permute-start.24 = (f32[2,40,128]{2,1,0:T(8,128)S(1)}, f32[2,40,128]{2,1,0:T(8,128)S(1)}, u32[]{:S(2)}, u32[]{:S(2)}) collective-permute-start(f32[2,40,128]{2,1,0:T(8,128)S(1)} %collective-permute-done.18.refs_2_), channel_id=1, source_target_pairs={{0,16},{8,24},{16,0},{24,8},{32,48},{40,56},{48,32},{56,40},{64,80... | collective-permute-start | bytes 122888 | tf_op jit(solution)/shard_map/ppermute | solution.py:48
  81.7 4.5 %collective-permute-start.19 = (f32[3,40,128]{2,1,0:T(8,128)S(1)}, f32[3,40,128]{2,1,0:T(8,128)S(1)}, u32[]{:S(2)}, u32[]{:S(2)}) collective-permute-start(f32[3,40,128]{2,1,0:T(8,128)S(1)} %pad_maximum_fusion.1.refs_0_), channel_id=1, source_target_pairs={{0,8},{8,0},{16,24},{24,16},{32,40},{40,32},{48,56},{56,48},{64,72... | collective-permute-start | bytes 184328 | tf_op jit(solution)/shard_map/ppermute | solution.py:48
  82.0 4.2 %collective-permute-start.20 = (f32[3,40,128]{2,1,0:T(8,128)S(1)}, f32[3,40,128]{2,1,0:T(8,128)S(1)}, u32[]{:S(2)}, u32[]{:S(2)}) collective-permute-start(f32[3,40,128]{2,1,0:T(8,128)S(1)} %collective-permute-done.17.refs_1_), channel_id=1, source_target_pairs={{0,8},{8,0},{16,24},{24,16},{32,40},{40,32},{48,56},{56,48},{64,72... | collective-permute-start | bytes 184328 | tf_op jit(solution)/shard_map/ppermute | solution.py:48
  83.7 2.5 %collective-permute-start.27 = (f32[2,40,128]{2,1,0:T(8,128)S(1)}, f32[2,40,128]{2,1,0:T(8,128)S(1)}, u32[]{:S(2)}, u32[]{:S(2)}) collective-permute-start(f32[2,40,128]{2,1,0:T(8,128)S(1)} %collective-permute-done.24.refs_8_), channel_id=1, source_target_pairs={{0,8},{8,0},{16,24},{24,16},{32,40},{40,32},{48,56},{56,48},{64,72... | collective-permute-start | bytes 122888 | tf_op jit(solution)/shard_map/ppermute | solution.py:48
  84.9 1.3 %collective-permute-start.25 = (f32[3,40,128]{2,1,0:T(8,128)S(1)}, f32[3,40,128]{2,1,0:T(8,128)S(1)}, u32[]{:S(2)}, u32[]{:S(2)}) collective-permute-start(f32[3,40,128]{2,1,0:T(8,128)S(1)} %collective-permute-done.22.refs_6_), channel_id=1, source_target_pairs={{0,8},{8,0},{16,24},{24,16},{32,40},{40,32},{48,56},{56,48},{64,72... | collective-permute-start | bytes 184328 | tf_op jit(solution)/shard_map/ppermute | solution.py:48
  84.9 1.4 %collective-permute-start.26 = (f32[3,40,128]{2,1,0:T(8,128)S(1)}, f32[3,40,128]{2,1,0:T(8,128)S(1)}, u32[]{:S(2)}, u32[]{:S(2)}) collective-permute-start(f32[3,40,128]{2,1,0:T(8,128)S(1)} %collective-permute-done.23.refs_7_), channel_id=1, source_target_pairs={{0,8},{8,0},{16,24},{24,16},{32,40},{40,32},{48,56},{56,48},{64,72... | collective-permute-start | bytes 184328 | tf_op jit(solution)/shard_map/ppermute | solution.py:48

commit v2 on v1

v2 whole, which is shorter than its diff:
```python
import itertools
import math

import jax
import jax.numpy as jnp
import numpy as np
from jax import lax
from jax.experimental import pallas as pl
from jax.experimental.pallas import tpu as pltpu
from jax.sharding import PartitionSpec as P

exact = lax.Precision.HIGHEST
f32 = jnp.float32
bf16 = jnp.bfloat16
MIB = 1024 * 1024

Z, A, H = 8, 4, 8
def ring(d, n):
    return min(d % n, -d % n)


def spread_tables():
    once = np.zeros((H, H), np.int32)
    twice = np.zeros((H, 2, H), np.int32)
    for c in range(H):
        hops = [
            [ring(h // 2 - c // 2, 4) + 2 * ((h ^ c) & 1) + ring(b - c, Z) for b in range(Z)]
            for h in range(H)
        ]
        flat = [hops[h][c] for h in range(H)]
        columns = sorted(range(H), key=lambda h: (-flat[h], h))
        planes = sorted(range(Z), key=lambda b: (ring(b - c, Z), (b - c) % Z))
        for h, b in zip(columns, planes):
            once[c][h] = b

        def fit(group, half):
            return min(
                (
                    (max(hops[h][b] for h, b in zip(group, p)), sum(hops[h][b] for h, b in zip(group, p)), p)
                    for p in itertools.permutations(range(4 * half, 4 * half + 4))
                )
            )

        best = None
        for low in itertools.combinations(range(H), 4):
            high = tuple(h for h in range(H) if h not in low)
            first = fit(low, 0), fit(high, 1)
            second = fit(low, 1), fit(high, 0)
            cost = (
                max(first[0][0], first[1][0]) + max(second[0][0], second[1][0]),
                sum(f[1] for f in first + second),
            )
            if best is None or cost < best[0]:
                best = cost, low, high, first, second
        _, low, high, first, second = best
        for k, fits in enumerate((first, second)):
            for group, found in zip((low, high), fits):
                for h, b in zip(group, found[2]):
                    twice[c][k][h] = b
    return once, twice


ONCE, TWICE = spread_tables()


def moves(table):
    return [
        ((4 * b + a) * H + h, (4 * int(table[b][h]) + a) * H + b)
        for b in range(Z)
        for a in range(A)
        for h in range(H)
    ]


def spots():
    out = np.zeros((H, 2, H), np.int32)
    for c in range(H):
        for k in range(2):
            for h in range(H):
                plane = int(TWICE[c][k][h])
                out[c][plane // 4][h] = 4 * k + plane % 4
    return out


SPOTS = spots()


def from_neighbour(v, bit):
    return lax.ppermute(v, "row", [(r, r ^ bit) for r in range(Z * A)])


def after(values, *others):
    return list(lax.optimization_barrier((*values, *others)))[: len(values)]


def gather_halves(first, second):
    own = jnp.concatenate([first, second], axis=0)
    near = jnp.concatenate([own, from_neighbour(own, 8)], axis=0)
    return [near, from_neighbour(near, 4)]


def gather_sides(pieces):
    return [from_neighbour(p, 2) for p in pieces]


def gather_cores(pieces, sides):
    return (
        pieces
        + [from_neighbour(p, 1) for p in pieces]
        + sides
        + [from_neighbour(p, 1) for p in sides]
    )


def side_of(row, source_side):
    return jnp.bitwise_xor(jnp.bitwise_and(row, 3), source_side) * 8


def half_position(row, spot, source_side):
    plane = jnp.bitwise_xor(jnp.bitwise_and(jnp.right_shift(row, 2), 3), jnp.bitwise_and(spot, 3))
    return (
        side_of(row, source_side)
        + jnp.bitwise_and(plane, 1) * 4
        + jnp.bitwise_and(plane, 2)
        + jnp.right_shift(spot, 2)
    )


def split(v):
    high = v.astype(bf16)
    return high, (v - high.astype(f32)).astype(bf16)


def dot(a, b, dims=((1,), (0,))):
    return lax.dot_general(a, b, (dims, ((), ())), preferred_element_type=f32)


def dot_exact(a, b, dims=((1,), (0,))):
    return lax.dot_general(a, b, (dims, ((), ())), precision=exact, preferred_element_type=f32)


def three(a, b, dims=((1,), (0,))):
    return dot(a[0], b[0], dims) + (dot(a[0], b[1], dims) + dot(a[1], b[0], dims))


def dot_three(a, b, dims=((1,), (0,))):
    return three(split(a), split(b), dims)


def norm_rows(v, gain):
    center = v - jnp.mean(v, axis=-1, keepdims=True)
    spread = jnp.mean(center * center, axis=-1, keepdims=True)
    return center * lax.rsqrt(spread + 1e-05) * gain


def start_all(copies):
    for copy in copies:
        copy.start()
    return copies


def wait_all(copies):
    for copy in copies:
        copy.wait()


def bias_kernel(
    pair_hbm,
    gain_hbm,
    weight_hbm,
    own_hbm,
    out_ref,
    copies_hbm,
    pair_ref,
    gain_ref,
    weight_ref,
    own_ref,
    sems,
):
    own_load = start_all([pltpu.make_async_copy(own_hbm, own_ref, sems.at[11])])
    loads = start_all(
        [
            pltpu.make_async_copy(gain_hbm, gain_ref, sems.at[8]),
            pltpu.make_async_copy(weight_hbm, weight_ref, sems.at[9]),
            pltpu.make_async_copy(pair_hbm, pair_ref, sems.at[10]),
        ]
    )
    wait_all(own_load)
    copies = start_all(
        [pltpu.make_async_copy(own_ref, copies_hbm.at[k], sems.at[k]) for k in range(H)]
    )
    wait_all(loads)
    rows = pair_ref[...].reshape(1024, 128)
    normed = norm_rows(rows, gain_ref[...])
    pick = lax.broadcasted_iota(jnp.int32, (8, 128), 0) == (
        lax.broadcasted_iota(jnp.int32, (8, 128), 1) // 16
    )
    wide = dot_exact(weight_ref[...], jnp.where(pick, 1.0, 0.0), ((0,), (0,)))
    result = dot_exact(normed, wide)
    lane = lax.broadcasted_iota(jnp.int32, (64, 128), 1) % 16
    total = jnp.zeros((64, 128), f32)
    for i in range(16):
        total = jnp.where(lane == i, result[64 * i : 64 * i + 64], total)
    out_ref[0] = total
    wait_all(copies)


def spread_kernel(left_ref, out_ref, sems):
    wait_all(
        start_all(
            [pltpu.make_async_copy(left_ref, out_ref.at[:, k], sems.at[k]) for k in range(H)]
        )
    )


def logits_kernel(
    all_ref, own_ref, gain_ref, wq_ref, wk_ref, wv_ref, wg_ref, logit_ref, value_ref, gate_ref
):
    gain = gain_ref[...]
    own = split(norm_rows(own_ref[...].reshape(128, 256), gain))
    query = three(own, split(wq_ref[...])) * (1.0 / math.sqrt(32))
    gate_ref[...] = jax.nn.sigmoid(three(own, split(wg_ref[...])))
    head_of_lane = lax.broadcasted_iota(jnp.int32, (128, 256), 1) // 32
    head_of_row = lax.broadcasted_iota(jnp.int32, (128, 256), 0) // 16
    keep = head_of_lane == head_of_row
    key_factor = split(wk_ref[...])
    value_factor = split(jnp.transpose(wv_ref[...]))
    for s in range(2):
        rows = split(
            norm_rows(jnp.concatenate([all_ref[b, s] for b in range(8)], axis=0), gain)
        )
        keys = split(three(rows, key_factor))
        value_ref[0, s], value_ref[1, s] = split(three(value_factor, rows, ((1,), (1,))))
        wide = []
        for a in range(4):
            part = query[64 * s + 16 * a : 64 * s + 16 * a + 16]
            wide.append(jnp.where(keep, jnp.concatenate([part] * 8, axis=0), 0.0))
        logit_ref[s] = three(keys, split(jnp.concatenate(wide, axis=0)), ((1,), (1,)))


def attend_kernel(
    spot_ref,
    *refs,
):
    attend(spot_ref, refs[:8], *refs[8:])


def attend(
    spot_ref,
    piece_refs,
    logit_ref,
    key_ref,
    value_ref,
    gate_ref,
    own_ref,
    wf_ref,
    gain_ref,
    first_ref,
    second_ref,
    live_ref,
    mask_ref,
    msa_ref,
    left_ref,
    right_ref,
    bias_ref,
    y_ref,
):
    for k, piece_ref in enumerate(piece_refs):
        bias_ref[4 * k : 4 * k + 4] = piece_ref[...]
    row = lax.axis_index("row")
    spots_at = (lax.axis_index("head") * 2 + jnp.right_shift(row, 4)) * H
    lane = lax.broadcasted_iota(jnp.int32, (32, 128), 1) // 16
    folded = [jnp.zeros((32, 128), f32) for _ in range(8)]
    for s in range(2):
        for a in range(4):
            columns = pl.ds(128 * a, 128)
            tiles = []
            for b in range(8):
                rows = pl.ds(64 * b, 64)
                tiles.append(
                    (logit_ref[s, rows, columns] + bias_ref[half_position(row, spot_ref[spots_at + b], a)])
                    + key_ref[rows, :]
                )
            logits = jnp.concatenate(tiles, axis=0)
            exponent = jnp.exp(logits - jnp.max(logits, axis=0, keepdims=True))
            weights = exponent * (1.0 / jnp.sum(exponent, axis=0, keepdims=True))
            part = three((value_ref[0, s], value_ref[1, s]), split(weights))
            for h in range(8):
                moved = pltpu.roll(
                    part[32 * h : 32 * h + 32], (64 * s + 16 * a - 16 * h) % 128, 1
                )
                folded[h] = jnp.where(lane == 4 * s + a, moved, folded[h])
    attended = jnp.transpose(jnp.concatenate(folded, axis=0)) * gate_ref[...]
    updated = own_ref[...].reshape(128, 256) + dot_three(attended, wf_ref[...])
    msa_ref[...] = updated.reshape(2, 64, 256)
    y = norm_rows(updated, gain_ref[...]) * live_ref[...]
    y = split(y)
    right = three(split(second_ref[...]), y, ((1,), (1,)))
    for k in range(Z):
        right_ref[k, 0:32, :] = right
        right_ref[k, 32:40, :] = mask_ref[...]
    y_ref[...] = three(y, split(first_ref[...]))
    lane = lax.broadcasted_iota(jnp.int32, (32, 128), 1) // 32
    left = jnp.zeros((32, 128), f32)
    for k in range(4):
        left = jnp.where(lane == k, y_ref[pl.ds(k, 32, stride=4), :], left)
    for s in range(2):
        for a in range(4):
            left_ref[a, 4 * s : 4 * s + 4, :] = left[16 * s + 4 * a : 16 * s + 4 * a + 4]


def outer_kernel(
    once_ref,
    rows_live_ref,
    *refs,
):
    outer_product(once_ref, rows_live_ref, refs[:4], *refs[4:])


def outer_product(
    once_ref,
    rows_live_ref,
    piece_refs,
    left_in_ref,
    weight_ref,
    pair_ref,
    cols_live_ref,
    out_ref,
    right_in_ref,
    sorted_ref,
    left_ref,
    right_ref,
):
    for q, piece_ref in enumerate(piece_refs):
        for k in range(Z):
            start = 40 * (Z * q + k)
            right_in_ref[start : start + 40, :] = piece_ref[k]
    row = lax.axis_index("row")
    for p in range(32):
        source = side_of(row, p // H) + once_ref[jnp.right_shift(row, 2) * H + p % H]
        spot = pl.multiple_of(source * 8, 8)
        sorted_ref[pl.ds(spot, 8), :] = left_in_ref[p]
    count = jnp.zeros((8, 128), f32)
    for k in range(32):
        count = count + right_in_ref[40 * k + 32 : 40 * k + 40, :]
    count = jnp.sum(count)
    left_rows = []
    for s in range(2):
        left_rows.append(
            jnp.concatenate(
                [sorted_ref[pl.ds(4 * s + q, 32, stride=8), :] for q in range(4)], axis=1
            )
        )
    left = jnp.concatenate(left_rows, axis=0)
    high = left.astype(bf16).astype(f32)
    low = left - high
    left_ref[...] = jnp.transpose(jnp.concatenate([high, high, low, jnp.zeros_like(low)], axis=0)).astype(bf16)
    lane = lax.broadcasted_iota(jnp.int32, (32, 128), 1) < 64
    for d in range(16):
        even = right_in_ref[pl.ds(2 * d, 32, stride=40), :]
        odd = right_in_ref[pl.ds(2 * d + 1, 32, stride=40), :]
        both = jnp.concatenate(
            [
                jnp.where(lane, even, pltpu.roll(odd, 64, 1)),
                jnp.where(lane, pltpu.roll(even, 64, 1), odd),
            ],
            axis=0,
        )
        high, low = split(both)
        columns = pl.ds(128 * d, 128)
        right_ref[0:64, columns] = high
        right_ref[64:128, columns] = low
        right_ref[128:192, columns] = high
        right_ref[192:256, columns] = jnp.zeros((64, 128), bf16)
    columns = [
        jnp.concatenate(
            [weight_ref[pl.ds(2 * d + e, 32, stride=32), :] for d in range(16)], axis=0
        )
        for e in range(2)
    ]
    weight = split(jnp.transpose(jnp.concatenate(columns, axis=1)))
    lane = lax.broadcasted_iota(jnp.int32, (128, 128), 1) < 64
    for q in range(8):
        outer = dot(left_ref[64 * q : 64 * q + 64, :], right_ref[...])
        stacked = jnp.concatenate(
            [
                jnp.concatenate(
                    [outer[32 * e : 32 * e + 32, 128 * d : 128 * d + 128] for d in range(16)],
                    axis=0,
                )
                for e in range(2)
            ],
            axis=1,
        )
        y = three(weight, split(stacked))
        top, bottom = y[0:128], y[128:256]
        total = jnp.where(
            lane,
            top[:, 0:128] + pltpu.roll(bottom[:, 0:128], 64, 1),
            pltpu.roll(top[:, 128:256], 64, 1) + bottom[:, 128:256],
        )
        total = jnp.transpose(total)
        for e in range(2):
            i = 2 * q + e
            norm = count * rows_live_ref[i] * cols_live_ref[...] + 0.001
            out_ref[i] = pair_ref[i] + total[64 * e : 64 * e + 64] / norm


def vmem(count):
    return [pl.BlockSpec(memory_space=pltpu.VMEM)] * count


def smem(count):
    return [pl.BlockSpec(memory_space=pltpu.SMEM)] * count


def hbm(count):
    return [pl.BlockSpec(memory_space=pltpu.HBM)] * count


def struct(*shape, dtype=f32):
    return jax.ShapeDtypeStruct(shape, dtype)


def call(kernel, inputs, outputs, shapes, scratch=(), limit=32, flops=0, touched=0):
    return pl.pallas_call(
        kernel,
        in_specs=inputs,
        out_specs=outputs,
        out_shape=shapes,
        scratch_shapes=list(scratch),
        compiler_params=pltpu.CompilerParams(vmem_limit_bytes=limit * MIB),
        cost_estimate=pl.CostEstimate(flops=flops, bytes_accessed=touched, transcendentals=0),
    )


def body(
    sequence_matrix,
    pair_representation,
    alignment_row_mask,
    residue_mask,
    attention_scale_vector,
    asking_factor_matrix,
    lookup_factor_matrix,
    content_factor_matrix,
    sigmoid_factor_matrix,
    final_factor_matrix,
    pair_norm_gain,
    bias_weight,
    tensor_scale_vector,
    first_factor_matrix,
    second_factor_matrix,
    outer_weight,
):
    head_index = lax.axis_index("head")
    row_index = lax.axis_index("row")
    both = ("row", "head")
    block, copies = call(
        bias_kernel,
        hbm(4),
        vmem(1) + hbm(1),
        [struct(1, 64, 128), struct(H, 2, 64, 256)],
        scratch=[
            pltpu.VMEM((16, 64, 128), f32),
            pltpu.VMEM((1, 128), f32),
            pltpu.VMEM((8, 128), f32),
            pltpu.VMEM((2, 64, 256), f32),
            pltpu.SemaphoreType.DMA((H + 4,)),
        ],
        limit=60,
        flops=2 * 1024 * 128 * 128 * 6,
        touched=600000,
    )(pair_representation, pair_norm_gain[None], bias_weight.T, sequence_matrix)
    everyone = lax.all_to_all(copies, "head", 0, 0, tiled=True)
    pieces = gather_halves(
        lax.ppermute(block, both, moves(TWICE[:, 0])), lax.ppermute(block, both, moves(TWICE[:, 1]))
    )
    bias = gather_cores(pieces, gather_sides(pieces))

    residue_live = residue_mask.astype(f32)
    key_bias = jnp.broadcast_to(((residue_live - 1.0) * 1000000000.0)[:, None], (512, 128))
    cols_live = lax.dynamic_slice_in_dim(residue_live, head_index * 64, 64)
    rows_live = lax.dynamic_slice_in_dim(residue_live, row_index * 16, 16)
    row_live = alignment_row_mask.astype(f32)
    live = (row_live[:, None] * cols_live[None, :]).reshape(128, 1)
    mask_tile = jnp.zeros((8, 128), f32).at[0, 0:2].set(row_live)
    spots = jnp.asarray(SPOTS.reshape(-1))
    once = jnp.asarray(ONCE.reshape(-1))
    logits, values, gate = call(
        logits_kernel,
        vmem(7),
        vmem(3),
        [struct(2, 512, 512), struct(2, 2, 256, 512, dtype=bf16), struct(128, 256)],
        flops=3 * 2 * 1024 * 256 * 1024,
        touched=6 * MIB,
    )(
        everyone,
        sequence_matrix,
        attention_scale_vector[None],
        asking_factor_matrix,
        lookup_factor_matrix,
        content_factor_matrix,
        sigmoid_factor_matrix,
    )
    msa_out, left, right = call(
        attend_kernel,
        smem(1) + vmem(19),
        vmem(3),
        [struct(2, 64, 256), struct(4, 8, 128), struct(Z, 40, 128)],
        scratch=[pltpu.VMEM((32, 64, 128), f32), pltpu.VMEM((128, 128), f32)],
        flops=3 * 2 * 1024 * 512 * 256,
        touched=6 * MIB,
    )(
        spots,
        *bias,
        logits,
        key_bias,
        values,
        gate,
        sequence_matrix,
        final_factor_matrix,
        tensor_scale_vector[None],
        jnp.tile(first_factor_matrix, (1, 4)),
        second_factor_matrix.T,
        live,
        mask_tile,
    )
    planes = lax.all_to_all(
        right,
        "row",
        0,
        0,
        tiled=True,
        axis_index_groups=[[4 * z + a for z in range(Z)] for a in range(A)],
    )
    left = lax.ppermute(left, both, [(d, s) for s, d in moves(ONCE)])
    left, planes = after([left, planes])
    (spread,) = call(
        spread_kernel,
        vmem(1),
        hbm(1),
        [struct(A, H, 8, 128)],
        scratch=[pltpu.SemaphoreType.DMA((H,))],
    )(left)
    left = lax.all_to_all(
        spread.reshape(A * H, 8, 128),
        both,
        0,
        0,
        tiled=True,
        axis_index_groups=[[32 * z + k for k in range(32)] for z in range(Z)],
    )
    right = gather_cores([planes], after(gather_sides([planes]), left))
    (pair_out,) = call(
        outer_kernel,
        smem(2) + vmem(8),
        vmem(1),
        [struct(16, 64, 128)],
        scratch=[
            pltpu.VMEM((1280, 128), f32),
            pltpu.VMEM((256, 128), f32),
            pltpu.VMEM((512, 256), bf16),
            pltpu.VMEM((256, 2048), bf16),
        ],
        flops=3 * 2 * 1024 * 1024 * 256,
        touched=4 * MIB,
    )(
        once,
        rows_live,
        *right,
        left,
        outer_weight,
        pair_representation,
        cols_live[:, None],
    )
    return msa_out, pair_out


def solution(mesh):
    cells = P("row", "head", None)
    return jax.shard_map(
        body,
        mesh=mesh,
        in_specs=(cells, cells, P("row")) + (P(),) * 13,
        out_specs=(cells, cells),
        check_vma=False,
    )
```

time: 92.2 us -> 87.3 us (0.947)
  starting transfers between devices: 60 us -> 54.8 us
  local copies, waits for them, and re-layouts: 5.22 us -> 0.78 us
  waiting for transfers between devices: 10.6 us -> 14.7 us
    ppermute x10 -> x3, starting transfers between devices: 25 us -> 15.3 us  [the longest x1 5.98 us: body(): left = lax.ppermute(left, both, [(d, s) for s, d in moves(ONCE)])]
    all_to_all x1 -> x2, waiting for transfers between devices: 0.39 us -> 7.38 us  [the longest x1 7.38 us: body(): lax.all_to_all(spread.reshape(A * H, 8, 128), both, 0, 0, tiled=True, axi...]
    all_to_all x1 -> x2, starting transfers between devices: 10.3 us -> 16.3 us  [the longest x1 9.32 us: body(): lax.all_to_all(spread.reshape(A * H, 8, 128), both, 0, 0, tiled=True, axi...]
    ppermute x10 -> x3, waiting for transfers between devices: 8.6 us -> 2.59 us  [the longest x1 2.58 us: body(): left = lax.ppermute(left, both, [(d, s) for s, d in moves(ONCE)])]
    unnamed x41 -> x34, local copies, waits for them, and re-layouts: 3.41 us -> 0.09 us
    ppermute x18 -> x11, waiting for transfers between devices: 1.63 us -> 4.71 us  [from_neighbour(): return lax.ppermute(v, 'row', [(r, r ^ bit) for r in range(Z * A)])]
    ppermute x18 -> x11, starting transfers between devices: 19.9 us -> 17.3 us  [from_neighbour(): return lax.ppermute(v, 'row', [(r, r ^ bit) for r in range(Z * A)])]
    all_to_all x1, starting transfers between devices: 4.74 us -> 5.83 us  [body(): everyone = lax.all_to_all(copies, 'head', 0, 0, tiled=True)]
  transfers between devices with their start and end apart: 30 -> 17, of which waited for: 8 -> 5; matrix products, arithmetic and copies ran while one was open for 2% -> 1% of each run, Pallas kernels for 4% -> 3%
where the time goes in v2:
time: 87.3 us; the launch traced here: 86.9 us
  starting transfers between devices  54.8 us (63%)
  Pallas kernels  15.6 us (18%)
  waiting for transfers between devices  14.7 us (17%)
  between operations  0.99 us (1%)
    ppermute x11, starting transfers between devices, from_neighbour(): return lax.ppermute(v, 'row', [(r, r ^ bit) for r in range(Z * A)])  17.3 us
    all_to_all x1, starting transfers between devices, body(): lax.all_to_all(spread.reshape(A * H, 8, 128), both, 0, 0, tiled=True, axi...  9.32 us
    all_to_all x1, waiting for transfers between devices, body(): lax.all_to_all(spread.reshape(A * H, 8, 128), both, 0, 0, tiled=True, axi...  7.38 us
    all_to_all x1, starting transfers between devices, body(): lax.all_to_all(right, 'row', 0, 0, tiled=True, axis_index_groups=[[4 * z...  7.02 us
    ppermute x1, starting transfers between devices, body(): left = lax.ppermute(left, both, [(d, s) for s, d in moves(ONCE)])  5.98 us
    all_to_all x1, starting transfers between devices, body(): everyone = lax.all_to_all(copies, 'head', 0, 0, tiled=True)  5.83 us
    pallas_call x1, Pallas kernels, body(): call(outer_kernel, smem(2) + vmem(8), vmem(1), [struct(16, 64, 128)], scr...  5.45 us
    ppermute x1, starting transfers between devices, body(): lax.ppermute(block, both, moves(TWICE[:, 0]))  5.25 us
  transfers between devices with their start and end apart: 17, of which 5 were waited for; matrix products, arithmetic and copies ran while one was open for 1% of the time, Pallas kernels for 3%

profile of v2, /device:TPU:1, one launch (start us, length us, event | category | flops | bytes accessed | tf_op | source)
XLA Modules:
  0.0 86.9 jit_solution(13079522980635129003)
XLA Ops:
  0.6 0.0 copy-start.1
  0.6 0.0 copy-start.15
  0.7 0.0 copy-start.13
  0.7 0.0 copy-start.14
  0.7 0.0 copy-start.11
  0.7 0.0 copy-start.7
  0.7 0.0 copy-start.8
  0.7 0.0 copy-start.9
  0.7 2.9 %shard_map.185 = (f32[1,64,128]{2,1,0:T(8,128)}, f32[8,2,64,256]{3,2,1,0:T(8,128)}) custom-call(f32[16,64,128]{2,1,0:T(8,128)} %refs_6_.1, f32[1,128]{1,0:T(1,128)} %bitcast.16, f32[8,128]{1,0:T(8,128)} %bitcast.15, f32[2,64,256]{2,1,0:T(8,128)} %refs_12_.1), custom_call_target="tpu_custom_call" | custom-call | flops 201326592 | bytes 600000 | tf_op jit(solution)/shard_map/pallas_call | solution.py:458
  3.6 5.2 %collective-permute-start = (f32[1,64,128]{2,1,0:T(8,128)}, f32[1,64,128]{2,1,0:T(8,128)S(1)}, u32[]{:S(2)}, u32[]{:S(2)}) collective-permute-start(f32[1,64,128]{2,1,0:T(8,128)} %get-tuple-element.25), channel_id=1, source_target_pairs={{0,96},{1,32},{2,64},{3,0},{4,160},{5,224},{6,128},{7,192},{8,104}... | collective-permute-start | bytes 98312 | tf_op jit(solution)/shard_map/ppermute | solution.py:476
  8.9 4.1 %collective-permute-start.1 = (f32[1,64,128]{2,1,0:T(8,128)}, f32[1,64,128]{2,1,0:T(8,128)S(1)}, u32[]{:S(2)}, u32[]{:S(2)}) collective-permute-start(f32[1,64,128]{2,1,0:T(8,128)} %get-tuple-element.25), channel_id=1, source_target_pairs={{0,128},{1,192},{2,160},{3,224},{4,64},{5,0},{6,96},{7,32},{8,136}... | collective-permute-start | bytes 98312 | tf_op jit(solution)/shard_map/ppermute | solution.py:476
  13.0 5.8 %all-to-all-start = ((f32[8,2,64,256]{3,2,1,0:T(8,128)}), f32[8,2,64,256]{3,2,1,0:T(8,128)S(1)}, u32[]{:S(2)}, u32[]{:S(2)}) async-start(f32[8,2,64,256]{3,2,1,0:T(8,128)} %get-tuple-element.26), calls=%async_computation | async-start | bytes 2097152 | tf_op jit(solution)/shard_map/all_to_all | solution.py:474
  18.9 0.0 copy-done.13
  18.9 0.1 copy.23.refs_15_
  19.0 0.1 dynamic_slice.6
  19.1 0.0 collective-permute-done
  19.1 0.0 collective-permute-done.1
  19.1 1.5 %collective-permute-start.2 = (f32[2,64,128]{2,1,0:T(8,128)S(1)}, f32[2,64,128]{2,1,0:T(8,128)S(1)}, u32[]{:S(2)}, u32[]{:S(2)}) collective-permute-start(f32[2,64,128]{2,1,0:T(8,128)S(1)} %pad_maximum_fusion), channel_id=1, source_target_pairs={{0,64},{8,72},{16,80},{24,88},{32,96},{40,104},{48,112},{56,120},{... | collective-permute-start | bytes 196616 | tf_op jit(solution)/shard_map/ppermute | solution.py:89
  20.6 2.6 %collective-permute-done.2 = f32[2,64,128]{2,1,0:T(8,128)S(1)} collective-permute-done((f32[2,64,128]{2,1,0:T(8,128)S(1)}, f32[2,64,128]{2,1,0:T(8,128)S(1)}, u32[]{:S(2)}, u32[]{:S(2)}) %collective-permute-start.2) | collective-permute-done | bytes 65568 | tf_op jit(solution)/shard_map/ppermute | solution.py:89
  23.2 2.2 %collective-permute-start.3 = (f32[4,64,128]{2,1,0:T(8,128)S(1)}, f32[4,64,128]{2,1,0:T(8,128)S(1)}, u32[]{:S(2)}, u32[]{:S(2)}) collective-permute-start(f32[4,64,128]{2,1,0:T(8,128)S(1)} %constant_dynamic-update-slice_fusion.refs_0_), channel_id=1, source_target_pairs={{0,32},{8,40},{16,48},{24,56},{32,0},{40,8},{48,16},{56,24},{64,96... | collective-permute-start | bytes 393224 | tf_op jit(solution)/shard_map/ppermute | solution.py:89
  25.4 0.1 broadcast_multiply_fusion
  25.5 0.1 mul.43.refs_17_
  25.7 1.2 %collective-permute-start.6 = (f32[4,64,128]{2,1,0:T(8,128)S(1)}, f32[4,64,128]{2,1,0:T(8,128)S(1)}, u32[]{:S(2)}, u32[]{:S(2)}) collective-permute-start(f32[4,64,128]{2,1,0:T(8,128)S(1)} %constant_dynamic-update-slice_fusion.refs_0_), channel_id=1, source_target_pairs={{0,16},{8,24},{16,0},{24,8},{32,48},{40,56},{48,32},{56,40},{64,80... | collective-permute-start | bytes 393224 | tf_op jit(solution)/shard_map/ppermute | solution.py:89
  26.9 1.2 %collective-permute-done.3.refs_1_ = f32[4,64,128]{2,1,0:T(8,128)S(1)} collective-permute-done((f32[4,64,128]{2,1,0:T(8,128)S(1)}, f32[4,64,128]{2,1,0:T(8,128)S(1)}, u32[]{:S(2)}, u32[]{:S(2)}) %collective-permute-start.3) | collective-permute-done | bytes 131104 | tf_op jit(solution)/shard_map/ppermute | solution.py:89
  28.1 1.1 %collective-permute-start.7 = (f32[4,64,128]{2,1,0:T(8,128)S(1)}, f32[4,64,128]{2,1,0:T(8,128)S(1)}, u32[]{:S(2)}, u32[]{:S(2)}) collective-permute-start(f32[4,64,128]{2,1,0:T(8,128)S(1)} %collective-permute-done.3.refs_1_), channel_id=1, source_target_pairs={{0,16},{8,24},{16,0},{24,8},{32,48},{40,56},{48,32},{56,40},{64,80... | collective-permute-start | bytes 393224 | tf_op jit(solution)/shard_map/ppermute | solution.py:89
  29.2 4.2 %collective-permute-start.4 = (f32[4,64,128]{2,1,0:T(8,128)S(1)}, f32[4,64,128]{2,1,0:T(8,128)S(1)}, u32[]{:S(2)}, u32[]{:S(2)}) collective-permute-start(f32[4,64,128]{2,1,0:T(8,128)S(1)} %constant_dynamic-update-slice_fusion.refs_0_), channel_id=1, source_target_pairs={{0,8},{8,0},{16,24},{24,16},{32,40},{40,32},{48,56},{56,48},{64,72... | collective-permute-start | bytes 393224 | tf_op jit(solution)/shard_map/ppermute | solution.py:89
  33.5 0.0 collective-permute-start.5
  33.5 0.0 collective-permute-done.6.refs_4_
  33.5 3.0 %collective-permute-start.8 = (f32[4,64,128]{2,1,0:T(8,128)S(1)}, f32[4,64,128]{2,1,0:T(8,128)S(1)}, u32[]{:S(2)}, u32[]{:S(2)}) collective-permute-start(f32[4,64,128]{2,1,0:T(8,128)S(1)} %collective-permute-done.6.refs_4_), channel_id=1, source_target_pairs={{0,8},{8,0},{16,24},{24,16},{32,40},{40,32},{48,56},{56,48},{64,72... | collective-permute-start | bytes 393224 | tf_op jit(solution)/shard_map/ppermute | solution.py:89
  36.4 0.0 collective-permute-done.7.refs_5_
  36.4 1.4 %collective-permute-start.9 = (f32[4,64,128]{2,1,0:T(8,128)S(1)}, f32[4,64,128]{2,1,0:T(8,128)S(1)}, u32[]{:S(2)}, u32[]{:S(2)}) collective-permute-start(f32[4,64,128]{2,1,0:T(8,128)S(1)} %collective-permute-done.7.refs_5_), channel_id=1, source_target_pairs={{0,8},{8,0},{16,24},{24,16},{32,40},{40,32},{48,56},{56,48},{64,72... | collective-permute-start | bytes 393224 | tf_op jit(solution)/shard_map/ppermute | solution.py:89
  37.8 0.0 all-to-all-done.all_ref
  37.9 0.0 copy-start
  37.9 0.0 copy-start.2
  37.9 0.0 copy-start.3
  37.9 0.0 copy-start.4
  37.9 2.3 %shard_map.186 = (f32[2,512,512]{2,1,0:T(8,128)S(1)}, bf16[2,2,256,512]{3,2,1,0:T(8,128)(2,1)S(1)}, f32[128,256]{1,0:T(8,128)S(1)}) custom-call(f32[8,2,64,256]{3,2,1,0:T(8,128)S(1)} %all-to-all-done.all_ref, f32[2,64,256]{2,1,0:T(8,128)S(1)} %copy-done.1, f32[1,256]{1,0:T(1,128)S(1)} %bitcast.13, f32[256,256]{1,0:T(8,128)S(1)} %copy-done.7, ...), custom_call_target="tpu_custom_call" | custom-call | flops 1610612736 | bytes 6291456 | tf_op jit(solution)/shard_map/pallas_call | solution.py:489
  40.3 0.0 collective-permute-done.4.refs_2_
  40.3 0.0 collective-permute-done.5.refs_3_
  40.3 0.0 collective-permute-done.8.refs_6_
  40.3 0.0 collective-permute-done.9.refs_7_
  40.3 0.1 broadcast_in_dim.23.refs_9_
  40.5 0.0 copy-start.5
  40.5 0.0 copy-start.6
  40.5 0.0 copy-start.12
  40.5 4.2 %shard_map.187 = (f32[2,64,256]{2,1,0:T(8,128)}, f32[4,8,128]{2,1,0:T(8,128)S(1)}, f32[8,40,128]{2,1,0:T(8,128)}) custom-call(s32[128]{0:T(128)S(1)} %copy-done.4, f32[4,64,128]{2,1,0:T(8,128)S(1)} %constant_dynamic-update-slice_fusion.refs_0_, f32[4,64,128]{2,1,0:T(8,128)S(1)} %collective-permute-done.3.refs_1_, ...), custom_call_target="tpu_custom_call" | custom-call | flops 805306368 | bytes 6291456 | tf_op jit(solution)/shard_map/pallas_call | solution.py:505
  44.7 7.0 %all-to-all-start.1 = ((f32[8,40,128]{2,1,0:T(8,128)}), f32[8,40,128]{2,1,0:T(8,128)S(1)}, u32[]{:S(2)}, u32[]{:S(2)}) async-start(f32[8,40,128]{2,1,0:T(8,128)} %get-tuple-element.32), calls=%async_computation.1 | async-start | bytes 327680 | tf_op jit(solution)/shard_map/all_to_all | solution.py:528
  51.7 6.0 %collective-permute-start.10 = (f32[4,8,128]{2,1,0:T(8,128)S(1)}, f32[4,8,128]{2,1,0:T(8,128)S(1)}, u32[]{:S(2)}, u32[]{:S(2)}) collective-permute-start(f32[4,8,128]{2,1,0:T(8,128)S(1)} %get-tuple-element.31), channel_id=1, source_target_pairs={{128,0},{64,1},{96,2},{32,3},{192,4},{0,5},{160,6},{224,7},{136,8}... | collective-permute-start | bytes 49160 | tf_op jit(solution)/shard_map/ppermute | solution.py:536
  57.7 2.6 %collective-permute-done.10.left_ref = f32[4,8,128]{2,1,0:T(8,128)S(1)} collective-permute-done((f32[4,8,128]{2,1,0:T(8,128)S(1)}, f32[4,8,128]{2,1,0:T(8,128)S(1)}, u32[]{:S(2)}, u32[]{:S(2)}) %collective-permute-start.10) | collective-permute-done | bytes 16416 | tf_op jit(solution)/shard_map/ppermute | solution.py:536
  60.3 0.0 all-to-all-done.1.refs_0_
  60.3 2.1 %collective-permute-start.12 = (f32[8,40,128]{2,1,0:T(8,128)S(1)}, f32[8,40,128]{2,1,0:T(8,128)S(1)}, u32[]{:S(2)}, u32[]{:S(2)}) collective-permute-start(f32[8,40,128]{2,1,0:T(8,128)S(1)} %all-to-all-done.1.refs_0_), channel_id=1, source_target_pairs={{0,16},{8,24},{16,0},{24,8},{32,48},{40,56},{48,32},{56,40},{64,80... | collective-permute-start | bytes 491528 | tf_op jit(solution)/shard_map/ppermute | solution.py:89
  62.3 0.7 shard_map.188
  63.1 9.3 %all-to-all-start.2 = ((f32[32,8,128]{2,1,0:T(8,128)}), f32[32,8,128]{2,1,0:T(8,128)S(1)}, u32[]{:S(2)}, u32[]{:S(2)}) async-start(f32[32,8,128]{2,1,0:T(8,128)} %bitcast.7), calls=%async_computation.2 | async-start | bytes 262144 | tf_op jit(solution)/shard_map/all_to_all | solution.py:545
  72.4 0.3 collective-permute-start.11
  72.7 7.4 %all-to-all-done.2.refs_4_ = f32[32,8,128]{2,1,0:T(8,128)S(1)} async-done(((f32[32,8,128]{2,1,0:T(8,128)}), f32[32,8,128]{2,1,0:T(8,128)S(1)}, u32[]{:S(2)}, u32[]{:S(2)}) %all-to-all-start.2) | async-done | bytes 131104 | tf_op jit(solution)/shard_map/all_to_all | solution.py:545
  80.1 0.0 collective-permute-done.12.refs_2_
  80.1 0.2 collective-permute-start.13
  80.3 0.1 dynamic_slice.7.rows_live_ref
  80.4 0.1 dynamic-slice_bitcast_fusion
  80.5 0.1 copy.25.refs_7_
  80.6 0.0 collective-permute-done.11.refs_1_
  80.6 0.9 %collective-permute-done.13.refs_3_ = f32[8,40,128]{2,1,0:T(8,128)S(1)} collective-permute-done((f32[8,40,128]{2,1,0:T(8,128)S(1)}, f32[8,40,128]{2,1,0:T(8,128)S(1)}, u32[]{:S(2)}, u32[]{:S(2)}) %collective-permute-start.13) | collective-permute-done | bytes 163872 | tf_op jit(solution)/shard_map/ppermute | solution.py:89
  81.5 0.0 copy-done.12
  81.5 5.5 %shard_map.189 = f32[16,64,128]{2,1,0:T(8,128)} custom-call(s32[64]{0:T(128)S(1)} %copy-done.12, f32[16]{0:T(128)S(1)} %dynamic_slice.7.rows_live_ref, f32[8,40,128]{2,1,0:T(8,128)S(1)} %all-to-all-done.1.refs_0_, f32[8,40,128]{2,1,0:T(8,128)S(1)} %collective-permute-done.11.refs_1_, f32[8,40,128]{2,1,0:T(8,128)S(1)} %collective-permute-done.12.refs_2_, ...), custom_call_target="tpu_custom_call" | custom-call | flops 1610612736 | bytes 4194304 | tf_op jit(solution)/shard_map/pallas_call | solution.py:554
  (24 shorter events, 0.1 us)
Async XLA Ops:
  0.6 37.2 %copy-start.1 = (f32[2,64,256]{2,1,0:T(8,128)S(1)}, f32[2,64,256]{2,1,0:T(8,128)}, u32[]{:S(2)}) copy-start(f32[2,64,256]{2,1,0:T(8,128)} %refs_12_.1) | copy-start | bytes 393220
  0.6 18.2 %copy-start.15 = (s32[2]{0:T(128)S(1)}, s32[2]{0:T(128)}, u32[]{:S(2)}) copy-start(s32[2]{0:T(128)} %param.22) | copy-start | bytes 28
  0.7 18.2 %copy-start.13 = (f32[256,32]{0,1:T(8,128)S(1)}, f32[256,32]{0,1:T(8,128)}, u32[]{:S(2)}) copy-start(f32[256,32]{0,1:T(8,128)} %param.33) | copy-start | bytes 98308
  0.7 18.3 %copy-start.14 = (s32[512]{0:T(512)S(1)}, s32[512]{0:T(512)}, u32[]{:S(2)}) copy-start(s32[512]{0:T(512)} %param.23) | copy-start | bytes 6148
  0.7 37.2 %copy-start.11 = (f32[256]{0:T(256)S(1)}, f32[256]{0:T(256)}, u32[]{:S(2)}) copy-start(f32[256]{0:T(256)} %param.24) | copy-start | bytes 3076
  0.7 37.2 %copy-start.7 = (f32[256,256]{1,0:T(8,128)S(1)}, f32[256,256]{1,0:T(8,128)}, u32[]{:S(2)}) copy-start(f32[256,256]{1,0:T(8,128)} %wq_ref.1) | copy-start | bytes 786436
  0.7 37.2 %copy-start.8 = (f32[256,256]{1,0:T(8,128)S(1)}, f32[256,256]{1,0:T(8,128)}, u32[]{:S(2)}) copy-start(f32[256,256]{1,0:T(8,128)} %wk_ref.1) | copy-start | bytes 786436
  0.7 37.2 %copy-start.9 = (f32[256,256]{1,0:T(8,128)S(1)}, f32[256,256]{1,0:T(8,128)}, u32[]{:S(2)}) copy-start(f32[256,256]{1,0:T(8,128)} %wv_ref.1) | copy-start | bytes 786436
  0.7 37.2 %copy-start.10 = (f32[256,256]{1,0:T(8,128)S(1)}, f32[256,256]{1,0:T(8,128)}, u32[]{:S(2)}) copy-start(f32[256,256]{1,0:T(8,128)} %wg_ref.1) | copy-start | bytes 786436
  3.6 15.4 %collective-permute-start = (f32[1,64,128]{2,1,0:T(8,128)}, f32[1,64,128]{2,1,0:T(8,128)S(1)}, u32[]{:S(2)}, u32[]{:S(2)}) collective-permute-start(f32[1,64,128]{2,1,0:T(8,128)} %get-tuple-element.25), channel_id=1, source_target_pairs={{0,96},{1,32},{2,64},{3,0},{4,160},{5,224},{6,128},{7,192},{8,104}... | collective-permute-start | bytes 98312 | tf_op jit(solution)/shard_map/ppermute | solution.py:476
  8.9 10.2 %collective-permute-start.1 = (f32[1,64,128]{2,1,0:T(8,128)}, f32[1,64,128]{2,1,0:T(8,128)S(1)}, u32[]{:S(2)}, u32[]{:S(2)}) collective-permute-start(f32[1,64,128]{2,1,0:T(8,128)} %get-tuple-element.25), channel_id=1, source_target_pairs={{0,128},{1,192},{2,160},{3,224},{4,64},{5,0},{6,96},{7,32},{8,136}... | collective-permute-start | bytes 98312 | tf_op jit(solution)/shard_map/ppermute | solution.py:476
  13.0 24.8 %all-to-all-start = ((f32[8,2,64,256]{3,2,1,0:T(8,128)}), f32[8,2,64,256]{3,2,1,0:T(8,128)S(1)}, u32[]{:S(2)}, u32[]{:S(2)}) async-start(f32[8,2,64,256]{3,2,1,0:T(8,128)} %get-tuple-element.26), calls=%async_computation | async-start | bytes 2097152 | tf_op jit(solution)/shard_map/all_to_all | solution.py:474
  19.1 4.1 %collective-permute-start.2 = (f32[2,64,128]{2,1,0:T(8,128)S(1)}, f32[2,64,128]{2,1,0:T(8,128)S(1)}, u32[]{:S(2)}, u32[]{:S(2)}) collective-permute-start(f32[2,64,128]{2,1,0:T(8,128)S(1)} %pad_maximum_fusion), channel_id=1, source_target_pairs={{0,64},{8,72},{16,80},{24,88},{32,96},{40,104},{48,112},{56,120},{... | collective-permute-start | bytes 196616 | tf_op jit(solution)/shard_map/ppermute | solution.py:89
  23.2 4.9 %collective-permute-start.3 = (f32[4,64,128]{2,1,0:T(8,128)S(1)}, f32[4,64,128]{2,1,0:T(8,128)S(1)}, u32[]{:S(2)}, u32[]{:S(2)}) collective-permute-start(f32[4,64,128]{2,1,0:T(8,128)S(1)} %constant_dynamic-update-slice_fusion.refs_0_), channel_id=1, source_target_pairs={{0,32},{8,40},{16,48},{24,56},{32,0},{40,8},{48,16},{56,24},{64,96... | collective-permute-start | bytes 393224 | tf_op jit(solution)/shard_map/ppermute | solution.py:89
  25.7 7.8 %collective-permute-start.6 = (f32[4,64,128]{2,1,0:T(8,128)S(1)}, f32[4,64,128]{2,1,0:T(8,128)S(1)}, u32[]{:S(2)}, u32[]{:S(2)}) collective-permute-start(f32[4,64,128]{2,1,0:T(8,128)S(1)} %constant_dynamic-update-slice_fusion.refs_0_), channel_id=1, source_target_pairs={{0,16},{8,24},{16,0},{24,8},{32,48},{40,56},{48,32},{56,40},{64,80... | collective-permute-start | bytes 393224 | tf_op jit(solution)/shard_map/ppermute | solution.py:89
  28.1 8.4 %collective-permute-start.7 = (f32[4,64,128]{2,1,0:T(8,128)S(1)}, f32[4,64,128]{2,1,0:T(8,128)S(1)}, u32[]{:S(2)}, u32[]{:S(2)}) collective-permute-start(f32[4,64,128]{2,1,0:T(8,128)S(1)} %collective-permute-done.3.refs_1_), channel_id=1, source_target_pairs={{0,16},{8,24},{16,0},{24,8},{32,48},{40,56},{48,32},{56,40},{64,80... | collective-permute-start | bytes 393224 | tf_op jit(solution)/shard_map/ppermute | solution.py:89
  29.2 11.0 %collective-permute-start.4 = (f32[4,64,128]{2,1,0:T(8,128)S(1)}, f32[4,64,128]{2,1,0:T(8,128)S(1)}, u32[]{:S(2)}, u32[]{:S(2)}) collective-permute-start(f32[4,64,128]{2,1,0:T(8,128)S(1)} %constant_dynamic-update-slice_fusion.refs_0_), channel_id=1, source_target_pairs={{0,8},{8,0},{16,24},{24,16},{32,40},{40,32},{48,56},{56,48},{64,72... | collective-permute-start | bytes 393224 | tf_op jit(solution)/shard_map/ppermute | solution.py:89
  33.5 6.8 %collective-permute-start.5 = (f32[4,64,128]{2,1,0:T(8,128)S(1)}, f32[4,64,128]{2,1,0:T(8,128)S(1)}, u32[]{:S(2)}, u32[]{:S(2)}) collective-permute-start(f32[4,64,128]{2,1,0:T(8,128)S(1)} %collective-permute-done.3.refs_1_), channel_id=1, source_target_pairs={{0,8},{8,0},{16,24},{24,16},{32,40},{40,32},{48,56},{56,48},{64,72... | collective-permute-start | bytes 393224 | tf_op jit(solution)/shard_map/ppermute | solution.py:89
  33.5 6.8 %collective-permute-start.8 = (f32[4,64,128]{2,1,0:T(8,128)S(1)}, f32[4,64,128]{2,1,0:T(8,128)S(1)}, u32[]{:S(2)}, u32[]{:S(2)}) collective-permute-start(f32[4,64,128]{2,1,0:T(8,128)S(1)} %collective-permute-done.6.refs_4_), channel_id=1, source_target_pairs={{0,8},{8,0},{16,24},{24,16},{32,40},{40,32},{48,56},{56,48},{64,72... | collective-permute-start | bytes 393224 | tf_op jit(solution)/shard_map/ppermute | solution.py:89
  36.4 3.8 %collective-permute-start.9 = (f32[4,64,128]{2,1,0:T(8,128)S(1)}, f32[4,64,128]{2,1,0:T(8,128)S(1)}, u32[]{:S(2)}, u32[]{:S(2)}) collective-permute-start(f32[4,64,128]{2,1,0:T(8,128)S(1)} %collective-permute-done.7.refs_5_), channel_id=1, source_target_pairs={{0,8},{8,0},{16,24},{24,16},{32,40},{40,32},{48,56},{56,48},{64,72... | collective-permute-start | bytes 393224 | tf_op jit(solution)/shard_map/ppermute | solution.py:89
  37.9 2.5 %copy-start = (f32[256,256]{1,0:T(8,128)S(1)}, f32[256,256]{1,0:T(8,128)}, u32[]{:S(2)}) copy-start(f32[256,256]{1,0:T(8,128)} %refs_13_.1) | copy-start | bytes 786436
  37.9 2.5 %copy-start.2 = (f32[256,32]{0,1:T(8,128)S(1)}, f32[256,32]{0,1:T(8,128)}, u32[]{:S(2)}) copy-start(f32[256,32]{0,1:T(8,128)} %param.34) | copy-start | bytes 98308
  37.9 2.5 %copy-start.3 = (f32[256]{0:T(256)S(1)}, f32[256]{0:T(256)}, u32[]{:S(2)}) copy-start(f32[256]{0:T(256)} %param.32) | copy-start | bytes 3076
  37.9 2.5 %copy-start.4 = (s32[128]{0:T(128)S(1)}, s32[128]{0:T(128)}, u32[]{:S(2)}) copy-start(s32[128]{0:T(128)} %constant.53.clone.spot_ref) | copy-start | bytes 1540
  40.5 41.0 %copy-start.5 = (f32[16,64,128]{2,1,0:T(8,128)S(1)}, f32[16,64,128]{2,1,0:T(8,128)}, u32[]{:S(2)}) copy-start(f32[16,64,128]{2,1,0:T(8,128)} %refs_6_.1) | copy-start | bytes 1572868
  40.5 41.0 %copy-start.6 = (f32[1024,128]{1,0:T(8,128)S(1)}, f32[1024,128]{1,0:T(8,128)}, u32[]{:S(2)}) copy-start(f32[1024,128]{1,0:T(8,128)} %refs_5_.1) | copy-start | bytes 1572868
  40.5 41.0 %copy-start.12 = (s32[64]{0:T(128)S(1)}, s32[64]{0:T(128)}, u32[]{:S(2)}) copy-start(s32[64]{0:T(128)} %constant.54.clone.once_ref) | copy-start | bytes 772
  44.7 15.6 %all-to-all-start.1 = ((f32[8,40,128]{2,1,0:T(8,128)}), f32[8,40,128]{2,1,0:T(8,128)S(1)}, u32[]{:S(2)}, u32[]{:S(2)}) async-start(f32[8,40,128]{2,1,0:T(8,128)} %get-tuple-element.32), calls=%async_computation.1 | async-start | bytes 327680 | tf_op jit(solution)/shard_map/all_to_all | solution.py:528
  51.7 8.6 %collective-permute-start.10 = (f32[4,8,128]{2,1,0:T(8,128)S(1)}, f32[4,8,128]{2,1,0:T(8,128)S(1)}, u32[]{:S(2)}, u32[]{:S(2)}) collective-permute-start(f32[4,8,128]{2,1,0:T(8,128)S(1)} %get-tuple-element.31), channel_id=1, source_target_pairs={{128,0},{64,1},{96,2},{32,3},{192,4},{0,5},{160,6},{224,7},{136,8}... | collective-permute-start | bytes 49160 | tf_op jit(solution)/shard_map/ppermute | solution.py:536
  60.3 19.8 %collective-permute-start.12 = (f32[8,40,128]{2,1,0:T(8,128)S(1)}, f32[8,40,128]{2,1,0:T(8,128)S(1)}, u32[]{:S(2)}, u32[]{:S(2)}) collective-permute-start(f32[8,40,128]{2,1,0:T(8,128)S(1)} %all-to-all-done.1.refs_0_), channel_id=1, source_target_pairs={{0,16},{8,24},{16,0},{24,8},{32,48},{40,56},{48,32},{56,40},{64,80... | collective-permute-start | bytes 491528 | tf_op jit(solution)/shard_map/ppermute | solution.py:89
  63.1 17.0 %all-to-all-start.2 = ((f32[32,8,128]{2,1,0:T(8,128)}), f32[32,8,128]{2,1,0:T(8,128)S(1)}, u32[]{:S(2)}, u32[]{:S(2)}) async-start(f32[32,8,128]{2,1,0:T(8,128)} %bitcast.7), calls=%async_computation.2 | async-start | bytes 262144 | tf_op jit(solution)/shard_map/all_to_all | solution.py:545
  72.4 8.2 %collective-permute-start.11 = (f32[8,40,128]{2,1,0:T(8,128)S(1)}, f32[8,40,128]{2,1,0:T(8,128)S(1)}, u32[]{:S(2)}, u32[]{:S(2)}) collective-permute-start(f32[8,40,128]{2,1,0:T(8,128)S(1)} %all-to-all-done.1.refs_0_), channel_id=1, source_target_pairs={{0,8},{8,0},{16,24},{24,16},{32,40},{40,32},{48,56},{56,48},{64,72... | collective-permute-start | bytes 491528 | tf_op jit(solution)/shard_map/ppermute | solution.py:89
  80.1 1.4 %collective-permute-start.13 = (f32[8,40,128]{2,1,0:T(8,128)S(1)}, f32[8,40,128]{2,1,0:T(8,128)S(1)}, u32[]{:S(2)}, u32[]{:S(2)}) collective-permute-start(f32[8,40,128]{2,1,0:T(8,128)S(1)} %collective-permute-done.12.refs_2_), channel_id=1, source_target_pairs={{0,8},{8,0},{16,24},{24,16},{32,40},{40,32},{48,56},{56,48},{64,72... | collective-permute-start | bytes 491528 | tf_op jit(solution)/shard_map/ppermute | solution.py:89

commit v3 on v2

--- a/solution.py
+++ b/solution.py
@@ -272,24 +272,32 @@
     lane = lax.broadcasted_iota(jnp.int32, (32, 128), 1) // 16
     folded = [jnp.zeros((32, 128), f32) for _ in range(8)]
     for s in range(2):
-        for a in range(4):
-            columns = pl.ds(128 * a, 128)
-            tiles = []
-            for b in range(8):
-                rows = pl.ds(64 * b, 64)
-                tiles.append(
-                    (logit_ref[s, rows, columns] + bias_ref[half_position(row, spot_ref[spots_at + b], a)])
-                    + key_ref[rows, :]
-                )
-            logits = jnp.concatenate(tiles, axis=0)
-            exponent = jnp.exp(logits - jnp.max(logits, axis=0, keepdims=True))
-            weights = exponent * (1.0 / jnp.sum(exponent, axis=0, keepdims=True))
-            part = three((value_ref[0, s], value_ref[1, s]), split(weights))
-            for h in range(8):
-                moved = pltpu.roll(
-                    part[32 * h : 32 * h + 32], (64 * s + 16 * a - 16 * h) % 128, 1
-                )
-                folded[h] = jnp.where(lane == 4 * s + a, moved, folded[h])
+        for pair in range(2):
+            halves = []
+            for a in (2 * pair, 2 * pair + 1):
+                columns = pl.ds(128 * a, 128)
+                tiles = []
+                for b in range(8):
+                    rows = pl.ds(64 * b, 64)
+                    spot = half_position(row, spot_ref[spots_at + b], a)
+                    tiles.append((logit_ref[s, rows, columns] + bias_ref[spot]) + key_ref[rows, :])
+                logits = jnp.concatenate(tiles, axis=0)
+                exponent = jnp.exp(logits - jnp.max(logits, axis=0, keepdims=True))
+                weights = exponent * (1.0 / jnp.sum(exponent, axis=0, keepdims=True))
+                halves.append(split(weights))
+            part = three(
+                (value_ref[0, s], value_ref[1, s]),
+                [jnp.concatenate([halves[0][k], halves[1][k]], axis=1) for k in range(2)],
+            )
+            for e in range(2):
+                a = 2 * pair + e
+                for h in range(8):
+                    moved = pltpu.roll(
+                        part[32 * h : 32 * h + 32, 128 * e : 128 * e + 128],
+                        (64 * s + 16 * a - 16 * h) % 128,
+                        1,
+                    )
+                    folded[h] = jnp.where(lane == 4 * s + a, moved, folded[h])
     attended = jnp.transpose(jnp.concatenate(folded, axis=0)) * gate_ref[...]
     updated = own_ref[...].reshape(128, 256) + dot_three(attended, wf_ref[...])
     msa_ref[...] = updated.reshape(2, 64, 256)
@@ -330,6 +338,7 @@
     sorted_ref,
     left_ref,
     right_ref,
+    outer_ref,
 ):
     for q, piece_ref in enumerate(piece_refs):
         for k in range(Z):
@@ -380,12 +389,17 @@
     ]
     weight = split(jnp.transpose(jnp.concatenate(columns, axis=1)))
     lane = lax.broadcasted_iota(jnp.int32, (128, 128), 1) < 64
+    for n in range(8):
+        columns = pl.ds(256 * n, 256)
+        outer_ref[:, columns] = dot(left_ref[...], right_ref[:, columns])
     for q in range(8):
-        outer = dot(left_ref[64 * q : 64 * q + 64, :], right_ref[...])
         stacked = jnp.concatenate(
             [
                 jnp.concatenate(
-                    [outer[32 * e : 32 * e + 32, 128 * d : 128 * d + 128] for d in range(16)],
+                    [
+                        outer_ref[64 * q + 32 * e : 64 * q + 32 * e + 32, 128 * d : 128 * d + 128]
+                        for d in range(16)
+                    ],
                     axis=0,
                 )
                 for e in range(2)
@@ -561,6 +575,7 @@
             pltpu.VMEM((256, 128), f32),
             pltpu.VMEM((512, 256), bf16),
             pltpu.VMEM((256, 2048), bf16),
+            pltpu.VMEM((512, 2048), f32),
         ],
         flops=3 * 2 * 1024 * 1024 * 256,
         touched=4 * MIB,

time: 87.3 us -> 86.1 us (0.986)
  Pallas kernels: 15.6 us -> 14.4 us
  transfers between devices with their start and end apart: 17 -> 17, of which waited for: 5 -> 5; matrix products, arithmetic and copies ran while one was open for 1% -> 1% of each run, Pallas kernels for 3% -> 4%
where the time goes in v3:
time: 86.1 us; the launch traced here: 85.7 us
  starting transfers between devices  54.8 us (64%)
  waiting for transfers between devices  14.7 us (17%)
  Pallas kernels  14.4 us (17%)
  between operations  0.99 us (1%)
    ppermute x11, starting transfers between devices, from_neighbour(): return lax.ppermute(v, 'row', [(r, r ^ bit) for r in range(Z * A)])  17.3 us
    all_to_all x1, starting transfers between devices, body(): lax.all_to_all(spread.reshape(A * H, 8, 128), both, 0, 0, tiled=True, axi...  9.32 us
    all_to_all x1, waiting for transfers between devices, body(): lax.all_to_all(spread.reshape(A * H, 8, 128), both, 0, 0, tiled=True, axi...  7.38 us
    all_to_all x1, starting transfers between devices, body(): lax.all_to_all(right, 'row', 0, 0, tiled=True, axis_index_groups=[[4 * z...  7.03 us
    ppermute x1, starting transfers between devices, body(): left = lax.ppermute(left, both, [(d, s) for s, d in moves(ONCE)])  5.97 us
    all_to_all x1, starting transfers between devices, body(): everyone = lax.all_to_all(copies, 'head', 0, 0, tiled=True)  5.83 us
    ppermute x1, starting transfers between devices, body(): lax.ppermute(block, both, moves(TWICE[:, 0]))  5.25 us
    pallas_call x1, Pallas kernels, body(): call(outer_kernel, smem(2) + vmem(8), vmem(1), [struct(16, 64, 128)], scr...  4.75 us
  transfers between devices with their start and end apart: 17, of which 5 were waited for; matrix products, arithmetic and copies ran while one was open for 1% of the time, Pallas kernels for 4%

profile of v3, /device:TPU:1, one launch (start us, length us, event | category | flops | bytes accessed | tf_op | source)
XLA Modules:
  0.0 85.7 jit_solution(18443212513300633654)
XLA Ops:
  0.6 0.0 copy-start.1
  0.6 0.0 copy-start.15
  0.7 0.0 copy-start.13
  0.7 0.0 copy-start.14
  0.7 0.0 copy-start.11
  0.7 0.0 copy-start.7
  0.7 0.0 copy-start.8
  0.7 0.0 copy-start.9
  0.7 2.9 %shard_map.185 = (f32[1,64,128]{2,1,0:T(8,128)}, f32[8,2,64,256]{3,2,1,0:T(8,128)}) custom-call(f32[16,64,128]{2,1,0:T(8,128)} %refs_6_.1, f32[1,128]{1,0:T(1,128)} %bitcast.16, f32[8,128]{1,0:T(8,128)} %bitcast.15, f32[2,64,256]{2,1,0:T(8,128)} %refs_12_.1), custom_call_target="tpu_custom_call" | custom-call | flops 201326592 | bytes 600000 | tf_op jit(solution)/shard_map/pallas_call | solution.py:472
  3.6 5.2 %collective-permute-start = (f32[1,64,128]{2,1,0:T(8,128)}, f32[1,64,128]{2,1,0:T(8,128)S(1)}, u32[]{:S(2)}, u32[]{:S(2)}) collective-permute-start(f32[1,64,128]{2,1,0:T(8,128)} %get-tuple-element.25), channel_id=1, source_target_pairs={{0,96},{1,32},{2,64},{3,0},{4,160},{5,224},{6,128},{7,192},{8,104}... | collective-permute-start | bytes 98312 | tf_op jit(solution)/shard_map/ppermute | solution.py:490
  8.9 4.1 %collective-permute-start.1 = (f32[1,64,128]{2,1,0:T(8,128)}, f32[1,64,128]{2,1,0:T(8,128)S(1)}, u32[]{:S(2)}, u32[]{:S(2)}) collective-permute-start(f32[1,64,128]{2,1,0:T(8,128)} %get-tuple-element.25), channel_id=1, source_target_pairs={{0,128},{1,192},{2,160},{3,224},{4,64},{5,0},{6,96},{7,32},{8,136}... | collective-permute-start | bytes 98312 | tf_op jit(solution)/shard_map/ppermute | solution.py:490
  13.0 5.8 %all-to-all-start = ((f32[8,2,64,256]{3,2,1,0:T(8,128)}), f32[8,2,64,256]{3,2,1,0:T(8,128)S(1)}, u32[]{:S(2)}, u32[]{:S(2)}) async-start(f32[8,2,64,256]{3,2,1,0:T(8,128)} %get-tuple-element.26), calls=%async_computation | async-start | bytes 2097152 | tf_op jit(solution)/shard_map/all_to_all | solution.py:488
  18.9 0.1 copy.23.refs_15_
  19.0 0.1 dynamic_slice.6
  19.1 0.0 collective-permute-done
  19.1 0.0 collective-permute-done.1
  19.1 1.5 %collective-permute-start.2 = (f32[2,64,128]{2,1,0:T(8,128)S(1)}, f32[2,64,128]{2,1,0:T(8,128)S(1)}, u32[]{:S(2)}, u32[]{:S(2)}) collective-permute-start(f32[2,64,128]{2,1,0:T(8,128)S(1)} %pad_maximum_fusion), channel_id=1, source_target_pairs={{0,64},{8,72},{16,80},{24,88},{32,96},{40,104},{48,112},{56,120},{... | collective-permute-start | bytes 196616 | tf_op jit(solution)/shard_map/ppermute | solution.py:89
  20.6 2.6 %collective-permute-done.2 = f32[2,64,128]{2,1,0:T(8,128)S(1)} collective-permute-done((f32[2,64,128]{2,1,0:T(8,128)S(1)}, f32[2,64,128]{2,1,0:T(8,128)S(1)}, u32[]{:S(2)}, u32[]{:S(2)}) %collective-permute-start.2) | collective-permute-done | bytes 65568 | tf_op jit(solution)/shard_map/ppermute | solution.py:89
  23.2 2.2 %collective-permute-start.3 = (f32[4,64,128]{2,1,0:T(8,128)S(1)}, f32[4,64,128]{2,1,0:T(8,128)S(1)}, u32[]{:S(2)}, u32[]{:S(2)}) collective-permute-start(f32[4,64,128]{2,1,0:T(8,128)S(1)} %constant_dynamic-update-slice_fusion.refs_0_), channel_id=1, source_target_pairs={{0,32},{8,40},{16,48},{24,56},{32,0},{40,8},{48,16},{56,24},{64,96... | collective-permute-start | bytes 393224 | tf_op jit(solution)/shard_map/ppermute | solution.py:89
  25.4 0.1 broadcast_multiply_fusion
  25.5 0.1 mul.43.refs_17_
  25.7 1.2 %collective-permute-start.6 = (f32[4,64,128]{2,1,0:T(8,128)S(1)}, f32[4,64,128]{2,1,0:T(8,128)S(1)}, u32[]{:S(2)}, u32[]{:S(2)}) collective-permute-start(f32[4,64,128]{2,1,0:T(8,128)S(1)} %constant_dynamic-update-slice_fusion.refs_0_), channel_id=1, source_target_pairs={{0,16},{8,24},{16,0},{24,8},{32,48},{40,56},{48,32},{56,40},{64,80... | collective-permute-start | bytes 393224 | tf_op jit(solution)/shard_map/ppermute | solution.py:89
  26.9 1.2 %collective-permute-done.3.refs_1_ = f32[4,64,128]{2,1,0:T(8,128)S(1)} collective-permute-done((f32[4,64,128]{2,1,0:T(8,128)S(1)}, f32[4,64,128]{2,1,0:T(8,128)S(1)}, u32[]{:S(2)}, u32[]{:S(2)}) %collective-permute-start.3) | collective-permute-done | bytes 131104 | tf_op jit(solution)/shard_map/ppermute | solution.py:89
  28.1 1.1 %collective-permute-start.7 = (f32[4,64,128]{2,1,0:T(8,128)S(1)}, f32[4,64,128]{2,1,0:T(8,128)S(1)}, u32[]{:S(2)}, u32[]{:S(2)}) collective-permute-start(f32[4,64,128]{2,1,0:T(8,128)S(1)} %collective-permute-done.3.refs_1_), channel_id=1, source_target_pairs={{0,16},{8,24},{16,0},{24,8},{32,48},{40,56},{48,32},{56,40},{64,80... | collective-permute-start | bytes 393224 | tf_op jit(solution)/shard_map/ppermute | solution.py:89
  29.2 4.2 %collective-permute-start.4 = (f32[4,64,128]{2,1,0:T(8,128)S(1)}, f32[4,64,128]{2,1,0:T(8,128)S(1)}, u32[]{:S(2)}, u32[]{:S(2)}) collective-permute-start(f32[4,64,128]{2,1,0:T(8,128)S(1)} %constant_dynamic-update-slice_fusion.refs_0_), channel_id=1, source_target_pairs={{0,8},{8,0},{16,24},{24,16},{32,40},{40,32},{48,56},{56,48},{64,72... | collective-permute-start | bytes 393224 | tf_op jit(solution)/shard_map/ppermute | solution.py:89
  33.5 0.0 collective-permute-start.5
  33.5 0.0 collective-permute-done.6.refs_4_
  33.5 3.0 %collective-permute-start.8 = (f32[4,64,128]{2,1,0:T(8,128)S(1)}, f32[4,64,128]{2,1,0:T(8,128)S(1)}, u32[]{:S(2)}, u32[]{:S(2)}) collective-permute-start(f32[4,64,128]{2,1,0:T(8,128)S(1)} %collective-permute-done.6.refs_4_), channel_id=1, source_target_pairs={{0,8},{8,0},{16,24},{24,16},{32,40},{40,32},{48,56},{56,48},{64,72... | collective-permute-start | bytes 393224 | tf_op jit(solution)/shard_map/ppermute | solution.py:89
  36.4 0.0 collective-permute-done.7.refs_5_
  36.4 1.4 %collective-permute-start.9 = (f32[4,64,128]{2,1,0:T(8,128)S(1)}, f32[4,64,128]{2,1,0:T(8,128)S(1)}, u32[]{:S(2)}, u32[]{:S(2)}) collective-permute-start(f32[4,64,128]{2,1,0:T(8,128)S(1)} %collective-permute-done.7.refs_5_), channel_id=1, source_target_pairs={{0,8},{8,0},{16,24},{24,16},{32,40},{40,32},{48,56},{56,48},{64,72... | collective-permute-start | bytes 393224 | tf_op jit(solution)/shard_map/ppermute | solution.py:89
  37.8 0.0 all-to-all-done.all_ref
  37.8 0.0 copy-done.11
  37.9 0.0 copy-start
  37.9 0.0 copy-start.2
  37.9 0.0 copy-start.3
  37.9 0.0 copy-start.4
  37.9 2.3 %shard_map.186 = (f32[2,512,512]{2,1,0:T(8,128)S(1)}, bf16[2,2,256,512]{3,2,1,0:T(8,128)(2,1)S(1)}, f32[128,256]{1,0:T(8,128)S(1)}) custom-call(f32[8,2,64,256]{3,2,1,0:T(8,128)S(1)} %all-to-all-done.all_ref, f32[2,64,256]{2,1,0:T(8,128)S(1)} %copy-done.1, f32[1,256]{1,0:T(1,128)S(1)} %bitcast.13, f32[256,256]{1,0:T(8,128)S(1)} %copy-done.7, ...), custom_call_target="tpu_custom_call" | custom-call | flops 1610612736 | bytes 6291456 | tf_op jit(solution)/shard_map/pallas_call | solution.py:503
  40.3 0.0 collective-permute-done.4.refs_2_
  40.3 0.0 collective-permute-done.5.refs_3_
  40.3 0.0 collective-permute-done.8.refs_6_
  40.3 0.0 collective-permute-done.9.refs_7_
  40.3 0.1 broadcast_in_dim.23.refs_9_
  40.5 0.0 copy-start.5
  40.5 0.0 copy-start.6
  40.5 0.0 copy-start.12
  40.5 3.7 %shard_map.187 = (f32[2,64,256]{2,1,0:T(8,128)}, f32[4,8,128]{2,1,0:T(8,128)S(1)}, f32[8,40,128]{2,1,0:T(8,128)}) custom-call(s32[128]{0:T(128)S(1)} %copy-done.4, f32[4,64,128]{2,1,0:T(8,128)S(1)} %constant_dynamic-update-slice_fusion.refs_0_, f32[4,64,128]{2,1,0:T(8,128)S(1)} %collective-permute-done.3.refs_1_, ...), custom_call_target="tpu_custom_call" | custom-call | flops 805306368 | bytes 6291456 | tf_op jit(solution)/shard_map/pallas_call | solution.py:519
  44.2 7.0 %all-to-all-start.1 = ((f32[8,40,128]{2,1,0:T(8,128)}), f32[8,40,128]{2,1,0:T(8,128)S(1)}, u32[]{:S(2)}, u32[]{:S(2)}) async-start(f32[8,40,128]{2,1,0:T(8,128)} %get-tuple-element.32), calls=%async_computation.1 | async-start | bytes 327680 | tf_op jit(solution)/shard_map/all_to_all | solution.py:542
  51.2 6.0 %collective-permute-start.10 = (f32[4,8,128]{2,1,0:T(8,128)S(1)}, f32[4,8,128]{2,1,0:T(8,128)S(1)}, u32[]{:S(2)}, u32[]{:S(2)}) collective-permute-start(f32[4,8,128]{2,1,0:T(8,128)S(1)} %get-tuple-element.31), channel_id=1, source_target_pairs={{128,0},{64,1},{96,2},{32,3},{192,4},{0,5},{160,6},{224,7},{136,8}... | collective-permute-start | bytes 49160 | tf_op jit(solution)/shard_map/ppermute | solution.py:550
  57.2 2.6 %collective-permute-done.10.left_ref = f32[4,8,128]{2,1,0:T(8,128)S(1)} collective-permute-done((f32[4,8,128]{2,1,0:T(8,128)S(1)}, f32[4,8,128]{2,1,0:T(8,128)S(1)}, u32[]{:S(2)}, u32[]{:S(2)}) %collective-permute-start.10) | collective-permute-done | bytes 16416 | tf_op jit(solution)/shard_map/ppermute | solution.py:550
  59.8 0.0 all-to-all-done.1.refs_0_
  59.8 2.1 %collective-permute-start.12 = (f32[8,40,128]{2,1,0:T(8,128)S(1)}, f32[8,40,128]{2,1,0:T(8,128)S(1)}, u32[]{:S(2)}, u32[]{:S(2)}) collective-permute-start(f32[8,40,128]{2,1,0:T(8,128)S(1)} %all-to-all-done.1.refs_0_), channel_id=1, source_target_pairs={{0,16},{8,24},{16,0},{24,8},{32,48},{40,56},{48,32},{56,40},{64,80... | collective-permute-start | bytes 491528 | tf_op jit(solution)/shard_map/ppermute | solution.py:89
  61.8 0.7 shard_map.188
  62.6 9.3 %all-to-all-start.2 = ((f32[32,8,128]{2,1,0:T(8,128)}), f32[32,8,128]{2,1,0:T(8,128)S(1)}, u32[]{:S(2)}, u32[]{:S(2)}) async-start(f32[32,8,128]{2,1,0:T(8,128)} %bitcast.7), calls=%async_computation.2 | async-start | bytes 262144 | tf_op jit(solution)/shard_map/all_to_all | solution.py:559
  71.9 0.3 collective-permute-start.11
  72.2 7.4 %all-to-all-done.2.refs_4_ = f32[32,8,128]{2,1,0:T(8,128)S(1)} async-done(((f32[32,8,128]{2,1,0:T(8,128)}), f32[32,8,128]{2,1,0:T(8,128)S(1)}, u32[]{:S(2)}, u32[]{:S(2)}) %all-to-all-start.2) | async-done | bytes 131104 | tf_op jit(solution)/shard_map/all_to_all | solution.py:559
  79.6 0.0 collective-permute-done.12.refs_2_
  79.6 0.2 collective-permute-start.13
  79.8 0.1 dynamic_slice.7.rows_live_ref
  79.9 0.1 dynamic-slice_bitcast_fusion
  80.0 0.1 copy.25.refs_7_
  80.1 0.0 collective-permute-done.11.refs_1_
  80.1 0.9 %collective-permute-done.13.refs_3_ = f32[8,40,128]{2,1,0:T(8,128)S(1)} collective-permute-done((f32[8,40,128]{2,1,0:T(8,128)S(1)}, f32[8,40,128]{2,1,0:T(8,128)S(1)}, u32[]{:S(2)}, u32[]{:S(2)}) %collective-permute-start.13) | collective-permute-done | bytes 163872 | tf_op jit(solution)/shard_map/ppermute | solution.py:89
  81.0 0.0 copy-done.12
  81.0 4.8 %shard_map.189 = f32[16,64,128]{2,1,0:T(8,128)} custom-call(s32[64]{0:T(128)S(1)} %copy-done.12, f32[16]{0:T(128)S(1)} %dynamic_slice.7.rows_live_ref, f32[8,40,128]{2,1,0:T(8,128)S(1)} %all-to-all-done.1.refs_0_, f32[8,40,128]{2,1,0:T(8,128)S(1)} %collective-permute-done.11.refs_1_, f32[8,40,128]{2,1,0:T(8,128)S(1)} %collective-permute-done.12.refs_2_, ...), custom_call_target="tpu_custom_call" | custom-call | flops 1610612736 | bytes 4194304 | tf_op jit(solution)/shard_map/pallas_call | solution.py:568
  (24 shorter events, 0.1 us)
Async XLA Ops:
  0.6 37.2 %copy-start.1 = (f32[2,64,256]{2,1,0:T(8,128)S(1)}, f32[2,64,256]{2,1,0:T(8,128)}, u32[]{:S(2)}) copy-start(f32[2,64,256]{2,1,0:T(8,128)} %refs_12_.1) | copy-start | bytes 393220
  0.6 18.2 %copy-start.15 = (s32[2]{0:T(128)S(1)}, s32[2]{0:T(128)}, u32[]{:S(2)}) copy-start(s32[2]{0:T(128)} %param.22) | copy-start | bytes 28
  0.7 18.2 %copy-start.13 = (f32[256,32]{0,1:T(8,128)S(1)}, f32[256,32]{0,1:T(8,128)}, u32[]{:S(2)}) copy-start(f32[256,32]{0,1:T(8,128)} %param.33) | copy-start | bytes 98308
  0.7 18.3 %copy-start.14 = (s32[512]{0:T(512)S(1)}, s32[512]{0:T(512)}, u32[]{:S(2)}) copy-start(s32[512]{0:T(512)} %param.23) | copy-start | bytes 6148
  0.7 37.2 %copy-start.11 = (f32[256]{0:T(256)S(1)}, f32[256]{0:T(256)}, u32[]{:S(2)}) copy-start(f32[256]{0:T(256)} %param.24) | copy-start | bytes 3076
  0.7 37.2 %copy-start.7 = (f32[256,256]{1,0:T(8,128)S(1)}, f32[256,256]{1,0:T(8,128)}, u32[]{:S(2)}) copy-start(f32[256,256]{1,0:T(8,128)} %wq_ref.1) | copy-start | bytes 786436
  0.7 37.2 %copy-start.8 = (f32[256,256]{1,0:T(8,128)S(1)}, f32[256,256]{1,0:T(8,128)}, u32[]{:S(2)}) copy-start(f32[256,256]{1,0:T(8,128)} %wk_ref.1) | copy-start | bytes 786436
  0.7 37.2 %copy-start.9 = (f32[256,256]{1,0:T(8,128)S(1)}, f32[256,256]{1,0:T(8,128)}, u32[]{:S(2)}) copy-start(f32[256,256]{1,0:T(8,128)} %wv_ref.1) | copy-start | bytes 786436
  0.7 37.2 %copy-start.10 = (f32[256,256]{1,0:T(8,128)S(1)}, f32[256,256]{1,0:T(8,128)}, u32[]{:S(2)}) copy-start(f32[256,256]{1,0:T(8,128)} %wg_ref.1) | copy-start | bytes 786436
  3.6 15.4 %collective-permute-start = (f32[1,64,128]{2,1,0:T(8,128)}, f32[1,64,128]{2,1,0:T(8,128)S(1)}, u32[]{:S(2)}, u32[]{:S(2)}) collective-permute-start(f32[1,64,128]{2,1,0:T(8,128)} %get-tuple-element.25), channel_id=1, source_target_pairs={{0,96},{1,32},{2,64},{3,0},{4,160},{5,224},{6,128},{7,192},{8,104}... | collective-permute-start | bytes 98312 | tf_op jit(solution)/shard_map/ppermute | solution.py:490
  8.9 10.2 %collective-permute-start.1 = (f32[1,64,128]{2,1,0:T(8,128)}, f32[1,64,128]{2,1,0:T(8,128)S(1)}, u32[]{:S(2)}, u32[]{:S(2)}) collective-permute-start(f32[1,64,128]{2,1,0:T(8,128)} %get-tuple-element.25), channel_id=1, source_target_pairs={{0,128},{1,192},{2,160},{3,224},{4,64},{5,0},{6,96},{7,32},{8,136}... | collective-permute-start | bytes 98312 | tf_op jit(solution)/shard_map/ppermute | solution.py:490
  13.0 24.8 %all-to-all-start = ((f32[8,2,64,256]{3,2,1,0:T(8,128)}), f32[8,2,64,256]{3,2,1,0:T(8,128)S(1)}, u32[]{:S(2)}, u32[]{:S(2)}) async-start(f32[8,2,64,256]{3,2,1,0:T(8,128)} %get-tuple-element.26), calls=%async_computation | async-start | bytes 2097152 | tf_op jit(solution)/shard_map/all_to_all | solution.py:488
  19.1 4.1 %collective-permute-start.2 = (f32[2,64,128]{2,1,0:T(8,128)S(1)}, f32[2,64,128]{2,1,0:T(8,128)S(1)}, u32[]{:S(2)}, u32[]{:S(2)}) collective-permute-start(f32[2,64,128]{2,1,0:T(8,128)S(1)} %pad_maximum_fusion), channel_id=1, source_target_pairs={{0,64},{8,72},{16,80},{24,88},{32,96},{40,104},{48,112},{56,120},{... | collective-permute-start | bytes 196616 | tf_op jit(solution)/shard_map/ppermute | solution.py:89
  23.2 4.9 %collective-permute-start.3 = (f32[4,64,128]{2,1,0:T(8,128)S(1)}, f32[4,64,128]{2,1,0:T(8,128)S(1)}, u32[]{:S(2)}, u32[]{:S(2)}) collective-permute-start(f32[4,64,128]{2,1,0:T(8,128)S(1)} %constant_dynamic-update-slice_fusion.refs_0_), channel_id=1, source_target_pairs={{0,32},{8,40},{16,48},{24,56},{32,0},{40,8},{48,16},{56,24},{64,96... | collective-permute-start | bytes 393224 | tf_op jit(solution)/shard_map/ppermute | solution.py:89
  25.7 7.8 %collective-permute-start.6 = (f32[4,64,128]{2,1,0:T(8,128)S(1)}, f32[4,64,128]{2,1,0:T(8,128)S(1)}, u32[]{:S(2)}, u32[]{:S(2)}) collective-permute-start(f32[4,64,128]{2,1,0:T(8,128)S(1)} %constant_dynamic-update-slice_fusion.refs_0_), channel_id=1, source_target_pairs={{0,16},{8,24},{16,0},{24,8},{32,48},{40,56},{48,32},{56,40},{64,80... | collective-permute-start | bytes 393224 | tf_op jit(solution)/shard_map/ppermute | solution.py:89
  28.1 8.4 %collective-permute-start.7 = (f32[4,64,128]{2,1,0:T(8,128)S(1)}, f32[4,64,128]{2,1,0:T(8,128)S(1)}, u32[]{:S(2)}, u32[]{:S(2)}) collective-permute-start(f32[4,64,128]{2,1,0:T(8,128)S(1)} %collective-permute-done.3.refs_1_), channel_id=1, source_target_pairs={{0,16},{8,24},{16,0},{24,8},{32,48},{40,56},{48,32},{56,40},{64,80... | collective-permute-start | bytes 393224 | tf_op jit(solution)/shard_map/ppermute | solution.py:89
  29.2 11.0 %collective-permute-start.4 = (f32[4,64,128]{2,1,0:T(8,128)S(1)}, f32[4,64,128]{2,1,0:T(8,128)S(1)}, u32[]{:S(2)}, u32[]{:S(2)}) collective-permute-start(f32[4,64,128]{2,1,0:T(8,128)S(1)} %constant_dynamic-update-slice_fusion.refs_0_), channel_id=1, source_target_pairs={{0,8},{8,0},{16,24},{24,16},{32,40},{40,32},{48,56},{56,48},{64,72... | collective-permute-start | bytes 393224 | tf_op jit(solution)/shard_map/ppermute | solution.py:89
  33.5 6.8 %collective-permute-start.5 = (f32[4,64,128]{2,1,0:T(8,128)S(1)}, f32[4,64,128]{2,1,0:T(8,128)S(1)}, u32[]{:S(2)}, u32[]{:S(2)}) collective-permute-start(f32[4,64,128]{2,1,0:T(8,128)S(1)} %collective-permute-done.3.refs_1_), channel_id=1, source_target_pairs={{0,8},{8,0},{16,24},{24,16},{32,40},{40,32},{48,56},{56,48},{64,72... | collective-permute-start | bytes 393224 | tf_op jit(solution)/shard_map/ppermute | solution.py:89
  33.5 6.8 %collective-permute-start.8 = (f32[4,64,128]{2,1,0:T(8,128)S(1)}, f32[4,64,128]{2,1,0:T(8,128)S(1)}, u32[]{:S(2)}, u32[]{:S(2)}) collective-permute-start(f32[4,64,128]{2,1,0:T(8,128)S(1)} %collective-permute-done.6.refs_4_), channel_id=1, source_target_pairs={{0,8},{8,0},{16,24},{24,16},{32,40},{40,32},{48,56},{56,48},{64,72... | collective-permute-start | bytes 393224 | tf_op jit(solution)/shard_map/ppermute | solution.py:89
  36.4 3.8 %collective-permute-start.9 = (f32[4,64,128]{2,1,0:T(8,128)S(1)}, f32[4,64,128]{2,1,0:T(8,128)S(1)}, u32[]{:S(2)}, u32[]{:S(2)}) collective-permute-start(f32[4,64,128]{2,1,0:T(8,128)S(1)} %collective-permute-done.7.refs_5_), channel_id=1, source_target_pairs={{0,8},{8,0},{16,24},{24,16},{32,40},{40,32},{48,56},{56,48},{64,72... | collective-permute-start | bytes 393224 | tf_op jit(solution)/shard_map/ppermute | solution.py:89
  37.9 2.5 %copy-start = (f32[256,256]{1,0:T(8,128)S(1)}, f32[256,256]{1,0:T(8,128)}, u32[]{:S(2)}) copy-start(f32[256,256]{1,0:T(8,128)} %refs_13_.1) | copy-start | bytes 786436
  37.9 2.5 %copy-start.2 = (f32[256,32]{0,1:T(8,128)S(1)}, f32[256,32]{0,1:T(8,128)}, u32[]{:S(2)}) copy-start(f32[256,32]{0,1:T(8,128)} %param.34) | copy-start | bytes 98308
  37.9 2.5 %copy-start.3 = (f32[256]{0:T(256)S(1)}, f32[256]{0:T(256)}, u32[]{:S(2)}) copy-start(f32[256]{0:T(256)} %param.32) | copy-start | bytes 3076
  37.9 2.5 %copy-start.4 = (s32[128]{0:T(128)S(1)}, s32[128]{0:T(128)}, u32[]{:S(2)}) copy-start(s32[128]{0:T(128)} %constant.53.clone.spot_ref) | copy-start | bytes 1540
  40.5 40.5 %copy-start.5 = (f32[16,64,128]{2,1,0:T(8,128)S(1)}, f32[16,64,128]{2,1,0:T(8,128)}, u32[]{:S(2)}) copy-start(f32[16,64,128]{2,1,0:T(8,128)} %refs_6_.1) | copy-start | bytes 1572868
  40.5 40.5 %copy-start.6 = (f32[1024,128]{1,0:T(8,128)S(1)}, f32[1024,128]{1,0:T(8,128)}, u32[]{:S(2)}) copy-start(f32[1024,128]{1,0:T(8,128)} %refs_5_.1) | copy-start | bytes 1572868
  40.5 40.5 %copy-start.12 = (s32[64]{0:T(128)S(1)}, s32[64]{0:T(128)}, u32[]{:S(2)}) copy-start(s32[64]{0:T(128)} %constant.54.clone.once_ref) | copy-start | bytes 772
  44.2 15.6 %all-to-all-start.1 = ((f32[8,40,128]{2,1,0:T(8,128)}), f32[8,40,128]{2,1,0:T(8,128)S(1)}, u32[]{:S(2)}, u32[]{:S(2)}) async-start(f32[8,40,128]{2,1,0:T(8,128)} %get-tuple-element.32), calls=%async_computation.1 | async-start | bytes 327680 | tf_op jit(solution)/shard_map/all_to_all | solution.py:542
  51.2 8.6 %collective-permute-start.10 = (f32[4,8,128]{2,1,0:T(8,128)S(1)}, f32[4,8,128]{2,1,0:T(8,128)S(1)}, u32[]{:S(2)}, u32[]{:S(2)}) collective-permute-start(f32[4,8,128]{2,1,0:T(8,128)S(1)} %get-tuple-element.31), channel_id=1, source_target_pairs={{128,0},{64,1},{96,2},{32,3},{192,4},{0,5},{160,6},{224,7},{136,8}... | collective-permute-start | bytes 49160 | tf_op jit(solution)/shard_map/ppermute | solution.py:550
  59.8 19.8 %collective-permute-start.12 = (f32[8,40,128]{2,1,0:T(8,128)S(1)}, f32[8,40,128]{2,1,0:T(8,128)S(1)}, u32[]{:S(2)}, u32[]{:S(2)}) collective-permute-start(f32[8,40,128]{2,1,0:T(8,128)S(1)} %all-to-all-done.1.refs_0_), channel_id=1, source_target_pairs={{0,16},{8,24},{16,0},{24,8},{32,48},{40,56},{48,32},{56,40},{64,80... | collective-permute-start | bytes 491528 | tf_op jit(solution)/shard_map/ppermute | solution.py:89
  62.6 17.0 %all-to-all-start.2 = ((f32[32,8,128]{2,1,0:T(8,128)}), f32[32,8,128]{2,1,0:T(8,128)S(1)}, u32[]{:S(2)}, u32[]{:S(2)}) async-start(f32[32,8,128]{2,1,0:T(8,128)} %bitcast.7), calls=%async_computation.2 | async-start | bytes 262144 | tf_op jit(solution)/shard_map/all_to_all | solution.py:559
  71.9 8.2 %collective-permute-start.11 = (f32[8,40,128]{2,1,0:T(8,128)S(1)}, f32[8,40,128]{2,1,0:T(8,128)S(1)}, u32[]{:S(2)}, u32[]{:S(2)}) collective-permute-start(f32[8,40,128]{2,1,0:T(8,128)S(1)} %all-to-all-done.1.refs_0_), channel_id=1, source_target_pairs={{0,8},{8,0},{16,24},{24,16},{32,40},{40,32},{48,56},{56,48},{64,72... | collective-permute-start | bytes 491528 | tf_op jit(solution)/shard_map/ppermute | solution.py:89
  79.6 1.4 %collective-permute-start.13 = (f32[8,40,128]{2,1,0:T(8,128)S(1)}, f32[8,40,128]{2,1,0:T(8,128)S(1)}, u32[]{:S(2)}, u32[]{:S(2)}) collective-permute-start(f32[8,40,128]{2,1,0:T(8,128)S(1)} %collective-permute-done.12.refs_2_), channel_id=1, source_target_pairs={{0,8},{8,0},{16,24},{24,16},{32,40},{40,32},{48,56},{56,48},{64,72... | collective-permute-start | bytes 491528 | tf_op jit(solution)/shard_map/ppermute | solution.py:89

commit v4 on v3

--- a/solution.py
+++ b/solution.py
@@ -53,6 +53,8 @@
             if best is None or cost < best[0]:
                 best = cost, low, high, first, second
         _, low, high, first, second = best
+        if max(f[0] for f in first) < max(f[0] for f in second):
+            first, second = second, first
         for k, fits in enumerate((first, second)):
             for group, found in zip((low, high), fits):
                 for h, b in zip(group, found[2]):
@@ -362,8 +364,10 @@
         )
     left = jnp.concatenate(left_rows, axis=0)
     high = left.astype(bf16).astype(f32)
-    low = left - high
-    left_ref[...] = jnp.transpose(jnp.concatenate([high, high, low, jnp.zeros_like(low)], axis=0)).astype(bf16)
+    halves = jnp.transpose(jnp.concatenate([high, left - high], axis=0))
+    lane = lax.broadcasted_iota(jnp.int32, (512, 128), 1) < 64
+    left_ref[:, 0:128] = halves.astype(bf16)
+    left_ref[:, 128:256] = jnp.where(lane, halves, 0.0).astype(bf16)
     lane = lax.broadcasted_iota(jnp.int32, (32, 128), 1) < 64
     for d in range(16):
         even = right_in_ref[pl.ds(2 * d, 32, stride=40), :]
@@ -378,8 +382,8 @@
         high, low = split(both)
         columns = pl.ds(128 * d, 128)
         right_ref[0:64, columns] = high
-        right_ref[64:128, columns] = low
-        right_ref[128:192, columns] = high
+        right_ref[64:128, columns] = high
+        right_ref[128:192, columns] = low
         right_ref[192:256, columns] = jnp.zeros((64, 128), bf16)
     columns = [
         jnp.concatenate(

time: 86.1 us -> 84.9 us (0.986)
  starting transfers between devices: 54.8 us -> 52.1 us
  waiting for transfers between devices: 14.7 us -> 16.4 us
    ppermute x11, waiting for transfers between devices: 4.71 us -> 6.42 us  [from_neighbour(): return lax.ppermute(v, 'row', [(r, r ^ bit) for r in range(Z * A)])]
    ppermute x11, starting transfers between devices: 17.3 us -> 15.6 us  [from_neighbour(): return lax.ppermute(v, 'row', [(r, r ^ bit) for r in range(Z * A)])]
    all_to_all x1, starting transfers between devices: 7.03 us -> 5.98 us  [body(): lax.all_to_all(right, 'row', 0, 0, tiled=True, axis_index_groups=[[4 * z...]
  transfers between devices with their start and end apart: 17 -> 17, of which waited for: 5 -> 6; matrix products, arithmetic and copies ran while one was open for 1% -> 1% of each run, Pallas kernels for 4% -> 4%
where the time goes in v4:
time: 84.9 us; the launch traced here: 84.6 us
  starting transfers between devices  52.1 us (61%)
  waiting for transfers between devices  16.4 us (19%)
  Pallas kernels  14.3 us (17%)
  between operations  0.99 us (1%)
    ppermute x11, starting transfers between devices, from_neighbour(): return lax.ppermute(v, 'row', [(r, r ^ bit) for r in range(Z * A)])  15.6 us
    all_to_all x1, starting transfers between devices, body(): lax.all_to_all(spread.reshape(A * H, 8, 128), both, 0, 0, tiled=True, axi...  9.34 us
    all_to_all x1, waiting for transfers between devices, body(): lax.all_to_all(spread.reshape(A * H, 8, 128), both, 0, 0, tiled=True, axi...  7.38 us
    ppermute x11, waiting for transfers between devices, from_neighbour(): return lax.ppermute(v, 'row', [(r, r ^ bit) for r in range(Z * A)])  6.42 us
    ppermute x1, starting transfers between devices, body(): left = lax.ppermute(left, both, [(d, s) for s, d in moves(ONCE)])  5.98 us
    all_to_all x1, starting transfers between devices, body(): lax.all_to_all(right, 'row', 0, 0, tiled=True, axis_index_groups=[[4 * z...  5.98 us
    all_to_all x1, starting transfers between devices, body(): everyone = lax.all_to_all(copies, 'head', 0, 0, tiled=True)  5.84 us
    ppermute x1, starting transfers between devices, body(): lax.ppermute(block, both, moves(TWICE[:, 0]))  5.25 us
  transfers between devices with their start and end apart: 17, of which 6 were waited for; matrix products, arithmetic and copies ran while one was open for 1% of the time, Pallas kernels for 4%

profile of v4, /device:TPU:1, one launch (start us, length us, event | category | flops | bytes accessed | tf_op | source)
XLA Modules:
  0.0 84.6 jit_solution(5388449488467610158)
XLA Ops:
  0.6 0.0 copy-start.1
  0.6 0.0 copy-start.15
  0.7 0.0 copy-start.13
  0.7 0.0 copy-start.14
  0.7 2.9 %shard_map.185 = (f32[1,64,128]{2,1,0:T(8,128)}, f32[8,2,64,256]{3,2,1,0:T(8,128)}) custom-call(f32[16,64,128]{2,1,0:T(8,128)} %refs_6_.1, f32[1,128]{1,0:T(1,128)} %bitcast.16, f32[8,128]{1,0:T(8,128)} %bitcast.15, f32[2,64,256]{2,1,0:T(8,128)} %refs_12_.1), custom_call_target="tpu_custom_call" | custom-call | flops 201326592 | bytes 600000 | tf_op jit(solution)/shard_map/pallas_call | solution.py:476
  3.6 5.2 %collective-permute-start = (f32[1,64,128]{2,1,0:T(8,128)}, f32[1,64,128]{2,1,0:T(8,128)S(1)}, u32[]{:S(2)}, u32[]{:S(2)}) collective-permute-start(f32[1,64,128]{2,1,0:T(8,128)} %get-tuple-element.25), channel_id=1, source_target_pairs={{0,96},{1,32},{2,64},{3,0},{4,160},{5,224},{6,128},{7,192},{8,104}... | collective-permute-start | bytes 98312 | tf_op jit(solution)/shard_map/ppermute | solution.py:494
  8.9 4.1 %collective-permute-start.1 = (f32[1,64,128]{2,1,0:T(8,128)}, f32[1,64,128]{2,1,0:T(8,128)S(1)}, u32[]{:S(2)}, u32[]{:S(2)}) collective-permute-start(f32[1,64,128]{2,1,0:T(8,128)} %get-tuple-element.25), channel_id=1, source_target_pairs={{0,128},{1,192},{2,160},{3,224},{4,64},{5,0},{6,96},{7,32},{8,136}... | collective-permute-start | bytes 98312 | tf_op jit(solution)/shard_map/ppermute | solution.py:494
  13.0 5.8 %all-to-all-start = ((f32[8,2,64,256]{3,2,1,0:T(8,128)}), f32[8,2,64,256]{3,2,1,0:T(8,128)S(1)}, u32[]{:S(2)}, u32[]{:S(2)}) async-start(f32[8,2,64,256]{3,2,1,0:T(8,128)} %get-tuple-element.26), calls=%async_computation | async-start | bytes 2097152 | tf_op jit(solution)/shard_map/all_to_all | solution.py:492
  18.9 0.1 copy.23.refs_15_
  19.0 0.0 copy-done.14
  19.0 0.1 dynamic_slice.6
  19.1 0.0 collective-permute-done
  19.1 0.0 collective-permute-done.1
  19.1 1.5 %collective-permute-start.2 = (f32[2,64,128]{2,1,0:T(8,128)S(1)}, f32[2,64,128]{2,1,0:T(8,128)S(1)}, u32[]{:S(2)}, u32[]{:S(2)}) collective-permute-start(f32[2,64,128]{2,1,0:T(8,128)S(1)} %pad_maximum_fusion), channel_id=1, source_target_pairs={{0,64},{8,72},{16,80},{24,88},{32,96},{40,104},{48,112},{56,120},{... | collective-permute-start | bytes 196616 | tf_op jit(solution)/shard_map/ppermute | solution.py:91
  20.6 2.6 %collective-permute-done.2 = f32[2,64,128]{2,1,0:T(8,128)S(1)} collective-permute-done((f32[2,64,128]{2,1,0:T(8,128)S(1)}, f32[2,64,128]{2,1,0:T(8,128)S(1)}, u32[]{:S(2)}, u32[]{:S(2)}) %collective-permute-start.2) | collective-permute-done | bytes 65568 | tf_op jit(solution)/shard_map/ppermute | solution.py:91
  23.2 2.2 %collective-permute-start.3 = (f32[4,64,128]{2,1,0:T(8,128)S(1)}, f32[4,64,128]{2,1,0:T(8,128)S(1)}, u32[]{:S(2)}, u32[]{:S(2)}) collective-permute-start(f32[4,64,128]{2,1,0:T(8,128)S(1)} %constant_dynamic-update-slice_fusion.refs_0_), channel_id=1, source_target_pairs={{0,32},{8,40},{16,48},{24,56},{32,0},{40,8},{48,16},{56,24},{64,96... | collective-permute-start | bytes 393224 | tf_op jit(solution)/shard_map/ppermute | solution.py:91
  25.4 0.1 broadcast_multiply_fusion
  25.4 0.1 mul.43.refs_17_
  25.6 0.4 collective-permute-start.6
  26.0 2.0 %collective-permute-done.3.refs_1_ = f32[4,64,128]{2,1,0:T(8,128)S(1)} collective-permute-done((f32[4,64,128]{2,1,0:T(8,128)S(1)}, f32[4,64,128]{2,1,0:T(8,128)S(1)}, u32[]{:S(2)}, u32[]{:S(2)}) %collective-permute-start.3) | collective-permute-done | bytes 131104 | tf_op jit(solution)/shard_map/ppermute | solution.py:91
  28.0 0.3 collective-permute-start.7
  28.3 3.6 %collective-permute-start.4 = (f32[4,64,128]{2,1,0:T(8,128)S(1)}, f32[4,64,128]{2,1,0:T(8,128)S(1)}, u32[]{:S(2)}, u32[]{:S(2)}) collective-permute-start(f32[4,64,128]{2,1,0:T(8,128)S(1)} %constant_dynamic-update-slice_fusion.refs_0_), channel_id=1, source_target_pairs={{0,8},{8,0},{16,24},{24,16},{32,40},{40,32},{48,56},{56,48},{64,72... | collective-permute-start | bytes 393224 | tf_op jit(solution)/shard_map/ppermute | solution.py:91
  32.0 0.0 collective-permute-start.5
  32.0 0.9 %collective-permute-done.6.refs_4_ = f32[4,64,128]{2,1,0:T(8,128)S(1)} collective-permute-done((f32[4,64,128]{2,1,0:T(8,128)S(1)}, f32[4,64,128]{2,1,0:T(8,128)S(1)}, u32[]{:S(2)}, u32[]{:S(2)}) %collective-permute-start.6) | collective-permute-done | bytes 131104 | tf_op jit(solution)/shard_map/ppermute | solution.py:91
  32.9 3.6 %collective-permute-start.8 = (f32[4,64,128]{2,1,0:T(8,128)S(1)}, f32[4,64,128]{2,1,0:T(8,128)S(1)}, u32[]{:S(2)}, u32[]{:S(2)}) collective-permute-start(f32[4,64,128]{2,1,0:T(8,128)S(1)} %collective-permute-done.6.refs_4_), channel_id=1, source_target_pairs={{0,8},{8,0},{16,24},{24,16},{32,40},{40,32},{48,56},{56,48},{64,72... | collective-permute-start | bytes 393224 | tf_op jit(solution)/shard_map/ppermute | solution.py:91
  36.4 0.0 collective-permute-done.7.refs_5_
  36.4 1.4 %collective-permute-start.9 = (f32[4,64,128]{2,1,0:T(8,128)S(1)}, f32[4,64,128]{2,1,0:T(8,128)S(1)}, u32[]{:S(2)}, u32[]{:S(2)}) collective-permute-start(f32[4,64,128]{2,1,0:T(8,128)S(1)} %collective-permute-done.7.refs_5_), channel_id=1, source_target_pairs={{0,8},{8,0},{16,24},{24,16},{32,40},{40,32},{48,56},{56,48},{64,72... | collective-permute-start | bytes 393224 | tf_op jit(solution)/shard_map/ppermute | solution.py:91
  37.8 0.0 all-to-all-done.all_ref
  37.9 0.0 copy-done.7
  37.9 0.0 copy-done.8
  37.9 0.0 copy-done.9
  37.9 0.0 copy-done.10
  37.9 0.0 copy-start
  37.9 0.0 copy-start.2
  37.9 0.0 copy-start.3
  37.9 0.0 copy-start.4
  37.9 2.3 %shard_map.186 = (f32[2,512,512]{2,1,0:T(8,128)S(1)}, bf16[2,2,256,512]{3,2,1,0:T(8,128)(2,1)S(1)}, f32[128,256]{1,0:T(8,128)S(1)}) custom-call(f32[8,2,64,256]{3,2,1,0:T(8,128)S(1)} %all-to-all-done.all_ref, f32[2,64,256]{2,1,0:T(8,128)S(1)} %copy-done.1, f32[1,256]{1,0:T(1,128)S(1)} %bitcast.13, f32[256,256]{1,0:T(8,128)S(1)} %copy-done.7, ...), custom_call_target="tpu_custom_call" | custom-call | flops 1610612736 | bytes 6291456 | tf_op jit(solution)/shard_map/pallas_call | solution.py:507
  40.3 0.0 collective-permute-done.4.refs_2_
  40.3 0.0 collective-permute-done.5.refs_3_
  40.3 0.0 collective-permute-done.8.refs_6_
  40.3 0.0 collective-permute-done.9.refs_7_
  40.3 0.1 broadcast_in_dim.23.refs_9_
  40.5 0.0 copy-start.5
  40.5 0.0 copy-start.6
  40.5 0.0 copy-start.12
  40.5 3.7 %shard_map.187 = (f32[2,64,256]{2,1,0:T(8,128)}, f32[4,8,128]{2,1,0:T(8,128)S(1)}, f32[8,40,128]{2,1,0:T(8,128)}) custom-call(s32[128]{0:T(128)S(1)} %copy-done.4, f32[4,64,128]{2,1,0:T(8,128)S(1)} %constant_dynamic-update-slice_fusion.refs_0_, f32[4,64,128]{2,1,0:T(8,128)S(1)} %collective-permute-done.3.refs_1_, ...), custom_call_target="tpu_custom_call" | custom-call | flops 805306368 | bytes 6291456 | tf_op jit(solution)/shard_map/pallas_call | solution.py:523
  44.2 6.0 %all-to-all-start.1 = ((f32[8,40,128]{2,1,0:T(8,128)}), f32[8,40,128]{2,1,0:T(8,128)S(1)}, u32[]{:S(2)}, u32[]{:S(2)}) async-start(f32[8,40,128]{2,1,0:T(8,128)} %get-tuple-element.32), calls=%async_computation.1 | async-start | bytes 327680 | tf_op jit(solution)/shard_map/all_to_all | solution.py:546
  50.2 6.0 %collective-permute-start.10 = (f32[4,8,128]{2,1,0:T(8,128)S(1)}, f32[4,8,128]{2,1,0:T(8,128)S(1)}, u32[]{:S(2)}, u32[]{:S(2)}) collective-permute-start(f32[4,8,128]{2,1,0:T(8,128)S(1)} %get-tuple-element.31), channel_id=1, source_target_pairs={{128,0},{64,1},{96,2},{32,3},{192,4},{0,5},{160,6},{224,7},{136,8}... | collective-permute-start | bytes 49160 | tf_op jit(solution)/shard_map/ppermute | solution.py:554
  56.1 2.6 %collective-permute-done.10.left_ref = f32[4,8,128]{2,1,0:T(8,128)S(1)} collective-permute-done((f32[4,8,128]{2,1,0:T(8,128)S(1)}, f32[4,8,128]{2,1,0:T(8,128)S(1)}, u32[]{:S(2)}, u32[]{:S(2)}) %collective-permute-start.10) | collective-permute-done | bytes 16416 | tf_op jit(solution)/shard_map/ppermute | solution.py:554
  58.7 0.0 all-to-all-done.1.refs_0_
  58.7 2.1 %collective-permute-start.12 = (f32[8,40,128]{2,1,0:T(8,128)S(1)}, f32[8,40,128]{2,1,0:T(8,128)S(1)}, u32[]{:S(2)}, u32[]{:S(2)}) collective-permute-start(f32[8,40,128]{2,1,0:T(8,128)S(1)} %all-to-all-done.1.refs_0_), channel_id=1, source_target_pairs={{0,16},{8,24},{16,0},{24,8},{32,48},{40,56},{48,32},{56,40},{64,80... | collective-permute-start | bytes 491528 | tf_op jit(solution)/shard_map/ppermute | solution.py:91
  60.8 0.7 shard_map.188
  61.5 9.3 %all-to-all-start.2 = ((f32[32,8,128]{2,1,0:T(8,128)}), f32[32,8,128]{2,1,0:T(8,128)S(1)}, u32[]{:S(2)}, u32[]{:S(2)}) async-start(f32[32,8,128]{2,1,0:T(8,128)} %bitcast.7), calls=%async_computation.2 | async-start | bytes 262144 | tf_op jit(solution)/shard_map/all_to_all | solution.py:563
  70.9 0.3 collective-permute-start.11
  71.2 7.4 %all-to-all-done.2.refs_4_ = f32[32,8,128]{2,1,0:T(8,128)S(1)} async-done(((f32[32,8,128]{2,1,0:T(8,128)}), f32[32,8,128]{2,1,0:T(8,128)S(1)}, u32[]{:S(2)}, u32[]{:S(2)}) %all-to-all-start.2) | async-done | bytes 131104 | tf_op jit(solution)/shard_map/all_to_all | solution.py:563
  78.5 0.0 collective-permute-done.12.refs_2_
  78.5 0.2 collective-permute-start.13
  78.8 0.1 dynamic_slice.7.rows_live_ref
  78.9 0.1 dynamic-slice_bitcast_fusion
  78.9 0.1 copy.25.refs_7_
  79.0 0.0 collective-permute-done.11.refs_1_
  79.0 0.9 %collective-permute-done.13.refs_3_ = f32[8,40,128]{2,1,0:T(8,128)S(1)} collective-permute-done((f32[8,40,128]{2,1,0:T(8,128)S(1)}, f32[8,40,128]{2,1,0:T(8,128)S(1)}, u32[]{:S(2)}, u32[]{:S(2)}) %collective-permute-start.13) | collective-permute-done | bytes 163872 | tf_op jit(solution)/shard_map/ppermute | solution.py:91
  79.9 0.0 copy-done.6
  80.0 4.7 %shard_map.189 = f32[16,64,128]{2,1,0:T(8,128)} custom-call(s32[64]{0:T(128)S(1)} %copy-done.12, f32[16]{0:T(128)S(1)} %dynamic_slice.7.rows_live_ref, f32[8,40,128]{2,1,0:T(8,128)S(1)} %all-to-all-done.1.refs_0_, f32[8,40,128]{2,1,0:T(8,128)S(1)} %collective-permute-done.11.refs_1_, f32[8,40,128]{2,1,0:T(8,128)S(1)} %collective-permute-done.12.refs_2_, ...), custom_call_target="tpu_custom_call" | custom-call | flops 1610612736 | bytes 4194304 | tf_op jit(solution)/shard_map/pallas_call | solution.py:572
  (24 shorter events, 0.1 us)
Async XLA Ops:
  0.6 37.2 %copy-start.1 = (f32[2,64,256]{2,1,0:T(8,128)S(1)}, f32[2,64,256]{2,1,0:T(8,128)}, u32[]{:S(2)}) copy-start(f32[2,64,256]{2,1,0:T(8,128)} %refs_12_.1) | copy-start | bytes 393220
  0.6 18.2 %copy-start.15 = (s32[2]{0:T(128)S(1)}, s32[2]{0:T(128)}, u32[]{:S(2)}) copy-start(s32[2]{0:T(128)} %param.22) | copy-start | bytes 28
  0.7 18.2 %copy-start.13 = (f32[256,32]{0,1:T(8,128)S(1)}, f32[256,32]{0,1:T(8,128)}, u32[]{:S(2)}) copy-start(f32[256,32]{0,1:T(8,128)} %param.33) | copy-start | bytes 98308
  0.7 18.3 %copy-start.14 = (s32[512]{0:T(512)S(1)}, s32[512]{0:T(512)}, u32[]{:S(2)}) copy-start(s32[512]{0:T(512)} %param.23) | copy-start | bytes 6148
  0.7 37.2 %copy-start.11 = (f32[256]{0:T(256)S(1)}, f32[256]{0:T(256)}, u32[]{:S(2)}) copy-start(f32[256]{0:T(256)} %param.24) | copy-start | bytes 3076
  0.7 37.2 %copy-start.7 = (f32[256,256]{1,0:T(8,128)S(1)}, f32[256,256]{1,0:T(8,128)}, u32[]{:S(2)}) copy-start(f32[256,256]{1,0:T(8,128)} %wq_ref.1) | copy-start | bytes 786436
  0.7 37.2 %copy-start.8 = (f32[256,256]{1,0:T(8,128)S(1)}, f32[256,256]{1,0:T(8,128)}, u32[]{:S(2)}) copy-start(f32[256,256]{1,0:T(8,128)} %wk_ref.1) | copy-start | bytes 786436
  0.7 37.2 %copy-start.9 = (f32[256,256]{1,0:T(8,128)S(1)}, f32[256,256]{1,0:T(8,128)}, u32[]{:S(2)}) copy-start(f32[256,256]{1,0:T(8,128)} %wv_ref.1) | copy-start | bytes 786436
  0.7 37.2 %copy-start.10 = (f32[256,256]{1,0:T(8,128)S(1)}, f32[256,256]{1,0:T(8,128)}, u32[]{:S(2)}) copy-start(f32[256,256]{1,0:T(8,128)} %wg_ref.1) | copy-start | bytes 786436
  3.6 15.4 %collective-permute-start = (f32[1,64,128]{2,1,0:T(8,128)}, f32[1,64,128]{2,1,0:T(8,128)S(1)}, u32[]{:S(2)}, u32[]{:S(2)}) collective-permute-start(f32[1,64,128]{2,1,0:T(8,128)} %get-tuple-element.25), channel_id=1, source_target_pairs={{0,96},{1,32},{2,64},{3,0},{4,160},{5,224},{6,128},{7,192},{8,104}... | collective-permute-start | bytes 98312 | tf_op jit(solution)/shard_map/ppermute | solution.py:494
  8.9 10.2 %collective-permute-start.1 = (f32[1,64,128]{2,1,0:T(8,128)}, f32[1,64,128]{2,1,0:T(8,128)S(1)}, u32[]{:S(2)}, u32[]{:S(2)}) collective-permute-start(f32[1,64,128]{2,1,0:T(8,128)} %get-tuple-element.25), channel_id=1, source_target_pairs={{0,128},{1,192},{2,160},{3,224},{4,64},{5,0},{6,96},{7,32},{8,136}... | collective-permute-start | bytes 98312 | tf_op jit(solution)/shard_map/ppermute | solution.py:494
  13.0 24.8 %all-to-all-start = ((f32[8,2,64,256]{3,2,1,0:T(8,128)}), f32[8,2,64,256]{3,2,1,0:T(8,128)S(1)}, u32[]{:S(2)}, u32[]{:S(2)}) async-start(f32[8,2,64,256]{3,2,1,0:T(8,128)} %get-tuple-element.26), calls=%async_computation | async-start | bytes 2097152 | tf_op jit(solution)/shard_map/all_to_all | solution.py:492
  19.1 4.1 %collective-permute-start.2 = (f32[2,64,128]{2,1,0:T(8,128)S(1)}, f32[2,64,128]{2,1,0:T(8,128)S(1)}, u32[]{:S(2)}, u32[]{:S(2)}) collective-permute-start(f32[2,64,128]{2,1,0:T(8,128)S(1)} %pad_maximum_fusion), channel_id=1, source_target_pairs={{0,64},{8,72},{16,80},{24,88},{32,96},{40,104},{48,112},{56,120},{... | collective-permute-start | bytes 196616 | tf_op jit(solution)/shard_map/ppermute | solution.py:91
  23.2 4.8 %collective-permute-start.3 = (f32[4,64,128]{2,1,0:T(8,128)S(1)}, f32[4,64,128]{2,1,0:T(8,128)S(1)}, u32[]{:S(2)}, u32[]{:S(2)}) collective-permute-start(f32[4,64,128]{2,1,0:T(8,128)S(1)} %constant_dynamic-update-slice_fusion.refs_0_), channel_id=1, source_target_pairs={{0,32},{8,40},{16,48},{24,56},{32,0},{40,8},{48,16},{56,24},{64,96... | collective-permute-start | bytes 393224 | tf_op jit(solution)/shard_map/ppermute | solution.py:91
  25.6 7.3 %collective-permute-start.6 = (f32[4,64,128]{2,1,0:T(8,128)S(1)}, f32[4,64,128]{2,1,0:T(8,128)S(1)}, u32[]{:S(2)}, u32[]{:S(2)}) collective-permute-start(f32[4,64,128]{2,1,0:T(8,128)S(1)} %constant_dynamic-update-slice_fusion.refs_0_), channel_id=1, source_target_pairs={{0,16},{8,24},{16,0},{24,8},{32,48},{40,56},{48,32},{56,40},{64,80... | collective-permute-start | bytes 393224 | tf_op jit(solution)/shard_map/ppermute | solution.py:91
  28.0 8.4 %collective-permute-start.7 = (f32[4,64,128]{2,1,0:T(8,128)S(1)}, f32[4,64,128]{2,1,0:T(8,128)S(1)}, u32[]{:S(2)}, u32[]{:S(2)}) collective-permute-start(f32[4,64,128]{2,1,0:T(8,128)S(1)} %collective-permute-done.3.refs_1_), channel_id=1, source_target_pairs={{0,16},{8,24},{16,0},{24,8},{32,48},{40,56},{48,32},{56,40},{64,80... | collective-permute-start | bytes 393224 | tf_op jit(solution)/shard_map/ppermute | solution.py:91
  28.3 11.9 %collective-permute-start.4 = (f32[4,64,128]{2,1,0:T(8,128)S(1)}, f32[4,64,128]{2,1,0:T(8,128)S(1)}, u32[]{:S(2)}, u32[]{:S(2)}) collective-permute-start(f32[4,64,128]{2,1,0:T(8,128)S(1)} %constant_dynamic-update-slice_fusion.refs_0_), channel_id=1, source_target_pairs={{0,8},{8,0},{16,24},{24,16},{32,40},{40,32},{48,56},{56,48},{64,72... | collective-permute-start | bytes 393224 | tf_op jit(solution)/shard_map/ppermute | solution.py:91
  32.0 8.3 %collective-permute-start.5 = (f32[4,64,128]{2,1,0:T(8,128)S(1)}, f32[4,64,128]{2,1,0:T(8,128)S(1)}, u32[]{:S(2)}, u32[]{:S(2)}) collective-permute-start(f32[4,64,128]{2,1,0:T(8,128)S(1)} %collective-permute-done.3.refs_1_), channel_id=1, source_target_pairs={{0,8},{8,0},{16,24},{24,16},{32,40},{40,32},{48,56},{56,48},{64,72... | collective-permute-start | bytes 393224 | tf_op jit(solution)/shard_map/ppermute | solution.py:91
  32.9 7.4 %collective-permute-start.8 = (f32[4,64,128]{2,1,0:T(8,128)S(1)}, f32[4,64,128]{2,1,0:T(8,128)S(1)}, u32[]{:S(2)}, u32[]{:S(2)}) collective-permute-start(f32[4,64,128]{2,1,0:T(8,128)S(1)} %collective-permute-done.6.refs_4_), channel_id=1, source_target_pairs={{0,8},{8,0},{16,24},{24,16},{32,40},{40,32},{48,56},{56,48},{64,72... | collective-permute-start | bytes 393224 | tf_op jit(solution)/shard_map/ppermute | solution.py:91
  36.4 3.8 %collective-permute-start.9 = (f32[4,64,128]{2,1,0:T(8,128)S(1)}, f32[4,64,128]{2,1,0:T(8,128)S(1)}, u32[]{:S(2)}, u32[]{:S(2)}) collective-permute-start(f32[4,64,128]{2,1,0:T(8,128)S(1)} %collective-permute-done.7.refs_5_), channel_id=1, source_target_pairs={{0,8},{8,0},{16,24},{24,16},{32,40},{40,32},{48,56},{56,48},{64,72... | collective-permute-start | bytes 393224 | tf_op jit(solution)/shard_map/ppermute | solution.py:91
  37.9 2.5 %copy-start = (f32[256,256]{1,0:T(8,128)S(1)}, f32[256,256]{1,0:T(8,128)}, u32[]{:S(2)}) copy-start(f32[256,256]{1,0:T(8,128)} %refs_13_.1) | copy-start | bytes 786436
  37.9 2.5 %copy-start.2 = (f32[256,32]{0,1:T(8,128)S(1)}, f32[256,32]{0,1:T(8,128)}, u32[]{:S(2)}) copy-start(f32[256,32]{0,1:T(8,128)} %param.34) | copy-start | bytes 98308
  37.9 2.5 %copy-start.3 = (f32[256]{0:T(256)S(1)}, f32[256]{0:T(256)}, u32[]{:S(2)}) copy-start(f32[256]{0:T(256)} %param.32) | copy-start | bytes 3076
  37.9 2.5 %copy-start.4 = (s32[128]{0:T(128)S(1)}, s32[128]{0:T(128)}, u32[]{:S(2)}) copy-start(s32[128]{0:T(128)} %constant.53.clone.spot_ref) | copy-start | bytes 1540
  40.5 39.5 %copy-start.5 = (f32[16,64,128]{2,1,0:T(8,128)S(1)}, f32[16,64,128]{2,1,0:T(8,128)}, u32[]{:S(2)}) copy-start(f32[16,64,128]{2,1,0:T(8,128)} %refs_6_.1) | copy-start | bytes 1572868
  40.5 39.5 %copy-start.6 = (f32[1024,128]{1,0:T(8,128)S(1)}, f32[1024,128]{1,0:T(8,128)}, u32[]{:S(2)}) copy-start(f32[1024,128]{1,0:T(8,128)} %refs_5_.1) | copy-start | bytes 1572868
  40.5 39.5 %copy-start.12 = (s32[64]{0:T(128)S(1)}, s32[64]{0:T(128)}, u32[]{:S(2)}) copy-start(s32[64]{0:T(128)} %constant.54.clone.once_ref) | copy-start | bytes 772
  44.2 14.5 %all-to-all-start.1 = ((f32[8,40,128]{2,1,0:T(8,128)}), f32[8,40,128]{2,1,0:T(8,128)S(1)}, u32[]{:S(2)}, u32[]{:S(2)}) async-start(f32[8,40,128]{2,1,0:T(8,128)} %get-tuple-element.32), calls=%async_computation.1 | async-start | bytes 327680 | tf_op jit(solution)/shard_map/all_to_all | solution.py:546
  50.2 8.6 %collective-permute-start.10 = (f32[4,8,128]{2,1,0:T(8,128)S(1)}, f32[4,8,128]{2,1,0:T(8,128)S(1)}, u32[]{:S(2)}, u32[]{:S(2)}) collective-permute-start(f32[4,8,128]{2,1,0:T(8,128)S(1)} %get-tuple-element.31), channel_id=1, source_target_pairs={{128,0},{64,1},{96,2},{32,3},{192,4},{0,5},{160,6},{224,7},{136,8}... | collective-permute-start | bytes 49160 | tf_op jit(solution)/shard_map/ppermute | solution.py:554
  58.7 19.8 %collective-permute-start.12 = (f32[8,40,128]{2,1,0:T(8,128)S(1)}, f32[8,40,128]{2,1,0:T(8,128)S(1)}, u32[]{:S(2)}, u32[]{:S(2)}) collective-permute-start(f32[8,40,128]{2,1,0:T(8,128)S(1)} %all-to-all-done.1.refs_0_), channel_id=1, source_target_pairs={{0,16},{8,24},{16,0},{24,8},{32,48},{40,56},{48,32},{56,40},{64,80... | collective-permute-start | bytes 491528 | tf_op jit(solution)/shard_map/ppermute | solution.py:91
  61.5 17.0 %all-to-all-start.2 = ((f32[32,8,128]{2,1,0:T(8,128)}), f32[32,8,128]{2,1,0:T(8,128)S(1)}, u32[]{:S(2)}, u32[]{:S(2)}) async-start(f32[32,8,128]{2,1,0:T(8,128)} %bitcast.7), calls=%async_computation.2 | async-start | bytes 262144 | tf_op jit(solution)/shard_map/all_to_all | solution.py:563
  70.9 8.2 %collective-permute-start.11 = (f32[8,40,128]{2,1,0:T(8,128)S(1)}, f32[8,40,128]{2,1,0:T(8,128)S(1)}, u32[]{:S(2)}, u32[]{:S(2)}) collective-permute-start(f32[8,40,128]{2,1,0:T(8,128)S(1)} %all-to-all-done.1.refs_0_), channel_id=1, source_target_pairs={{0,8},{8,0},{16,24},{24,16},{32,40},{40,32},{48,56},{56,48},{64,72... | collective-permute-start | bytes 491528 | tf_op jit(solution)/shard_map/ppermute | solution.py:91
  78.5 1.4 %collective-permute-start.13 = (f32[8,40,128]{2,1,0:T(8,128)S(1)}, f32[8,40,128]{2,1,0:T(8,128)S(1)}, u32[]{:S(2)}, u32[]{:S(2)}) collective-permute-start(f32[8,40,128]{2,1,0:T(8,128)S(1)} %collective-permute-done.12.refs_2_), channel_id=1, source_target_pairs={{0,8},{8,0},{16,24},{24,16},{32,40},{40,32},{48,56},{56,48},{64,72... | collective-permute-start | bytes 491528 | tf_op jit(solution)/shard_map/ppermute | solution.py:91

commit v5 on v4

--- a/solution.py
+++ b/solution.py
@@ -28,7 +28,7 @@
             for h in range(H)
         ]
         flat = [hops[h][c] for h in range(H)]
-        columns = sorted(range(H), key=lambda h: (-flat[h], h))
+        columns = sorted(range(H), key=lambda h: (-flat[h], (h // 2 - c // 2) % 4))
         planes = sorted(range(Z), key=lambda b: (ring(b - c, Z), (b - c) % Z))
         for h, b in zip(columns, planes):
             once[c][h] = b
@@ -552,7 +552,6 @@
         axis_index_groups=[[4 * z + a for z in range(Z)] for a in range(A)],
     )
     left = lax.ppermute(left, both, [(d, s) for s, d in moves(ONCE)])
-    left, planes = after([left, planes])
     (spread,) = call(
         spread_kernel,
         vmem(1),
@@ -568,7 +567,7 @@
         tiled=True,
         axis_index_groups=[[32 * z + k for k in range(32)] for z in range(Z)],
     )
-    right = gather_cores([planes], after(gather_sides([planes]), left))
+    right = gather_cores([planes], after(gather_sides(after([planes], spread)), left))
     (pair_out,) = call(
         outer_kernel,
         smem(2) + vmem(8),

time: 84.9 us -> 84.4 us (level)
  no operation moved by 1% of the time
where the time goes in v5:
time: 84.4 us; the launch traced here: 84.1 us
  starting transfers between devices  51.5 us (61%)
  waiting for transfers between devices  16.4 us (19%)
  Pallas kernels  14.3 us (17%)
  between operations  1 us (1%)
    ppermute x11, starting transfers between devices, from_neighbour(): return lax.ppermute(v, 'row', [(r, r ^ bit) for r in range(Z * A)])  15.7 us
    all_to_all x1, starting transfers between devices, body(): lax.all_to_all(spread.reshape(A * H, 8, 128), both, 0, 0, tiled=True, axi...  8.67 us
    all_to_all x1, waiting for transfers between devices, body(): lax.all_to_all(spread.reshape(A * H, 8, 128), both, 0, 0, tiled=True, axi...  7.38 us
    ppermute x11, waiting for transfers between devices, from_neighbour(): return lax.ppermute(v, 'row', [(r, r ^ bit) for r in range(Z * A)])  6.42 us
    ppermute x1, starting transfers between devices, body(): left = lax.ppermute(left, both, [(d, s) for s, d in moves(ONCE)])  5.98 us
    all_to_all x1, starting transfers between devices, body(): lax.all_to_all(right, 'row', 0, 0, tiled=True, axis_index_groups=[[4 * z...  5.98 us
    all_to_all x1, starting transfers between devices, body(): everyone = lax.all_to_all(copies, 'head', 0, 0, tiled=True)  5.84 us
    ppermute x1, starting transfers between devices, body(): lax.ppermute(block, both, moves(TWICE[:, 0]))  5.25 us
  transfers between devices with their start and end apart: 17, of which 6 were waited for; matrix products, arithmetic and copies ran while one was open for 1% of the time, Pallas kernels for 4%

profile of v5, /device:TPU:1, one launch (start us, length us, event | category | flops | bytes accessed | tf_op | source)
XLA Modules:
  0.0 84.1 jit_solution(8053250907683099584)
XLA Ops:
  0.6 0.0 copy-start.1
  0.6 0.0 copy-start.15
  0.7 0.0 copy-start.13
  0.7 0.0 copy-start.14
  0.7 0.0 copy-start.11
  0.7 0.0 copy-start.7
  0.7 0.0 copy-start.8
  0.7 0.0 copy-start.9
  0.7 0.0 copy-start.10
  0.7 2.9 %shard_map.185 = (f32[1,64,128]{2,1,0:T(8,128)}, f32[8,2,64,256]{3,2,1,0:T(8,128)}) custom-call(f32[16,64,128]{2,1,0:T(8,128)} %refs_6_.1, f32[1,128]{1,0:T(1,128)} %bitcast.16, f32[8,128]{1,0:T(8,128)} %bitcast.15, f32[2,64,256]{2,1,0:T(8,128)} %refs_12_.1), custom_call_target="tpu_custom_call" | custom-call | flops 201326592 | bytes 600000 | tf_op jit(solution)/shard_map/pallas_call | solution.py:476
  3.6 5.2 %collective-permute-start = (f32[1,64,128]{2,1,0:T(8,128)}, f32[1,64,128]{2,1,0:T(8,128)S(1)}, u32[]{:S(2)}, u32[]{:S(2)}) collective-permute-start(f32[1,64,128]{2,1,0:T(8,128)} %get-tuple-element.24), channel_id=1, source_target_pairs={{0,96},{1,32},{2,64},{3,0},{4,160},{5,224},{6,128},{7,192},{8,104}... | collective-permute-start | bytes 98312 | tf_op jit(solution)/shard_map/ppermute | solution.py:494
  8.9 4.1 %collective-permute-start.1 = (f32[1,64,128]{2,1,0:T(8,128)}, f32[1,64,128]{2,1,0:T(8,128)S(1)}, u32[]{:S(2)}, u32[]{:S(2)}) collective-permute-start(f32[1,64,128]{2,1,0:T(8,128)} %get-tuple-element.24), channel_id=1, source_target_pairs={{0,128},{1,192},{2,160},{3,224},{4,64},{5,0},{6,96},{7,32},{8,136}... | collective-permute-start | bytes 98312 | tf_op jit(solution)/shard_map/ppermute | solution.py:494
  13.0 5.8 %all-to-all-start = ((f32[8,2,64,256]{3,2,1,0:T(8,128)}), f32[8,2,64,256]{3,2,1,0:T(8,128)S(1)}, u32[]{:S(2)}, u32[]{:S(2)}) async-start(f32[8,2,64,256]{3,2,1,0:T(8,128)} %get-tuple-element.25), calls=%async_computation | async-start | bytes 2097152 | tf_op jit(solution)/shard_map/all_to_all | solution.py:492
  18.9 0.1 copy.23.refs_15_
  19.0 0.1 dynamic_slice.6
  19.1 0.0 collective-permute-done
  19.1 0.0 collective-permute-done.1
  19.1 1.5 %collective-permute-start.2 = (f32[2,64,128]{2,1,0:T(8,128)S(1)}, f32[2,64,128]{2,1,0:T(8,128)S(1)}, u32[]{:S(2)}, u32[]{:S(2)}) collective-permute-start(f32[2,64,128]{2,1,0:T(8,128)S(1)} %pad_maximum_fusion), channel_id=1, source_target_pairs={{0,64},{8,72},{16,80},{24,88},{32,96},{40,104},{48,112},{56,120},{... | collective-permute-start | bytes 196616 | tf_op jit(solution)/shard_map/ppermute | solution.py:91
  20.6 2.6 %collective-permute-done.2 = f32[2,64,128]{2,1,0:T(8,128)S(1)} collective-permute-done((f32[2,64,128]{2,1,0:T(8,128)S(1)}, f32[2,64,128]{2,1,0:T(8,128)S(1)}, u32[]{:S(2)}, u32[]{:S(2)}) %collective-permute-start.2) | collective-permute-done | bytes 65568 | tf_op jit(solution)/shard_map/ppermute | solution.py:91
  23.2 2.2 %collective-permute-start.3 = (f32[4,64,128]{2,1,0:T(8,128)S(1)}, f32[4,64,128]{2,1,0:T(8,128)S(1)}, u32[]{:S(2)}, u32[]{:S(2)}) collective-permute-start(f32[4,64,128]{2,1,0:T(8,128)S(1)} %constant_dynamic-update-slice_fusion.refs_0_), channel_id=1, source_target_pairs={{0,32},{8,40},{16,48},{24,56},{32,0},{40,8},{48,16},{56,24},{64,96... | collective-permute-start | bytes 393224 | tf_op jit(solution)/shard_map/ppermute | solution.py:91
  25.4 0.1 broadcast_multiply_fusion
  25.4 0.1 mul.43.refs_17_
  25.6 0.4 collective-permute-start.6
  26.0 2.0 %collective-permute-done.3.refs_1_ = f32[4,64,128]{2,1,0:T(8,128)S(1)} collective-permute-done((f32[4,64,128]{2,1,0:T(8,128)S(1)}, f32[4,64,128]{2,1,0:T(8,128)S(1)}, u32[]{:S(2)}, u32[]{:S(2)}) %collective-permute-start.3) | collective-permute-done | bytes 131104 | tf_op jit(solution)/shard_map/ppermute | solution.py:91
  28.0 0.3 collective-permute-start.7
  28.3 3.6 %collective-permute-start.4 = (f32[4,64,128]{2,1,0:T(8,128)S(1)}, f32[4,64,128]{2,1,0:T(8,128)S(1)}, u32[]{:S(2)}, u32[]{:S(2)}) collective-permute-start(f32[4,64,128]{2,1,0:T(8,128)S(1)} %constant_dynamic-update-slice_fusion.refs_0_), channel_id=1, source_target_pairs={{0,8},{8,0},{16,24},{24,16},{32,40},{40,32},{48,56},{56,48},{64,72... | collective-permute-start | bytes 393224 | tf_op jit(solution)/shard_map/ppermute | solution.py:91
  32.0 0.0 collective-permute-start.5
  32.0 0.9 %collective-permute-done.6.refs_4_ = f32[4,64,128]{2,1,0:T(8,128)S(1)} collective-permute-done((f32[4,64,128]{2,1,0:T(8,128)S(1)}, f32[4,64,128]{2,1,0:T(8,128)S(1)}, u32[]{:S(2)}, u32[]{:S(2)}) %collective-permute-start.6) | collective-permute-done | bytes 131104 | tf_op jit(solution)/shard_map/ppermute | solution.py:91
  32.9 3.6 %collective-permute-start.8 = (f32[4,64,128]{2,1,0:T(8,128)S(1)}, f32[4,64,128]{2,1,0:T(8,128)S(1)}, u32[]{:S(2)}, u32[]{:S(2)}) collective-permute-start(f32[4,64,128]{2,1,0:T(8,128)S(1)} %collective-permute-done.6.refs_4_), channel_id=1, source_target_pairs={{0,8},{8,0},{16,24},{24,16},{32,40},{40,32},{48,56},{56,48},{64,72... | collective-permute-start | bytes 393224 | tf_op jit(solution)/shard_map/ppermute | solution.py:91
  36.4 0.0 collective-permute-done.7.refs_5_
  36.4 1.4 %collective-permute-start.9 = (f32[4,64,128]{2,1,0:T(8,128)S(1)}, f32[4,64,128]{2,1,0:T(8,128)S(1)}, u32[]{:S(2)}, u32[]{:S(2)}) collective-permute-start(f32[4,64,128]{2,1,0:T(8,128)S(1)} %collective-permute-done.7.refs_5_), channel_id=1, source_target_pairs={{0,8},{8,0},{16,24},{24,16},{32,40},{40,32},{48,56},{56,48},{64,72... | collective-permute-start | bytes 393224 | tf_op jit(solution)/shard_map/ppermute | solution.py:91
  37.8 0.0 all-to-all-done.all_ref
  37.8 0.0 copy-done.11
  37.9 0.0 copy-start
  37.9 0.0 copy-start.2
  37.9 0.0 copy-start.3
  37.9 0.0 copy-start.4
  37.9 2.3 %shard_map.186 = (f32[2,512,512]{2,1,0:T(8,128)S(1)}, bf16[2,2,256,512]{3,2,1,0:T(8,128)(2,1)S(1)}, f32[128,256]{1,0:T(8,128)S(1)}) custom-call(f32[8,2,64,256]{3,2,1,0:T(8,128)S(1)} %all-to-all-done.all_ref, f32[2,64,256]{2,1,0:T(8,128)S(1)} %copy-done.1, f32[1,256]{1,0:T(1,128)S(1)} %bitcast.13, f32[256,256]{1,0:T(8,128)S(1)} %copy-done.7, ...), custom_call_target="tpu_custom_call" | custom-call | flops 1610612736 | bytes 6291456 | tf_op jit(solution)/shard_map/pallas_call | solution.py:507
  40.3 0.0 collective-permute-done.4.refs_2_
  40.3 0.0 collective-permute-done.5.refs_3_
  40.3 0.0 collective-permute-done.8.refs_6_
  40.3 0.0 collective-permute-done.9.refs_7_
  40.3 0.1 broadcast_in_dim.23.refs_9_
  40.5 0.0 copy-start.5
  40.5 0.0 copy-start.6
  40.5 0.0 copy-start.12
  40.5 3.7 %shard_map.187 = (f32[2,64,256]{2,1,0:T(8,128)}, f32[4,8,128]{2,1,0:T(8,128)S(1)}, f32[8,40,128]{2,1,0:T(8,128)}) custom-call(s32[128]{0:T(128)S(1)} %copy-done.4, f32[4,64,128]{2,1,0:T(8,128)S(1)} %constant_dynamic-update-slice_fusion.refs_0_, f32[4,64,128]{2,1,0:T(8,128)S(1)} %collective-permute-done.3.refs_1_, ...), custom_call_target="tpu_custom_call" | custom-call | flops 805306368 | bytes 6291456 | tf_op jit(solution)/shard_map/pallas_call | solution.py:523
  44.2 6.0 %all-to-all-start.1 = ((f32[8,40,128]{2,1,0:T(8,128)}), f32[8,40,128]{2,1,0:T(8,128)S(1)}, u32[]{:S(2)}, u32[]{:S(2)}) async-start(f32[8,40,128]{2,1,0:T(8,128)} %get-tuple-element.30), calls=%async_computation.1 | async-start | bytes 327680 | tf_op jit(solution)/shard_map/all_to_all | solution.py:546
  50.2 6.0 %collective-permute-start.11 = (f32[4,8,128]{2,1,0:T(8,128)S(1)}, f32[4,8,128]{2,1,0:T(8,128)S(1)}, u32[]{:S(2)}, u32[]{:S(2)}) collective-permute-start(f32[4,8,128]{2,1,0:T(8,128)S(1)} %get-tuple-element.31), channel_id=1, source_target_pairs={{128,0},{64,1},{96,2},{32,3},{192,4},{0,5},{160,6},{224,7},{136,8}... | collective-permute-start | bytes 49160 | tf_op jit(solution)/shard_map/ppermute | solution.py:554
  56.1 2.6 %collective-permute-done.11.left_ref = f32[4,8,128]{2,1,0:T(8,128)S(1)} collective-permute-done((f32[4,8,128]{2,1,0:T(8,128)S(1)}, f32[4,8,128]{2,1,0:T(8,128)S(1)}, u32[]{:S(2)}, u32[]{:S(2)}) %collective-permute-start.11) | collective-permute-done | bytes 16416 | tf_op jit(solution)/shard_map/ppermute | solution.py:554
  58.7 0.7 shard_map.188
  59.5 0.0 all-to-all-done.1.refs_0_
  59.5 2.2 %collective-permute-start.12 = (f32[8,40,128]{2,1,0:T(8,128)S(1)}, f32[8,40,128]{2,1,0:T(8,128)S(1)}, u32[]{:S(2)}, u32[]{:S(2)}) collective-permute-start(f32[8,40,128]{2,1,0:T(8,128)S(1)} %all-to-all-done.1.refs_0_), channel_id=1, source_target_pairs={{0,16},{8,24},{16,0},{24,8},{32,48},{40,56},{48,32},{56,40},{64,80... | collective-permute-start | bytes 491528 | tf_op jit(solution)/shard_map/ppermute | solution.py:91
  61.6 8.7 %all-to-all-start.2 = ((f32[32,8,128]{2,1,0:T(8,128)}), f32[32,8,128]{2,1,0:T(8,128)S(1)}, u32[]{:S(2)}, u32[]{:S(2)}) async-start(f32[32,8,128]{2,1,0:T(8,128)} %bitcast.7), calls=%async_computation.2 | async-start | bytes 262144 | tf_op jit(solution)/shard_map/all_to_all | solution.py:562
  70.3 0.3 collective-permute-start.10
  70.6 7.4 %all-to-all-done.2.refs_4_ = f32[32,8,128]{2,1,0:T(8,128)S(1)} async-done(((f32[32,8,128]{2,1,0:T(8,128)}), f32[32,8,128]{2,1,0:T(8,128)S(1)}, u32[]{:S(2)}, u32[]{:S(2)}) %all-to-all-start.2) | async-done | bytes 131104 | tf_op jit(solution)/shard_map/all_to_all | solution.py:562
  78.0 0.0 collective-permute-done.12.refs_2_
  78.0 0.2 collective-permute-start.13
  78.2 0.1 dynamic_slice.7.rows_live_ref
  78.3 0.1 dynamic-slice_bitcast_fusion
  78.4 0.1 copy.25.refs_7_
  78.5 0.0 collective-permute-done.10.refs_1_
  78.5 0.9 %collective-permute-done.13.refs_3_ = f32[8,40,128]{2,1,0:T(8,128)S(1)} collective-permute-done((f32[8,40,128]{2,1,0:T(8,128)S(1)}, f32[8,40,128]{2,1,0:T(8,128)S(1)}, u32[]{:S(2)}, u32[]{:S(2)}) %collective-permute-start.13) | collective-permute-done | bytes 163872 | tf_op jit(solution)/shard_map/ppermute | solution.py:91
  79.4 4.7 %shard_map.189 = f32[16,64,128]{2,1,0:T(8,128)} custom-call(s32[64]{0:T(128)S(1)} %copy-done.12, f32[16]{0:T(128)S(1)} %dynamic_slice.7.rows_live_ref, f32[8,40,128]{2,1,0:T(8,128)S(1)} %all-to-all-done.1.refs_0_, f32[8,40,128]{2,1,0:T(8,128)S(1)} %collective-permute-done.10.refs_1_, f32[8,40,128]{2,1,0:T(8,128)S(1)} %collective-permute-done.12.refs_2_, ...), custom_call_target="tpu_custom_call" | custom-call | flops 1610612736 | bytes 4194304 | tf_op jit(solution)/shard_map/pallas_call | solution.py:571
  (24 shorter events, 0.1 us)
Async XLA Ops:
  0.6 37.2 %copy-start.1 = (f32[2,64,256]{2,1,0:T(8,128)S(1)}, f32[2,64,256]{2,1,0:T(8,128)}, u32[]{:S(2)}) copy-start(f32[2,64,256]{2,1,0:T(8,128)} %refs_12_.1) | copy-start | bytes 393220
  0.6 18.2 %copy-start.15 = (s32[2]{0:T(128)S(1)}, s32[2]{0:T(128)}, u32[]{:S(2)}) copy-start(s32[2]{0:T(128)} %param.22) | copy-start | bytes 28
  0.7 18.2 %copy-start.13 = (f32[256,32]{0,1:T(8,128)S(1)}, f32[256,32]{0,1:T(8,128)}, u32[]{:S(2)}) copy-start(f32[256,32]{0,1:T(8,128)} %param.33) | copy-start | bytes 98308
  0.7 18.3 %copy-start.14 = (s32[512]{0:T(512)S(1)}, s32[512]{0:T(512)}, u32[]{:S(2)}) copy-start(s32[512]{0:T(512)} %param.23) | copy-start | bytes 6148
  0.7 37.2 %copy-start.11 = (f32[256]{0:T(256)S(1)}, f32[256]{0:T(256)}, u32[]{:S(2)}) copy-start(f32[256]{0:T(256)} %param.24) | copy-start | bytes 3076
  0.7 37.2 %copy-start.7 = (f32[256,256]{1,0:T(8,128)S(1)}, f32[256,256]{1,0:T(8,128)}, u32[]{:S(2)}) copy-start(f32[256,256]{1,0:T(8,128)} %wq_ref.1) | copy-start | bytes 786436
  0.7 37.2 %copy-start.8 = (f32[256,256]{1,0:T(8,128)S(1)}, f32[256,256]{1,0:T(8,128)}, u32[]{:S(2)}) copy-start(f32[256,256]{1,0:T(8,128)} %wk_ref.1) | copy-start | bytes 786436
  0.7 37.2 %copy-start.9 = (f32[256,256]{1,0:T(8,128)S(1)}, f32[256,256]{1,0:T(8,128)}, u32[]{:S(2)}) copy-start(f32[256,256]{1,0:T(8,128)} %wv_ref.1) | copy-start | bytes 786436
  0.7 37.2 %copy-start.10 = (f32[256,256]{1,0:T(8,128)S(1)}, f32[256,256]{1,0:T(8,128)}, u32[]{:S(2)}) copy-start(f32[256,256]{1,0:T(8,128)} %wg_ref.1) | copy-start | bytes 786436
  3.6 15.4 %collective-permute-start = (f32[1,64,128]{2,1,0:T(8,128)}, f32[1,64,128]{2,1,0:T(8,128)S(1)}, u32[]{:S(2)}, u32[]{:S(2)}) collective-permute-start(f32[1,64,128]{2,1,0:T(8,128)} %get-tuple-element.24), channel_id=1, source_target_pairs={{0,96},{1,32},{2,64},{3,0},{4,160},{5,224},{6,128},{7,192},{8,104}... | collective-permute-start | bytes 98312 | tf_op jit(solution)/shard_map/ppermute | solution.py:494
  8.9 10.2 %collective-permute-start.1 = (f32[1,64,128]{2,1,0:T(8,128)}, f32[1,64,128]{2,1,0:T(8,128)S(1)}, u32[]{:S(2)}, u32[]{:S(2)}) collective-permute-start(f32[1,64,128]{2,1,0:T(8,128)} %get-tuple-element.24), channel_id=1, source_target_pairs={{0,128},{1,192},{2,160},{3,224},{4,64},{5,0},{6,96},{7,32},{8,136}... | collective-permute-start | bytes 98312 | tf_op jit(solution)/shard_map/ppermute | solution.py:494
  13.0 24.8 %all-to-all-start = ((f32[8,2,64,256]{3,2,1,0:T(8,128)}), f32[8,2,64,256]{3,2,1,0:T(8,128)S(1)}, u32[]{:S(2)}, u32[]{:S(2)}) async-start(f32[8,2,64,256]{3,2,1,0:T(8,128)} %get-tuple-element.25), calls=%async_computation | async-start | bytes 2097152 | tf_op jit(solution)/shard_map/all_to_all | solution.py:492
  19.1 4.1 %collective-permute-start.2 = (f32[2,64,128]{2,1,0:T(8,128)S(1)}, f32[2,64,128]{2,1,0:T(8,128)S(1)}, u32[]{:S(2)}, u32[]{:S(2)}) collective-permute-start(f32[2,64,128]{2,1,0:T(8,128)S(1)} %pad_maximum_fusion), channel_id=1, source_target_pairs={{0,64},{8,72},{16,80},{24,88},{32,96},{40,104},{48,112},{56,120},{... | collective-permute-start | bytes 196616 | tf_op jit(solution)/shard_map/ppermute | solution.py:91
  23.2 4.8 %collective-permute-start.3 = (f32[4,64,128]{2,1,0:T(8,128)S(1)}, f32[4,64,128]{2,1,0:T(8,128)S(1)}, u32[]{:S(2)}, u32[]{:S(2)}) collective-permute-start(f32[4,64,128]{2,1,0:T(8,128)S(1)} %constant_dynamic-update-slice_fusion.refs_0_), channel_id=1, source_target_pairs={{0,32},{8,40},{16,48},{24,56},{32,0},{40,8},{48,16},{56,24},{64,96... | collective-permute-start | bytes 393224 | tf_op jit(solution)/shard_map/ppermute | solution.py:91
  25.6 7.3 %collective-permute-start.6 = (f32[4,64,128]{2,1,0:T(8,128)S(1)}, f32[4,64,128]{2,1,0:T(8,128)S(1)}, u32[]{:S(2)}, u32[]{:S(2)}) collective-permute-start(f32[4,64,128]{2,1,0:T(8,128)S(1)} %constant_dynamic-update-slice_fusion.refs_0_), channel_id=1, source_target_pairs={{0,16},{8,24},{16,0},{24,8},{32,48},{40,56},{48,32},{56,40},{64,80... | collective-permute-start | bytes 393224 | tf_op jit(solution)/shard_map/ppermute | solution.py:91
  28.0 8.4 %collective-permute-start.7 = (f32[4,64,128]{2,1,0:T(8,128)S(1)}, f32[4,64,128]{2,1,0:T(8,128)S(1)}, u32[]{:S(2)}, u32[]{:S(2)}) collective-permute-start(f32[4,64,128]{2,1,0:T(8,128)S(1)} %collective-permute-done.3.refs_1_), channel_id=1, source_target_pairs={{0,16},{8,24},{16,0},{24,8},{32,48},{40,56},{48,32},{56,40},{64,80... | collective-permute-start | bytes 393224 | tf_op jit(solution)/shard_map/ppermute | solution.py:91
  28.3 11.9 %collective-permute-start.4 = (f32[4,64,128]{2,1,0:T(8,128)S(1)}, f32[4,64,128]{2,1,0:T(8,128)S(1)}, u32[]{:S(2)}, u32[]{:S(2)}) collective-permute-start(f32[4,64,128]{2,1,0:T(8,128)S(1)} %constant_dynamic-update-slice_fusion.refs_0_), channel_id=1, source_target_pairs={{0,8},{8,0},{16,24},{24,16},{32,40},{40,32},{48,56},{56,48},{64,72... | collective-permute-start | bytes 393224 | tf_op jit(solution)/shard_map/ppermute | solution.py:91
  32.0 8.3 %collective-permute-start.5 = (f32[4,64,128]{2,1,0:T(8,128)S(1)}, f32[4,64,128]{2,1,0:T(8,128)S(1)}, u32[]{:S(2)}, u32[]{:S(2)}) collective-permute-start(f32[4,64,128]{2,1,0:T(8,128)S(1)} %collective-permute-done.3.refs_1_), channel_id=1, source_target_pairs={{0,8},{8,0},{16,24},{24,16},{32,40},{40,32},{48,56},{56,48},{64,72... | collective-permute-start | bytes 393224 | tf_op jit(solution)/shard_map/ppermute | solution.py:91
  32.9 7.4 %collective-permute-start.8 = (f32[4,64,128]{2,1,0:T(8,128)S(1)}, f32[4,64,128]{2,1,0:T(8,128)S(1)}, u32[]{:S(2)}, u32[]{:S(2)}) collective-permute-start(f32[4,64,128]{2,1,0:T(8,128)S(1)} %collective-permute-done.6.refs_4_), channel_id=1, source_target_pairs={{0,8},{8,0},{16,24},{24,16},{32,40},{40,32},{48,56},{56,48},{64,72... | collective-permute-start | bytes 393224 | tf_op jit(solution)/shard_map/ppermute | solution.py:91
  36.4 3.8 %collective-permute-start.9 = (f32[4,64,128]{2,1,0:T(8,128)S(1)}, f32[4,64,128]{2,1,0:T(8,128)S(1)}, u32[]{:S(2)}, u32[]{:S(2)}) collective-permute-start(f32[4,64,128]{2,1,0:T(8,128)S(1)} %collective-permute-done.7.refs_5_), channel_id=1, source_target_pairs={{0,8},{8,0},{16,24},{24,16},{32,40},{40,32},{48,56},{56,48},{64,72... | collective-permute-start | bytes 393224 | tf_op jit(solution)/shard_map/ppermute | solution.py:91
  37.9 2.5 %copy-start = (f32[256,256]{1,0:T(8,128)S(1)}, f32[256,256]{1,0:T(8,128)}, u32[]{:S(2)}) copy-start(f32[256,256]{1,0:T(8,128)} %refs_13_.1) | copy-start | bytes 786436
  37.9 2.5 %copy-start.2 = (f32[256,32]{0,1:T(8,128)S(1)}, f32[256,32]{0,1:T(8,128)}, u32[]{:S(2)}) copy-start(f32[256,32]{0,1:T(8,128)} %param.34) | copy-start | bytes 98308
  37.9 2.5 %copy-start.3 = (f32[256]{0:T(256)S(1)}, f32[256]{0:T(256)}, u32[]{:S(2)}) copy-start(f32[256]{0:T(256)} %param.32) | copy-start | bytes 3076
  37.9 2.5 %copy-start.4 = (s32[128]{0:T(128)S(1)}, s32[128]{0:T(128)}, u32[]{:S(2)}) copy-start(s32[128]{0:T(128)} %constant.53.clone.spot_ref) | copy-start | bytes 1540
  40.5 38.9 %copy-start.5 = (f32[16,64,128]{2,1,0:T(8,128)S(1)}, f32[16,64,128]{2,1,0:T(8,128)}, u32[]{:S(2)}) copy-start(f32[16,64,128]{2,1,0:T(8,128)} %refs_6_.1) | copy-start | bytes 1572868
  40.5 38.9 %copy-start.6 = (f32[1024,128]{1,0:T(8,128)S(1)}, f32[1024,128]{1,0:T(8,128)}, u32[]{:S(2)}) copy-start(f32[1024,128]{1,0:T(8,128)} %refs_5_.1) | copy-start | bytes 1572868
  40.5 38.9 %copy-start.12 = (s32[64]{0:T(128)S(1)}, s32[64]{0:T(128)}, u32[]{:S(2)}) copy-start(s32[64]{0:T(128)} %constant.54.clone.once_ref) | copy-start | bytes 772
  44.2 15.3 %all-to-all-start.1 = ((f32[8,40,128]{2,1,0:T(8,128)}), f32[8,40,128]{2,1,0:T(8,128)S(1)}, u32[]{:S(2)}, u32[]{:S(2)}) async-start(f32[8,40,128]{2,1,0:T(8,128)} %get-tuple-element.30), calls=%async_computation.1 | async-start | bytes 327680 | tf_op jit(solution)/shard_map/all_to_all | solution.py:546
  50.2 8.6 %collective-permute-start.11 = (f32[4,8,128]{2,1,0:T(8,128)S(1)}, f32[4,8,128]{2,1,0:T(8,128)S(1)}, u32[]{:S(2)}, u32[]{:S(2)}) collective-permute-start(f32[4,8,128]{2,1,0:T(8,128)S(1)} %get-tuple-element.31), channel_id=1, source_target_pairs={{128,0},{64,1},{96,2},{32,3},{192,4},{0,5},{160,6},{224,7},{136,8}... | collective-permute-start | bytes 49160 | tf_op jit(solution)/shard_map/ppermute | solution.py:554
  59.5 18.5 %collective-permute-start.12 = (f32[8,40,128]{2,1,0:T(8,128)S(1)}, f32[8,40,128]{2,1,0:T(8,128)S(1)}, u32[]{:S(2)}, u32[]{:S(2)}) collective-permute-start(f32[8,40,128]{2,1,0:T(8,128)S(1)} %all-to-all-done.1.refs_0_), channel_id=1, source_target_pairs={{0,16},{8,24},{16,0},{24,8},{32,48},{40,56},{48,32},{56,40},{64,80... | collective-permute-start | bytes 491528 | tf_op jit(solution)/shard_map/ppermute | solution.py:91
  61.6 16.4 %all-to-all-start.2 = ((f32[32,8,128]{2,1,0:T(8,128)}), f32[32,8,128]{2,1,0:T(8,128)S(1)}, u32[]{:S(2)}, u32[]{:S(2)}) async-start(f32[32,8,128]{2,1,0:T(8,128)} %bitcast.7), calls=%async_computation.2 | async-start | bytes 262144 | tf_op jit(solution)/shard_map/all_to_all | solution.py:562
  70.3 8.2 %collective-permute-start.10 = (f32[8,40,128]{2,1,0:T(8,128)S(1)}, f32[8,40,128]{2,1,0:T(8,128)S(1)}, u32[]{:S(2)}, u32[]{:S(2)}) collective-permute-start(f32[8,40,128]{2,1,0:T(8,128)S(1)} %all-to-all-done.1.refs_0_), channel_id=1, source_target_pairs={{0,8},{8,0},{16,24},{24,16},{32,40},{40,32},{48,56},{56,48},{64,72... | collective-permute-start | bytes 491528 | tf_op jit(solution)/shard_map/ppermute | solution.py:91
  78.0 1.4 %collective-permute-start.13 = (f32[8,40,128]{2,1,0:T(8,128)S(1)}, f32[8,40,128]{2,1,0:T(8,128)S(1)}, u32[]{:S(2)}, u32[]{:S(2)}) collective-permute-start(f32[8,40,128]{2,1,0:T(8,128)S(1)} %collective-permute-done.12.refs_2_), channel_id=1, source_target_pairs={{0,8},{8,0},{16,24},{24,16},{32,40},{40,32},{48,56},{56,48},{64,72... | collective-permute-start | bytes 491528 | tf_op jit(solution)/shard_map/ppermute | solution.py:91

commit v6 on v5

--- a/solution.py
+++ b/solution.py
@@ -335,12 +335,14 @@
     weight_ref,
     pair_ref,
     cols_live_ref,
-    out_ref,
+    out_hbm,
     right_in_ref,
     sorted_ref,
     left_ref,
     right_ref,
     outer_ref,
+    out_ref,
+    sems,
 ):
     for q, piece_ref in enumerate(piece_refs):
         for k in range(Z):
@@ -396,6 +398,7 @@
     for n in range(8):
         columns = pl.ds(256 * n, 256)
         outer_ref[:, columns] = dot(left_ref[...], right_ref[:, columns])
+    stores = []
     for q in range(8):
         stacked = jnp.concatenate(
             [
@@ -422,6 +425,14 @@
             i = 2 * q + e
             norm = count * rows_live_ref[i] * cols_live_ref[...] + 0.001
             out_ref[i] = pair_ref[i] + total[64 * e : 64 * e + 64] / norm
+        stores += start_all(
+            [
+                pltpu.make_async_copy(
+                    out_ref.at[2 * q : 2 * q + 2], out_hbm.at[2 * q : 2 * q + 2], sems.at[q]
+                )
+            ]
+        )
+    wait_all(stores)
 
 
 def vmem(count):
@@ -571,7 +582,7 @@
     (pair_out,) = call(
         outer_kernel,
         smem(2) + vmem(8),
-        vmem(1),
+        hbm(1),
         [struct(16, 64, 128)],
         scratch=[
             pltpu.VMEM((1280, 128), f32),
@@ -579,6 +590,8 @@
             pltpu.VMEM((512, 256), bf16),
             pltpu.VMEM((256, 2048), bf16),
             pltpu.VMEM((512, 2048), f32),
+            pltpu.VMEM((16, 64, 128), f32),
+            pltpu.SemaphoreType.DMA((8,)),
         ],
         flops=3 * 2 * 1024 * 1024 * 256,
         touched=4 * MIB,

time: 84.4 us -> 84.5 us (level)
  no operation moved by 1% of the time
where the time goes in v6:
time: 84.5 us; the launch traced here: 84.2 us
  starting transfers between devices  51.5 us (61%)
  waiting for transfers between devices  16.4 us (19%)
  Pallas kernels  14.2 us (17%)
  between operations  1.16 us (1%)
    ppermute x11, starting transfers between devices, from_neighbour(): return lax.ppermute(v, 'row', [(r, r ^ bit) for r in range(Z * A)])  15.7 us
    all_to_all x1, starting transfers between devices, body(): lax.all_to_all(spread.reshape(A * H, 8, 128), both, 0, 0, tiled=True, axi...  8.67 us
    all_to_all x1, waiting for transfers between devices, body(): lax.all_to_all(spread.reshape(A * H, 8, 128), both, 0, 0, tiled=True, axi...  7.38 us
    ppermute x11, waiting for transfers between devices, from_neighbour(): return lax.ppermute(v, 'row', [(r, r ^ bit) for r in range(Z * A)])  6.42 us
    ppermute x1, starting transfers between devices, body(): left = lax.ppermute(left, both, [(d, s) for s, d in moves(ONCE)])  5.98 us
    all_to_all x1, starting transfers between devices, body(): lax.all_to_all(right, 'row', 0, 0, tiled=True, axis_index_groups=[[4 * z...  5.98 us
    all_to_all x1, starting transfers between devices, body(): everyone = lax.all_to_all(copies, 'head', 0, 0, tiled=True)  5.84 us
    ppermute x1, starting transfers between devices, body(): lax.ppermute(block, both, moves(TWICE[:, 0]))  5.25 us
  transfers between devices with their start and end apart: 17, of which 6 were waited for; matrix products, arithmetic and copies ran while one was open for 1% of the time, Pallas kernels for 4%

profile of v6, /device:TPU:1, one launch (start us, length us, event | category | flops | bytes accessed | tf_op | source)
XLA Modules:
  0.0 84.2 jit_solution(7176355789792137808)
XLA Ops:
  0.6 0.0 copy-start.1
  0.6 0.0 copy-start.15
  0.7 0.0 copy-start.13
  0.7 0.0 copy-start.14
  0.7 0.0 copy-start.11
  0.7 2.9 %shard_map.185 = (f32[1,64,128]{2,1,0:T(8,128)}, f32[8,2,64,256]{3,2,1,0:T(8,128)}) custom-call(f32[16,64,128]{2,1,0:T(8,128)} %refs_6_.1, f32[1,128]{1,0:T(1,128)} %bitcast.16, f32[8,128]{1,0:T(8,128)} %bitcast.15, f32[2,64,256]{2,1,0:T(8,128)} %refs_12_.1), custom_call_target="tpu_custom_call" | custom-call | flops 201326592 | bytes 600000 | tf_op jit(solution)/shard_map/pallas_call | solution.py:487
  3.6 5.2 %collective-permute-start = (f32[1,64,128]{2,1,0:T(8,128)}, f32[1,64,128]{2,1,0:T(8,128)S(1)}, u32[]{:S(2)}, u32[]{:S(2)}) collective-permute-start(f32[1,64,128]{2,1,0:T(8,128)} %get-tuple-element.24), channel_id=1, source_target_pairs={{0,96},{1,32},{2,64},{3,0},{4,160},{5,224},{6,128},{7,192},{8,104}... | collective-permute-start | bytes 98312 | tf_op jit(solution)/shard_map/ppermute | solution.py:505
  8.9 4.1 %collective-permute-start.1 = (f32[1,64,128]{2,1,0:T(8,128)}, f32[1,64,128]{2,1,0:T(8,128)S(1)}, u32[]{:S(2)}, u32[]{:S(2)}) collective-permute-start(f32[1,64,128]{2,1,0:T(8,128)} %get-tuple-element.24), channel_id=1, source_target_pairs={{0,128},{1,192},{2,160},{3,224},{4,64},{5,0},{6,96},{7,32},{8,136}... | collective-permute-start | bytes 98312 | tf_op jit(solution)/shard_map/ppermute | solution.py:505
  13.0 5.8 %all-to-all-start = ((f32[8,2,64,256]{3,2,1,0:T(8,128)}), f32[8,2,64,256]{3,2,1,0:T(8,128)S(1)}, u32[]{:S(2)}, u32[]{:S(2)}) async-start(f32[8,2,64,256]{3,2,1,0:T(8,128)} %get-tuple-element.25), calls=%async_computation | async-start | bytes 2097152 | tf_op jit(solution)/shard_map/all_to_all | solution.py:503
  18.9 0.1 copy.23.refs_15_
  19.0 0.0 copy-done.14
  19.0 0.1 dynamic_slice.6
  19.1 0.0 collective-permute-done
  19.1 0.0 collective-permute-done.1
  19.1 1.5 %collective-permute-start.2 = (f32[2,64,128]{2,1,0:T(8,128)S(1)}, f32[2,64,128]{2,1,0:T(8,128)S(1)}, u32[]{:S(2)}, u32[]{:S(2)}) collective-permute-start(f32[2,64,128]{2,1,0:T(8,128)S(1)} %pad_maximum_fusion), channel_id=1, source_target_pairs={{0,64},{8,72},{16,80},{24,88},{32,96},{40,104},{48,112},{56,120},{... | collective-permute-start | bytes 196616 | tf_op jit(solution)/shard_map/ppermute | solution.py:91
  20.6 2.6 %collective-permute-done.2 = f32[2,64,128]{2,1,0:T(8,128)S(1)} collective-permute-done((f32[2,64,128]{2,1,0:T(8,128)S(1)}, f32[2,64,128]{2,1,0:T(8,128)S(1)}, u32[]{:S(2)}, u32[]{:S(2)}) %collective-permute-start.2) | collective-permute-done | bytes 65568 | tf_op jit(solution)/shard_map/ppermute | solution.py:91
  23.2 2.2 %collective-permute-start.3 = (f32[4,64,128]{2,1,0:T(8,128)S(1)}, f32[4,64,128]{2,1,0:T(8,128)S(1)}, u32[]{:S(2)}, u32[]{:S(2)}) collective-permute-start(f32[4,64,128]{2,1,0:T(8,128)S(1)} %constant_dynamic-update-slice_fusion.refs_0_), channel_id=1, source_target_pairs={{0,32},{8,40},{16,48},{24,56},{32,0},{40,8},{48,16},{56,24},{64,96... | collective-permute-start | bytes 393224 | tf_op jit(solution)/shard_map/ppermute | solution.py:91
  25.4 0.1 broadcast_multiply_fusion
  25.4 0.1 mul.43.refs_17_
  25.6 0.4 collective-permute-start.6
  26.0 2.0 %collective-permute-done.3.refs_1_ = f32[4,64,128]{2,1,0:T(8,128)S(1)} collective-permute-done((f32[4,64,128]{2,1,0:T(8,128)S(1)}, f32[4,64,128]{2,1,0:T(8,128)S(1)}, u32[]{:S(2)}, u32[]{:S(2)}) %collective-permute-start.3) | collective-permute-done | bytes 131104 | tf_op jit(solution)/shard_map/ppermute | solution.py:91
  28.0 0.3 collective-permute-start.7
  28.3 3.6 %collective-permute-start.4 = (f32[4,64,128]{2,1,0:T(8,128)S(1)}, f32[4,64,128]{2,1,0:T(8,128)S(1)}, u32[]{:S(2)}, u32[]{:S(2)}) collective-permute-start(f32[4,64,128]{2,1,0:T(8,128)S(1)} %constant_dynamic-update-slice_fusion.refs_0_), channel_id=1, source_target_pairs={{0,8},{8,0},{16,24},{24,16},{32,40},{40,32},{48,56},{56,48},{64,72... | collective-permute-start | bytes 393224 | tf_op jit(solution)/shard_map/ppermute | solution.py:91
  32.0 0.0 collective-permute-start.5
  32.0 0.9 %collective-permute-done.6.refs_4_ = f32[4,64,128]{2,1,0:T(8,128)S(1)} collective-permute-done((f32[4,64,128]{2,1,0:T(8,128)S(1)}, f32[4,64,128]{2,1,0:T(8,128)S(1)}, u32[]{:S(2)}, u32[]{:S(2)}) %collective-permute-start.6) | collective-permute-done | bytes 131104 | tf_op jit(solution)/shard_map/ppermute | solution.py:91
  32.9 3.6 %collective-permute-start.8 = (f32[4,64,128]{2,1,0:T(8,128)S(1)}, f32[4,64,128]{2,1,0:T(8,128)S(1)}, u32[]{:S(2)}, u32[]{:S(2)}) collective-permute-start(f32[4,64,128]{2,1,0:T(8,128)S(1)} %collective-permute-done.6.refs_4_), channel_id=1, source_target_pairs={{0,8},{8,0},{16,24},{24,16},{32,40},{40,32},{48,56},{56,48},{64,72... | collective-permute-start | bytes 393224 | tf_op jit(solution)/shard_map/ppermute | solution.py:91
  36.4 0.0 collective-permute-done.7.refs_5_
  36.4 1.4 %collective-permute-start.9 = (f32[4,64,128]{2,1,0:T(8,128)S(1)}, f32[4,64,128]{2,1,0:T(8,128)S(1)}, u32[]{:S(2)}, u32[]{:S(2)}) collective-permute-start(f32[4,64,128]{2,1,0:T(8,128)S(1)} %collective-permute-done.7.refs_5_), channel_id=1, source_target_pairs={{0,8},{8,0},{16,24},{24,16},{32,40},{40,32},{48,56},{56,48},{64,72... | collective-permute-start | bytes 393224 | tf_op jit(solution)/shard_map/ppermute | solution.py:91
  37.8 0.0 all-to-all-done.all_ref
  37.9 0.0 copy-done.7
  37.9 0.0 copy-done.8
  37.9 0.0 copy-done.9
  37.9 0.0 copy-done.10
  37.9 0.0 copy-start
  37.9 0.0 copy-start.2
  37.9 0.0 copy-start.3
  37.9 0.0 copy-start.4
  37.9 2.3 %shard_map.186 = (f32[2,512,512]{2,1,0:T(8,128)S(1)}, bf16[2,2,256,512]{3,2,1,0:T(8,128)(2,1)S(1)}, f32[128,256]{1,0:T(8,128)S(1)}) custom-call(f32[8,2,64,256]{3,2,1,0:T(8,128)S(1)} %all-to-all-done.all_ref, f32[2,64,256]{2,1,0:T(8,128)S(1)} %copy-done.1, f32[1,256]{1,0:T(1,128)S(1)} %bitcast.13, f32[256,256]{1,0:T(8,128)S(1)} %copy-done.7, ...), custom_call_target="tpu_custom_call" | custom-call | flops 1610612736 | bytes 6291456 | tf_op jit(solution)/shard_map/pallas_call | solution.py:518
  40.3 0.0 collective-permute-done.4.refs_2_
  40.3 0.0 collective-permute-done.5.refs_3_
  40.3 0.0 collective-permute-done.8.refs_6_
  40.3 0.0 collective-permute-done.9.refs_7_
  40.3 0.1 broadcast_in_dim.23.refs_9_
  40.5 0.0 copy-start.5
  40.5 0.0 copy-start.6
  40.5 0.0 copy-start.12
  40.5 3.7 %shard_map.187 = (f32[2,64,256]{2,1,0:T(8,128)}, f32[4,8,128]{2,1,0:T(8,128)S(1)}, f32[8,40,128]{2,1,0:T(8,128)}) custom-call(s32[128]{0:T(128)S(1)} %copy-done.4, f32[4,64,128]{2,1,0:T(8,128)S(1)} %constant_dynamic-update-slice_fusion.refs_0_, f32[4,64,128]{2,1,0:T(8,128)S(1)} %collective-permute-done.3.refs_1_, ...), custom_call_target="tpu_custom_call" | custom-call | flops 805306368 | bytes 6291456 | tf_op jit(solution)/shard_map/pallas_call | solution.py:534
  44.2 6.0 %all-to-all-start.1 = ((f32[8,40,128]{2,1,0:T(8,128)}), f32[8,40,128]{2,1,0:T(8,128)S(1)}, u32[]{:S(2)}, u32[]{:S(2)}) async-start(f32[8,40,128]{2,1,0:T(8,128)} %get-tuple-element.30), calls=%async_computation.1 | async-start | bytes 327680 | tf_op jit(solution)/shard_map/all_to_all | solution.py:557
  50.2 6.0 %collective-permute-start.11 = (f32[4,8,128]{2,1,0:T(8,128)S(1)}, f32[4,8,128]{2,1,0:T(8,128)S(1)}, u32[]{:S(2)}, u32[]{:S(2)}) collective-permute-start(f32[4,8,128]{2,1,0:T(8,128)S(1)} %get-tuple-element.31), channel_id=1, source_target_pairs={{128,0},{64,1},{96,2},{32,3},{192,4},{0,5},{160,6},{224,7},{136,8}... | collective-permute-start | bytes 49160 | tf_op jit(solution)/shard_map/ppermute | solution.py:565
  56.1 2.6 %collective-permute-done.11.left_ref = f32[4,8,128]{2,1,0:T(8,128)S(1)} collective-permute-done((f32[4,8,128]{2,1,0:T(8,128)S(1)}, f32[4,8,128]{2,1,0:T(8,128)S(1)}, u32[]{:S(2)}, u32[]{:S(2)}) %collective-permute-start.11) | collective-permute-done | bytes 16416 | tf_op jit(solution)/shard_map/ppermute | solution.py:565
  58.7 0.7 shard_map.188
  59.5 0.0 all-to-all-done.1.refs_0_
  59.5 2.2 %collective-permute-start.12 = (f32[8,40,128]{2,1,0:T(8,128)S(1)}, f32[8,40,128]{2,1,0:T(8,128)S(1)}, u32[]{:S(2)}, u32[]{:S(2)}) collective-permute-start(f32[8,40,128]{2,1,0:T(8,128)S(1)} %all-to-all-done.1.refs_0_), channel_id=1, source_target_pairs={{0,16},{8,24},{16,0},{24,8},{32,48},{40,56},{48,32},{56,40},{64,80... | collective-permute-start | bytes 491528 | tf_op jit(solution)/shard_map/ppermute | solution.py:91
  61.6 8.7 %all-to-all-start.2 = ((f32[32,8,128]{2,1,0:T(8,128)}), f32[32,8,128]{2,1,0:T(8,128)S(1)}, u32[]{:S(2)}, u32[]{:S(2)}) async-start(f32[32,8,128]{2,1,0:T(8,128)} %bitcast.7), calls=%async_computation.2 | async-start | bytes 262144 | tf_op jit(solution)/shard_map/all_to_all | solution.py:573
  70.3 0.3 collective-permute-start.10
  70.6 7.4 %all-to-all-done.2.refs_4_ = f32[32,8,128]{2,1,0:T(8,128)S(1)} async-done(((f32[32,8,128]{2,1,0:T(8,128)}), f32[32,8,128]{2,1,0:T(8,128)S(1)}, u32[]{:S(2)}, u32[]{:S(2)}) %all-to-all-start.2) | async-done | bytes 131104 | tf_op jit(solution)/shard_map/all_to_all | solution.py:573
  78.0 0.0 collective-permute-done.12.refs_2_
  78.0 0.2 collective-permute-start.13
  78.2 0.1 dynamic_slice.7.rows_live_ref
  78.3 0.1 dynamic-slice_bitcast_fusion
  78.4 0.1 copy.25.refs_7_
  78.5 0.0 collective-permute-done.10.refs_1_
  78.5 0.9 %collective-permute-done.13.refs_3_ = f32[8,40,128]{2,1,0:T(8,128)S(1)} collective-permute-done((f32[8,40,128]{2,1,0:T(8,128)S(1)}, f32[8,40,128]{2,1,0:T(8,128)S(1)}, u32[]{:S(2)}, u32[]{:S(2)}) %collective-permute-start.13) | collective-permute-done | bytes 163872 | tf_op jit(solution)/shard_map/ppermute | solution.py:91
  79.4 4.6 %shard_map.189 = f32[16,64,128]{2,1,0:T(8,128)} custom-call(s32[64]{0:T(128)S(1)} %copy-done.12, f32[16]{0:T(128)S(1)} %dynamic_slice.7.rows_live_ref, f32[8,40,128]{2,1,0:T(8,128)S(1)} %all-to-all-done.1.refs_0_, f32[8,40,128]{2,1,0:T(8,128)S(1)} %collective-permute-done.10.refs_1_, f32[8,40,128]{2,1,0:T(8,128)S(1)} %collective-permute-done.12.refs_2_, ...), custom_call_target="tpu_custom_call" | custom-call | flops 1610612736 | bytes 4194304 | tf_op jit(solution)/shard_map/pallas_call | solution.py:582
  (24 shorter events, 0.1 us)
Async XLA Ops:
  0.6 37.2 %copy-start.1 = (f32[2,64,256]{2,1,0:T(8,128)S(1)}, f32[2,64,256]{2,1,0:T(8,128)}, u32[]{:S(2)}) copy-start(f32[2,64,256]{2,1,0:T(8,128)} %refs_12_.1) | copy-start | bytes 393220
  0.6 18.2 %copy-start.15 = (s32[2]{0:T(128)S(1)}, s32[2]{0:T(128)}, u32[]{:S(2)}) copy-start(s32[2]{0:T(128)} %param.22) | copy-start | bytes 28
  0.7 18.2 %copy-start.13 = (f32[256,32]{0,1:T(8,128)S(1)}, f32[256,32]{0,1:T(8,128)}, u32[]{:S(2)}) copy-start(f32[256,32]{0,1:T(8,128)} %param.33) | copy-start | bytes 98308
  0.7 18.3 %copy-start.14 = (s32[512]{0:T(512)S(1)}, s32[512]{0:T(512)}, u32[]{:S(2)}) copy-start(s32[512]{0:T(512)} %param.23) | copy-start | bytes 6148
  0.7 37.2 %copy-start.11 = (f32[256]{0:T(256)S(1)}, f32[256]{0:T(256)}, u32[]{:S(2)}) copy-start(f32[256]{0:T(256)} %param.24) | copy-start | bytes 3076
  0.7 37.2 %copy-start.7 = (f32[256,256]{1,0:T(8,128)S(1)}, f32[256,256]{1,0:T(8,128)}, u32[]{:S(2)}) copy-start(f32[256,256]{1,0:T(8,128)} %wq_ref.1) | copy-start | bytes 786436
  0.7 37.2 %copy-start.8 = (f32[256,256]{1,0:T(8,128)S(1)}, f32[256,256]{1,0:T(8,128)}, u32[]{:S(2)}) copy-start(f32[256,256]{1,0:T(8,128)} %wk_ref.1) | copy-start | bytes 786436
  0.7 37.2 %copy-start.9 = (f32[256,256]{1,0:T(8,128)S(1)}, f32[256,256]{1,0:T(8,128)}, u32[]{:S(2)}) copy-start(f32[256,256]{1,0:T(8,128)} %wv_ref.1) | copy-start | bytes 786436
  0.7 37.2 %copy-start.10 = (f32[256,256]{1,0:T(8,128)S(1)}, f32[256,256]{1,0:T(8,128)}, u32[]{:S(2)}) copy-start(f32[256,256]{1,0:T(8,128)} %wg_ref.1) | copy-start | bytes 786436
  3.6 15.4 %collective-permute-start = (f32[1,64,128]{2,1,0:T(8,128)}, f32[1,64,128]{2,1,0:T(8,128)S(1)}, u32[]{:S(2)}, u32[]{:S(2)}) collective-permute-start(f32[1,64,128]{2,1,0:T(8,128)} %get-tuple-element.24), channel_id=1, source_target_pairs={{0,96},{1,32},{2,64},{3,0},{4,160},{5,224},{6,128},{7,192},{8,104}... | collective-permute-start | bytes 98312 | tf_op jit(solution)/shard_map/ppermute | solution.py:505
  8.9 10.2 %collective-permute-start.1 = (f32[1,64,128]{2,1,0:T(8,128)}, f32[1,64,128]{2,1,0:T(8,128)S(1)}, u32[]{:S(2)}, u32[]{:S(2)}) collective-permute-start(f32[1,64,128]{2,1,0:T(8,128)} %get-tuple-element.24), channel_id=1, source_target_pairs={{0,128},{1,192},{2,160},{3,224},{4,64},{5,0},{6,96},{7,32},{8,136}... | collective-permute-start | bytes 98312 | tf_op jit(solution)/shard_map/ppermute | solution.py:505
  13.0 24.8 %all-to-all-start = ((f32[8,2,64,256]{3,2,1,0:T(8,128)}), f32[8,2,64,256]{3,2,1,0:T(8,128)S(1)}, u32[]{:S(2)}, u32[]{:S(2)}) async-start(f32[8,2,64,256]{3,2,1,0:T(8,128)} %get-tuple-element.25), calls=%async_computation | async-start | bytes 2097152 | tf_op jit(solution)/shard_map/all_to_all | solution.py:503
  19.1 4.1 %collective-permute-start.2 = (f32[2,64,128]{2,1,0:T(8,128)S(1)}, f32[2,64,128]{2,1,0:T(8,128)S(1)}, u32[]{:S(2)}, u32[]{:S(2)}) collective-permute-start(f32[2,64,128]{2,1,0:T(8,128)S(1)} %pad_maximum_fusion), channel_id=1, source_target_pairs={{0,64},{8,72},{16,80},{24,88},{32,96},{40,104},{48,112},{56,120},{... | collective-permute-start | bytes 196616 | tf_op jit(solution)/shard_map/ppermute | solution.py:91
  23.2 4.8 %collective-permute-start.3 = (f32[4,64,128]{2,1,0:T(8,128)S(1)}, f32[4,64,128]{2,1,0:T(8,128)S(1)}, u32[]{:S(2)}, u32[]{:S(2)}) collective-permute-start(f32[4,64,128]{2,1,0:T(8,128)S(1)} %constant_dynamic-update-slice_fusion.refs_0_), channel_id=1, source_target_pairs={{0,32},{8,40},{16,48},{24,56},{32,0},{40,8},{48,16},{56,24},{64,96... | collective-permute-start | bytes 393224 | tf_op jit(solution)/shard_map/ppermute | solution.py:91
  25.6 7.3 %collective-permute-start.6 = (f32[4,64,128]{2,1,0:T(8,128)S(1)}, f32[4,64,128]{2,1,0:T(8,128)S(1)}, u32[]{:S(2)}, u32[]{:S(2)}) collective-permute-start(f32[4,64,128]{2,1,0:T(8,128)S(1)} %constant_dynamic-update-slice_fusion.refs_0_), channel_id=1, source_target_pairs={{0,16},{8,24},{16,0},{24,8},{32,48},{40,56},{48,32},{56,40},{64,80... | collective-permute-start | bytes 393224 | tf_op jit(solution)/shard_map/ppermute | solution.py:91
  28.0 8.4 %collective-permute-start.7 = (f32[4,64,128]{2,1,0:T(8,128)S(1)}, f32[4,64,128]{2,1,0:T(8,128)S(1)}, u32[]{:S(2)}, u32[]{:S(2)}) collective-permute-start(f32[4,64,128]{2,1,0:T(8,128)S(1)} %collective-permute-done.3.refs_1_), channel_id=1, source_target_pairs={{0,16},{8,24},{16,0},{24,8},{32,48},{40,56},{48,32},{56,40},{64,80... | collective-permute-start | bytes 393224 | tf_op jit(solution)/shard_map/ppermute | solution.py:91
  28.3 11.9 %collective-permute-start.4 = (f32[4,64,128]{2,1,0:T(8,128)S(1)}, f32[4,64,128]{2,1,0:T(8,128)S(1)}, u32[]{:S(2)}, u32[]{:S(2)}) collective-permute-start(f32[4,64,128]{2,1,0:T(8,128)S(1)} %constant_dynamic-update-slice_fusion.refs_0_), channel_id=1, source_target_pairs={{0,8},{8,0},{16,24},{24,16},{32,40},{40,32},{48,56},{56,48},{64,72... | collective-permute-start | bytes 393224 | tf_op jit(solution)/shard_map/ppermute | solution.py:91
  32.0 8.3 %collective-permute-start.5 = (f32[4,64,128]{2,1,0:T(8,128)S(1)}, f32[4,64,128]{2,1,0:T(8,128)S(1)}, u32[]{:S(2)}, u32[]{:S(2)}) collective-permute-start(f32[4,64,128]{2,1,0:T(8,128)S(1)} %collective-permute-done.3.refs_1_), channel_id=1, source_target_pairs={{0,8},{8,0},{16,24},{24,16},{32,40},{40,32},{48,56},{56,48},{64,72... | collective-permute-start | bytes 393224 | tf_op jit(solution)/shard_map/ppermute | solution.py:91
  32.9 7.4 %collective-permute-start.8 = (f32[4,64,128]{2,1,0:T(8,128)S(1)}, f32[4,64,128]{2,1,0:T(8,128)S(1)}, u32[]{:S(2)}, u32[]{:S(2)}) collective-permute-start(f32[4,64,128]{2,1,0:T(8,128)S(1)} %collective-permute-done.6.refs_4_), channel_id=1, source_target_pairs={{0,8},{8,0},{16,24},{24,16},{32,40},{40,32},{48,56},{56,48},{64,72... | collective-permute-start | bytes 393224 | tf_op jit(solution)/shard_map/ppermute | solution.py:91
  36.4 3.8 %collective-permute-start.9 = (f32[4,64,128]{2,1,0:T(8,128)S(1)}, f32[4,64,128]{2,1,0:T(8,128)S(1)}, u32[]{:S(2)}, u32[]{:S(2)}) collective-permute-start(f32[4,64,128]{2,1,0:T(8,128)S(1)} %collective-permute-done.7.refs_5_), channel_id=1, source_target_pairs={{0,8},{8,0},{16,24},{24,16},{32,40},{40,32},{48,56},{56,48},{64,72... | collective-permute-start | bytes 393224 | tf_op jit(solution)/shard_map/ppermute | solution.py:91
  37.9 2.5 %copy-start = (f32[256,256]{1,0:T(8,128)S(1)}, f32[256,256]{1,0:T(8,128)}, u32[]{:S(2)}) copy-start(f32[256,256]{1,0:T(8,128)} %refs_13_.1) | copy-start | bytes 786436
  37.9 2.5 %copy-start.2 = (f32[256,32]{0,1:T(8,128)S(1)}, f32[256,32]{0,1:T(8,128)}, u32[]{:S(2)}) copy-start(f32[256,32]{0,1:T(8,128)} %param.34) | copy-start | bytes 98308
  37.9 2.5 %copy-start.3 = (f32[256]{0:T(256)S(1)}, f32[256]{0:T(256)}, u32[]{:S(2)}) copy-start(f32[256]{0:T(256)} %param.32) | copy-start | bytes 3076
  37.9 2.5 %copy-start.4 = (s32[128]{0:T(128)S(1)}, s32[128]{0:T(128)}, u32[]{:S(2)}) copy-start(s32[128]{0:T(128)} %constant.53.clone.spot_ref) | copy-start | bytes 1540
  40.5 38.9 %copy-start.5 = (f32[16,64,128]{2,1,0:T(8,128)S(1)}, f32[16,64,128]{2,1,0:T(8,128)}, u32[]{:S(2)}) copy-start(f32[16,64,128]{2,1,0:T(8,128)} %refs_6_.1) | copy-start | bytes 1572868
  40.5 38.9 %copy-start.6 = (f32[1024,128]{1,0:T(8,128)S(1)}, f32[1024,128]{1,0:T(8,128)}, u32[]{:S(2)}) copy-start(f32[1024,128]{1,0:T(8,128)} %refs_5_.1) | copy-start | bytes 1572868
  40.5 38.9 %copy-start.12 = (s32[64]{0:T(128)S(1)}, s32[64]{0:T(128)}, u32[]{:S(2)}) copy-start(s32[64]{0:T(128)} %constant.54.clone.once_ref) | copy-start | bytes 772
  44.2 15.3 %all-to-all-start.1 = ((f32[8,40,128]{2,1,0:T(8,128)}), f32[8,40,128]{2,1,0:T(8,128)S(1)}, u32[]{:S(2)}, u32[]{:S(2)}) async-start(f32[8,40,128]{2,1,0:T(8,128)} %get-tuple-element.30), calls=%async_computation.1 | async-start | bytes 327680 | tf_op jit(solution)/shard_map/all_to_all | solution.py:557
  50.2 8.6 %collective-permute-start.11 = (f32[4,8,128]{2,1,0:T(8,128)S(1)}, f32[4,8,128]{2,1,0:T(8,128)S(1)}, u32[]{:S(2)}, u32[]{:S(2)}) collective-permute-start(f32[4,8,128]{2,1,0:T(8,128)S(1)} %get-tuple-element.31), channel_id=1, source_target_pairs={{128,0},{64,1},{96,2},{32,3},{192,4},{0,5},{160,6},{224,7},{136,8}... | collective-permute-start | bytes 49160 | tf_op jit(solution)/shard_map/ppermute | solution.py:565
  59.5 18.5 %collective-permute-start.12 = (f32[8,40,128]{2,1,0:T(8,128)S(1)}, f32[8,40,128]{2,1,0:T(8,128)S(1)}, u32[]{:S(2)}, u32[]{:S(2)}) collective-permute-start(f32[8,40,128]{2,1,0:T(8,128)S(1)} %all-to-all-done.1.refs_0_), channel_id=1, source_target_pairs={{0,16},{8,24},{16,0},{24,8},{32,48},{40,56},{48,32},{56,40},{64,80... | collective-permute-start | bytes 491528 | tf_op jit(solution)/shard_map/ppermute | solution.py:91
  61.6 16.4 %all-to-all-start.2 = ((f32[32,8,128]{2,1,0:T(8,128)}), f32[32,8,128]{2,1,0:T(8,128)S(1)}, u32[]{:S(2)}, u32[]{:S(2)}) async-start(f32[32,8,128]{2,1,0:T(8,128)} %bitcast.7), calls=%async_computation.2 | async-start | bytes 262144 | tf_op jit(solution)/shard_map/all_to_all | solution.py:573
  70.3 8.2 %collective-permute-start.10 = (f32[8,40,128]{2,1,0:T(8,128)S(1)}, f32[8,40,128]{2,1,0:T(8,128)S(1)}, u32[]{:S(2)}, u32[]{:S(2)}) collective-permute-start(f32[8,40,128]{2,1,0:T(8,128)S(1)} %all-to-all-done.1.refs_0_), channel_id=1, source_target_pairs={{0,8},{8,0},{16,24},{24,16},{32,40},{40,32},{48,56},{56,48},{64,72... | collective-permute-start | bytes 491528 | tf_op jit(solution)/shard_map/ppermute | solution.py:91
  78.0 1.4 %collective-permute-start.13 = (f32[8,40,128]{2,1,0:T(8,128)S(1)}, f32[8,40,128]{2,1,0:T(8,128)S(1)}, u32[]{:S(2)}, u32[]{:S(2)}) collective-permute-start(f32[8,40,128]{2,1,0:T(8,128)S(1)} %collective-permute-done.12.refs_2_), channel_id=1, source_target_pairs={{0,8},{8,0},{16,24},{24,16},{32,40},{40,32},{48,56},{56,48},{64,72... | collective-permute-start | bytes 491528 | tf_op jit(solution)/shard_map/ppermute | solution.py:91
